TPU v7x, 32 devices: a whole 2x2x4 slice. The times are simulated.
32 devices in a mesh: slab: 8 (over z, x), sub: 4 (over y, core).
Axes of the slice: x: 2, y: 2, z: 4, core: 2. Of those that a mesh axis runs over, the one named last changes fastest.
Arguments:
- state: float32 [9, 56, 2048], P(None, None, ('slab', 'sub')), may hold values from -6 to 6
- star: float32 [3, 9, 9, 2048], P(None, None, None, ('slab', 'sub')), may hold values from -2 to 2
- aminus: float32 [4, 9, 9, 2048], P(None, None, None, ('slab', 'sub')), may hold values from -1 to 1
- aplus: float32 [4, 9, 9, 2048], P(None, None, None, ('slab', 'sub')), may hold values from -1 to 1
- ck_stiff: float32 [3, 56, 56], replicated, may hold values from -0.75 to 0.75
- vol_stiff: float32 [3, 56, 56], replicated, may hold values from -0.75 to 0.75
- flux_local: float32 [4, 56, 56], replicated, may hold values from -0.75 to 0.75
- lift: float32 [4, 56, 21], replicated, may hold values from -1.25 to 1.25
- rotate: float32 [3, 21, 21], replicated, may hold values from -1.25 to 1.25
- project: float32 [4, 21, 56], replicated, may hold values from -0.75 to 0.75
- cluster: int32 [2048], P(('slab', 'sub')), may hold values from 0 to 2, as said below
- orient: int32 [4, 2048], P(None, ('slab', 'sub')), may hold values from 0 to 2
- neighbour: int32 [4, 2048], P(None, ('slab', 'sub')), may hold values from 0 to 383, as said below
- send_elem: int32 [4, 1024], P(None, ('slab', 'sub')), may hold values from 0 to 63
- send_face: int32 [4, 1024], P(None, ('slab', 'sub')), may hold values from 0 to 3
Outputs:
- new_state: float32 [9, 56, 2048], P(None, None, ('slab', 'sub'))
Inputs may be any that keep to these rules, and one draw needn't show every extreme that they name: cluster 0, 1, 2 means 1, 2, 4 steps in the coarsest step. `neighbour`: an entry x below 256 names face x // 64 of local element x % 64; otherwise x - 256 = d * 32 + s names slot s of direction d. An element of cluster 2 names only slots below 8, of cluster 1 only slots from 8 below 16, of cluster 0 only slots from 16.
All inputs are finite; a program needn't handle non-finite values.
Results may differ from a plain program's by a relative error of at most 0.0003.
Values sent between devices are 32-bit elements; how exact they have to be, the bound alone decides.
No kernel may reach another device: no remote copies, remote signals or barrier semaphores. Data moves between devices by JAX's collectives and lax.ppermute only.
A program may use at most 64 MiB of HBM per device.

v0:
```python
import functools

import jax
import jax.numpy as jnp
from jax import lax
from jax.experimental import pallas as pl
from jax.experimental.pallas import tpu as pltpu
from jax.sharding import PartitionSpec as P

FIELDS = 9
PAIRS = 5
MODES = 56
MODES_UP = 64
FACE_MODES = 21
FACE_UP = 24
ROWS = 2 * PAIRS * FACE_UP
DERIVS = 6
TICKS = 4
SLOT = 8
TIME_STEP = 1.0
F32 = jnp.float32
BF16 = jnp.bfloat16
BLOCKS = ((0, 32), (32, 24))


def from_behind(x, axis, by):
    size = lax.axis_size(axis)
    return lax.ppermute(x, axis, [(i, (i + by) % size) for i in range(size)])


def taylor_constants():
    width = TIME_STEP / TICKS
    table = []
    for begin in range(TICKS):
        factorial = 1.0
        row = []
        for order in range(DERIVS):
            factorial = factorial * (order + 1)
            span = float((begin + 1) ** (order + 1) - begin ** (order + 1))
            row.append(span * width ** (order + 1) / factorial)
        table.append(row)
    return table


def low_half(shape, half):
    return lax.broadcasted_iota(jnp.int32, shape, len(shape) - 1) < half


def swap(x, half):
    return pltpu.roll(x, half, x.ndim - 1)


def pair(a, b):
    return jnp.concatenate([a, b], axis=-1)


def halves(x):
    high = x.astype(BF16).astype(F32)
    return high, x - high


def pad_rows(x, rows):
    if x.shape[0] == rows:
        return x
    return jnp.concatenate([x, jnp.zeros((rows - x.shape[0], x.shape[1]), x.dtype)], axis=0)


def timing(cluster, tick):
    period = jnp.where(cluster == 0, 4, jnp.where(cluster == 1, 2, 1))
    offset = jnp.where(cluster == 0, tick % 4, jnp.where(cluster == 1, tick % 2, 0))
    return offset, offset == period - 1


def put_right(ref, start, values):
    rows = values.shape[0]
    up = -(-rows // 16) * 16
    high = pad_rows(values, up).astype(BF16)
    low = pad_rows(values - values.astype(BF16).astype(F32), up).astype(BF16)
    return high, low


def store_right(ref, row, col, values):
    high, low = put_right(ref, row, values)
    up = high.shape[0]
    width = values.shape[1]
    ref[row : row + up, col : col + width] = high
    ref[MODES_UP + row : MODES_UP + row + up, col : col + width] = high
    ref[2 * MODES_UP + row : 2 * MODES_UP + row + up, col : col + width] = low


def left_parts(matrix, up):
    rows = matrix.shape[0]
    high, low = halves(matrix)
    gap = jnp.zeros((rows, up - matrix.shape[1]), F32)
    return jnp.concatenate([high, gap, low, gap, high, gap], axis=1)


def contract(m_ref, coef_ref, dirs, lanes, emit):
    half = lanes // 2
    for row, count in BLOCKS:
        sums = [None] * FIELDS
        for d in range(dirs):
            for q in range(PAIRS):
                values = m_ref[d * MODES + row : d * MODES + row + count, q * lanes : (q + 1) * lanes]
                for g in range(FIELDS):
                    term = coef_ref[d * PAIRS + q, g : g + 1, :] * values
                    sums[g] = term if sums[g] is None else sums[g] + term
        low = low_half((count, lanes), half)
        for q in range(PAIRS):
            first = sums[2 * q]
            if 2 * q + 1 < FIELDS:
                second = sums[2 * q + 1]
                result = jnp.where(low, first, second) + swap(jnp.where(low, second, first), half)
            else:
                result = jnp.where(low, first + swap(first, half), 0.0)
            emit(row, count, q, result)


def predict(state_ref, ck_ref, star_ref, weight_ref, right_ref, m_ref, i_ref, lanes):
    for row, count in BLOCKS:
        for q in range(PAIRS):
            cols = slice(q * lanes, (q + 1) * lanes)
            values = state_ref[row : row + count, cols]
            i_ref[row : row + count, cols] = weight_ref[0:1, :] * values
            store_right(right_ref, row, q * lanes, values)

    def step(order, carry):
        m_ref[0 : 3 * MODES, :] = jnp.dot(ck_ref[...], right_ref[...], preferred_element_type=F32)
        weight = weight_ref[pl.ds(order + 1, 1), :]

        def emit(row, count, q, result):
            cols = slice(q * lanes, (q + 1) * lanes)
            i_ref[row : row + count, cols] += weight * result
            store_right(right_ref, row, q * lanes, result)

        contract(m_ref, star_ref, 3, lanes, emit)
        return carry

    lax.fori_loop(0, DERIVS - 1, step, 0)


def store_weights(weight_ref, cluster, tick):
    offset, _ = timing(cluster, tick)
    table = taylor_constants()
    for order in range(DERIVS):
        row = jnp.full(cluster.shape, table[0][order], F32)
        for begin in range(1, TICKS):
            row = jnp.where(offset == begin, table[begin][order], row)
        weight_ref[order : order + 1, :] = row


def project_faces(i_ref, proj_ref, right_ref, table_ref, lanes):
    half = lanes // 2
    for row, count in BLOCKS:
        for q in range(PAIRS):
            store_right(right_ref, row, q * lanes, i_ref[row : row + count, q * lanes : (q + 1) * lanes])
    faces = jnp.dot(proj_ref[...], right_ref[...], preferred_element_type=F32)
    low = low_half((FACE_UP, lanes), half)
    for q in range(PAIRS):
        for k in range(2):
            one = faces[2 * k * FACE_UP : (2 * k + 1) * FACE_UP, q * lanes : (q + 1) * lanes]
            two = faces[(2 * k + 1) * FACE_UP : (2 * k + 2) * FACE_UP, q * lanes : (q + 1) * lanes]
            crossed = swap(jnp.where(low, two, one), half)
            table_ref[2 * q * FACE_UP : (2 * q + 1) * FACE_UP, k * lanes : (k + 1) * lanes] = jnp.where(low, one, crossed)
            table_ref[(2 * q + 1) * FACE_UP : (2 * q + 2) * FACE_UP, k * lanes : (k + 1) * lanes] = jnp.where(
                low, crossed, two
            )


def pick(table, chosen):
    rows = table.shape[0]
    high, low = halves(table)
    both = jnp.concatenate([high, low], axis=0).astype(BF16)
    out = jnp.dot(both, chosen, preferred_element_type=F32)
    return out[:rows] + out[rows:]


def one_hot(index_row, rows, base=0):
    sub = lax.broadcasted_iota(jnp.int32, (rows, index_row.shape[1]), 0) + base
    return jnp.where(sub == index_row, 1.0, 0.0).astype(BF16)


def fill_messages(tables, send_index, out_refs, lanes):
    lane = lax.broadcasted_iota(jnp.int32, (FACE_UP, lanes), 1)
    column = lane // 32
    place = (lane // SLOT) % 4
    for group, table in enumerate(tables):
        elems4 = table.shape[1]
        chosen = one_hot(send_index[group : group + 1, :], elems4)
        picked = pick(table, chosen)
        quads = []
        for quad in range(3):
            merged = picked[4 * quad * FACE_UP : (4 * quad + 1) * FACE_UP]
            for c in range(1, 4):
                f = 4 * quad + c
                if f < FIELDS:
                    merged = jnp.where(column == c, picked[f * FACE_UP : (f + 1) * FACE_UP], merged)
            quads.append(merged)
        for d in range(4):
            message = None
            for quad in range(3):
                shift = ((quad - d) * SLOT) % lanes
                moved = quads[quad] if shift == 0 else pltpu.roll(quads[quad], shift, 1)
                message = moved if message is None else jnp.where(place == quad, moved, message)
            out_refs[d][group * FACE_UP : (group + 1) * FACE_UP, :] = message


def take_messages(in_refs, groups, far_ref, lanes):
    lane = lax.broadcasted_iota(jnp.int32, (FACE_UP, lanes), 1)
    column = lane // 32
    place = (lane // SLOT) % 4
    lefts = []
    for group in range(groups):
        arrived = [ref[group * FACE_UP : (group + 1) * FACE_UP, :] for ref in in_refs]
        pieces = []
        for quad in range(3):
            merged = None
            for d in range(4):
                shift = ((d - quad) * SLOT) % lanes
                moved = arrived[d] if shift == 0 else pltpu.roll(arrived[d], shift, 1)
                merged = moved if merged is None else jnp.where(place == d, moved, merged)
            for c in range(4):
                if 4 * quad + c < FIELDS:
                    pieces.append(jnp.where(column == c, merged, 0.0))
        pieces.append(jnp.zeros((FACE_UP, lanes), F32))
        lefts.append(jnp.concatenate(pieces, axis=0))
    left = lefts[0] if groups == 1 else jnp.concatenate(lefts, axis=1)
    return pick(left, far_ref[0 : groups * lanes, :])


def outer_update(in_refs, groups, near_ref, far_ref, aplus_ref, turn_ref, orient_ref, base_ref, cluster, tick, c_ref, out_ref, lanes):
    half = lanes // 2
    low = low_half((FACE_UP, lanes), half)
    values = near_ref[...] + take_messages(in_refs, groups, far_ref, lanes)
    zeros = jnp.zeros((SLOT, lanes), F32)
    for k in range(2):
        sums = [None] * FIELDS
        for f in range(FIELDS):
            part = values[f * FACE_UP : (f + 1) * FACE_UP, k * lanes : (k + 1) * lanes]
            for g in range(FIELDS):
                term = aplus_ref[k * FIELDS + f, g : g + 1, :] * part
                sums[g] = term if sums[g] is None else sums[g] + term
        for q in range(PAIRS):
            first = sums[2 * q]
            if 2 * q + 1 < FIELDS:
                second = sums[2 * q + 1]
                crossed = swap(jnp.where(low, second, first), half)
                sides = (jnp.where(low, first, crossed), jnp.where(low, crossed, second))
            else:
                crossed = swap(first, half)
                sides = (jnp.where(low, first, 0.0), jnp.where(low, crossed, 0.0))
            for side in range(2):
                high, rest = halves(sides[side])
                stacked = jnp.concatenate([high, high, rest, zeros], axis=0).astype(BF16)
                c_ref[2 * k + side, :, q * lanes : (q + 1) * lanes] = stacked
    _, finished = timing(cluster, tick)
    for j in range(4):
        turned = jnp.dot(turn_ref[j], c_ref[j], preferred_element_type=F32)
        which = orient_ref[j : j + 1, :]
        which = pair(which, which)
        for q in range(PAIRS):
            cols = slice(q * lanes, (q + 1) * lanes)
            term = jnp.where(
                which == 0,
                turned[0:MODES, cols],
                jnp.where(which == 1, turned[MODES : 2 * MODES, cols], turned[2 * MODES : 3 * MODES, cols]),
            )
            before = base_ref[:, cols] if j == 0 else out_ref[:, cols]
            out_ref[:, cols] = jnp.where(finished, before - term, before)


def pack_pairs(ref, axis_pairs, lead, out_ref):
    for a in range(lead):
        for q in range(axis_pairs):
            one = ref[a, 2 * q]
            two = ref[a, 2 * q + 1] if 2 * q + 1 < FIELDS else jnp.zeros_like(one)
            out_ref[a * axis_pairs + q] = pair(one, two)


def first_kernel(
    state_ref, star_ref, ck_ref, project_ref, cluster_ref, send_ref,
    m0, m1, m2, m3, packed_ref, star_out, ck_out, proj_out, i_ref, table_ref,
    right_ref, m_ref, weight_ref, *, lanes,
):
    for q in range(PAIRS):
        one = state_ref[2 * q]
        two = state_ref[2 * q + 1] if 2 * q + 1 < FIELDS else jnp.zeros_like(one)
        packed_ref[:, q * lanes : (q + 1) * lanes] = pair(one, two)
    pack_pairs(star_ref, PAIRS, 3, star_out)
    ck = -ck_ref[...].reshape(3 * MODES, MODES)
    ck_out[...] = left_parts(ck, MODES_UP).astype(BF16)
    proj_rows = [pad_rows(project_ref[j], FACE_UP) for j in range(4)]
    proj_out[...] = left_parts(jnp.concatenate(proj_rows, axis=0), MODES_UP).astype(BF16)
    cluster = pair(cluster_ref[...], cluster_ref[...])
    store_weights(weight_ref, cluster, 0)
    predict(packed_ref, ck_out, star_out, weight_ref, right_ref, m_ref, i_ref, lanes)
    project_faces(i_ref, proj_out, right_ref, table_ref, lanes)
    fill_messages([table_ref[...]], send_ref[...], (m0, m1, m2, m3), lanes)


def prepare_kernel(
    star_ref, aminus_ref, aplus_ref, vol_ref, flux_ref, lift_ref, rotate_ref, neighbour_ref,
    coef_out, aplus_out, left_out, turn_out, near_out, far_out, *, lanes,
):
    half = lanes // 2
    pack_pairs(star_ref, PAIRS, 3, coef_out)
    for a in range(4):
        for q in range(PAIRS):
            one = aminus_ref[a, 2 * q]
            two = aminus_ref[a, 2 * q + 1] if 2 * q + 1 < FIELDS else jnp.zeros_like(one)
            coef_out[(3 + a) * PAIRS + q] = pair(one, two)
    for k in range(2):
        for f in range(FIELDS):
            aplus_out[k * FIELDS + f] = pair(aplus_ref[2 * k, f], aplus_ref[2 * k + 1, f])
    left_out[0 : 3 * MODES, :] = left_parts(vol_ref[...].reshape(3 * MODES, MODES), MODES_UP)
    left_out[3 * MODES : 7 * MODES, :] = left_parts(-flux_ref[...].reshape(4 * MODES, MODES), MODES_UP)
    for j in range(4):
        for which in range(3):
            turned = jnp.dot(lift_ref[j], rotate_ref[which], precision=lax.Precision.HIGHEST, preferred_element_type=F32)
            parts = left_parts(turned, FACE_UP)
            gap = jnp.zeros((MODES, SLOT), F32)
            turn_out[j, which * MODES : (which + 1) * MODES, :] = jnp.concatenate([parts, gap], axis=1)
    row = jnp.concatenate([neighbour_ref[j : j + 1, :] for j in range(4)], axis=1)
    near_out[...] = one_hot(row, 4 * half)
    sub = lax.broadcasted_iota(jnp.int32, (lanes, 4 * half), 0)
    for group in range(4):
        target = 4 * half + ((sub // SLOT) % 4) * 32 + group * SLOT + sub % SLOT
        far_out[group * lanes : (group + 1) * lanes, :] = jnp.where(target == row, 1.0, 0.0).astype(BF16)


def local_kernel(
    i_ref, packed_ref, table_ref, cluster_ref, coef_ref, left_ref, near_ref, own_ref, seen_ref,
    base_out, own_out, seen_out, right_ref, m_ref, *, lanes, tick,
):
    cluster = pair(cluster_ref[...], cluster_ref[...])
    offset, finished = timing(cluster, tick)
    fresh = offset == 0
    for row, count in BLOCKS:
        for q in range(PAIRS):
            cols = slice(q * lanes, (q + 1) * lanes)
            values = i_ref[row : row + count, cols]
            if tick:
                values = jnp.where(fresh, values, own_ref[row : row + count, cols] + values)
            own_out[row : row + count, cols] = values
            store_right(right_ref, row, q * lanes, values)
    seen = pick(table_ref[...], near_ref[...])
    if tick:
        twice = pair(fresh, fresh) if False else jnp.concatenate([offset, offset], axis=1) == 0
        seen = jnp.where(twice, seen, seen_ref[...] + seen)
    seen_out[...] = seen
    m_ref[...] = jnp.dot(left_ref[...], right_ref[...], preferred_element_type=F32)

    def emit(row, count, q, result):
        cols = slice(q * lanes, (q + 1) * lanes)
        before = packed_ref[row : row + count, cols]
        base_out[row : row + count, cols] = jnp.where(finished, before + result, before)

    contract(m_ref, coef_ref, 7, lanes, emit)


def tick_kernel(
    r0, r1, r2, r3, near_ref, far_ref, aplus_ref, turn_ref, orient_ref, base_ref, cluster_ref,
    ck_ref, proj_ref, star_ref, send_ref, *rest, lanes, tick, olds, groups,
):
    old_refs = rest[:olds]
    m0, m1, m2, m3, packed_ref, i_ref, table_ref = rest[olds : olds + 7]
    rest = rest[olds + 7 :]
    sum_ref = None
    if tick == 1:
        sum_ref, rest = rest[0], rest[1:]
    right_ref, m_ref, weight_ref, c_ref = rest
    cluster = pair(cluster_ref[...], cluster_ref[...])
    outer_update(
        (r0, r1, r2, r3), groups, near_ref, far_ref, aplus_ref, turn_ref, orient_ref, base_ref,
        cluster, tick - 1, c_ref, packed_ref, lanes,
    )
    store_weights(weight_ref, cluster, tick)
    predict(packed_ref, ck_ref, star_ref, weight_ref, right_ref, m_ref, i_ref, lanes)
    project_faces(i_ref, proj_ref, right_ref, table_ref, lanes)
    table = table_ref[...]
    tables = [table]
    if tick == 1:
        two = old_refs[0][...] + table
        sum_ref[...] = two
        tables.append(two)
    if tick == 3:
        two = old_refs[0][...] + table
        four = old_refs[1][...] + two
        tables += [two, four, four]
    fill_messages(tables, send_ref[...], (m0, m1, m2, m3), lanes)


def last_kernel(
    r0, r1, r2, r3, near_ref, far_ref, aplus_ref, turn_ref, orient_ref, base_ref, cluster_ref,
    out_ref, packed_ref, c_ref, *, lanes,
):
    half = lanes // 2
    cluster = pair(cluster_ref[...], cluster_ref[...])
    outer_update(
        (r0, r1, r2, r3), 4, near_ref, far_ref, aplus_ref, turn_ref, orient_ref, base_ref,
        cluster, TICKS - 1, c_ref, packed_ref, lanes,
    )
    for f in range(FIELDS):
        begin = (f // 2) * lanes + (f % 2) * half
        out_ref[f] = packed_ref[:, begin : begin + half]


def call(body, outs, scratch, name, flops, arrays):
    moved = sum(a.size * a.dtype.itemsize for a in arrays)
    return pl.pallas_call(
        body,
        out_shape=outs,
        in_specs=[pl.BlockSpec(memory_space=pltpu.VMEM)] * len(arrays),
        out_specs=[pl.BlockSpec(memory_space=pltpu.VMEM)] * len(outs),
        scratch_shapes=scratch,
        compiler_params=pltpu.CompilerParams(vmem_limit_bytes=24 << 20),
        cost_estimate=pl.CostEstimate(flops=flops, bytes_accessed=moved, transcendentals=0),
        name=name,
    )(*arrays)


def shards(
    state, star, aminus, aplus, ck_stiff, vol_stiff, flux_local, lift, rotate, project,
    cluster, orient, neighbour, send_elem, send_face,
):
    elems = state.shape[-1]
    lanes = 2 * elems
    wide = PAIRS * lanes
    shape = jax.ShapeDtypeStruct
    cluster_row = cluster.reshape(1, elems)
    slots = send_elem.shape[1]
    groups = slots // SLOT
    send = (send_face * elems + send_elem).reshape(4, groups, SLOT)
    send = jnp.tile(jnp.transpose(send, (1, 0, 2)).reshape(groups, 4 * SLOT), (1, lanes // (4 * SLOT)))

    modal = shape((MODES, wide), F32)
    table = shape((ROWS, 4 * elems), F32)
    right = pltpu.VMEM((3 * MODES_UP, wide), BF16)
    weights = pltpu.VMEM((SLOT, lanes), F32)
    faces = pltpu.VMEM((4, 80, wide), BF16)

    def message(count):
        return [shape((count * FACE_UP, lanes), F32)] * 4

    out = call(
        functools.partial(first_kernel, lanes=lanes),
        message(1)
        + [
            modal,
            shape((3 * PAIRS, FIELDS, lanes), F32),
            shape((3 * MODES, 3 * MODES_UP), BF16),
            shape((4 * FACE_UP, 3 * MODES_UP), BF16),
            modal,
            table,
        ],
        [right, pltpu.VMEM((3 * MODES, wide), F32), weights],
        "first", 400_000_000, (state, star, ck_stiff, project, cluster_row, send),
    )
    messages, (packed, star_pairs, ck_left, proj_left, integral, table_now) = out[:4], out[4:]
    coef, aplus_pairs, left, turn, near_hot, far_hot = call(
        functools.partial(prepare_kernel, lanes=lanes),
        [
            shape((7 * PAIRS, FIELDS, lanes), F32),
            shape((2 * FIELDS, FIELDS, lanes), F32),
            shape((7 * MODES, 3 * MODES_UP), F32),
            shape((4, 3 * MODES, 80), F32),
            shape((4 * elems, 4 * elems), BF16),
            shape((4 * lanes, 4 * elems), BF16),
        ],
        [],
        "prepare", 100_000_000,
        (star, aminus, aplus, vol_stiff, flux_local, lift, rotate, neighbour),
    )
    left = left.astype(BF16)
    turn = turn.astype(BF16)
    own = integral
    seen = table_now
    tables = []
    two = None
    for tick in range(TICKS):
        arrived = [
            from_behind(messages[0], "slab", 1),
            from_behind(messages[1], "slab", -1),
            from_behind(messages[2], "sub", 1),
            from_behind(messages[3], "sub", -1),
        ]
        base, own, seen = call(
            functools.partial(local_kernel, lanes=lanes, tick=tick),
            [modal, modal, table],
            [right, pltpu.VMEM((7 * MODES, wide), F32)],
            f"local{tick}", 300_000_000,
            (integral, packed, table_now, cluster_row, coef, left, near_hot, own, seen),
        )
        count = (1, 2, 1, 4)[tick]
        common = (*arrived, seen, far_hot, aplus_pairs, turn, orient, base, cluster_row)
        if tick == TICKS - 1:
            return call(
                functools.partial(last_kernel, lanes=lanes),
                [shape(state.shape, F32)],
                [pltpu.VMEM((MODES, wide), F32), faces],
                "last", 100_000_000, common,
            )[0]
        olds = {0: (table_now,), 1: (), 2: (table_now, two)}[tick]
        sends = (1, 2, 1, 4)[tick + 1]
        out = call(
            functools.partial(tick_kernel, lanes=lanes, tick=tick + 1, olds=len(olds), groups=count),
            message(sends) + [modal, modal, table] + ([table] if tick == 0 else []),
            [right, pltpu.VMEM((3 * MODES, wide), F32), weights, faces],
            f"tick{tick + 1}", 500_000_000,
            (*common, ck_left, proj_left, star_pairs, send, *olds),
        )
        messages, (packed, integral, table_now) = out[:4], out[4:7]
        if tick == 0:
            two = out[7]


def solution(mesh):
    placed = (
        P(None, None, ("slab", "sub")),
        P(None, None, None, ("slab", "sub")),
        P(None, None, None, ("slab", "sub")),
        P(None, None, None, ("slab", "sub")),
        P(),
        P(),
        P(),
        P(),
        P(),
        P(),
        P(("slab", "sub")),
        P(None, ("slab", "sub")),
        P(None, ("slab", "sub")),
        P(None, ("slab", "sub")),
        P(None, ("slab", "sub")),
    )
    return jax.shard_map(
        shards,
        mesh=mesh,
        in_specs=placed,
        out_specs=P(None, None, ("slab", "sub")),
        check_vma=False,
    )
```

profile of v0, /device:TPU:1, one launch (start us, length us, event | category | flops | bytes accessed | tf_op | source)
XLA Modules:
  0.0 58.9 jit_solution(9019264787430981155)
XLA Ops:
  0.0 0.7 %multiply_add_fusion = s32[4,32]{1,0:T(4,128)S(1)} fusion(s32[4,32]{1,0:T(4,128)} %param.28, s32[4,32]{1,0:T(4,128)} %param.29), kind=kLoop, calls=%fused_computation | loop fusion | flops 256 | bytes 1536 | tf_op jit(solution)/shard_map/add | solution.py:433
  0.7 0.1 reshape.11
  0.8 0.1 tile.10
  0.9 0.1 tile.12.send_ref
  1.0 0.0 copy-start.7
  1.0 1.0 %copy.17.star_ref = f32[3,9,9,64]{3,2,1,0:T(8,128)S(1)} copy(f32[3,9,9,64]{3,0,2,1:T(4,128)} %param.16) | data formatting | bytes 124416 | tf_op args[1]
  2.0 0.0 copy-start.3
  2.0 0.6 %copy-done.3 = s32[64]{0:T(128)S(1)} copy-done((s32[64]{0:T(128)S(1)}, s32[64]{0:T(128)}, u32[]{:S(2)}) %copy-start.3) | copy-done | bytes 280
  2.6 3.3 %first.1 = (f32[24,128]{1,0:T(8,128)S(1)}, f32[24,128]{1,0:T(8,128)S(1)}, f32[24,128]{1,0:T(8,128)S(1)}, f32[24,128]{1,0:T(8,128)S(1)}, f32[56,640]{1,0:T(8,128)...) custom-call(f32[9,56,64]{2,1,0:T(8,128)S(1)} %copy-done.6, ...), custom_call_target="tpu_custom_call" | custom-call | flops 400000000 | bytes 249984 | tf_op jit(solution)/shard_map/first/pallas_call | solution.py:410
  6.0 2.1 %collective-permute-start = (f32[24,128]{1,0:T(8,128)S(1)}, f32[24,128]{1,0:T(8,128)S(1)}, u32[]{:S(2)}, u32[]{:S(2)}) collective-permute-start(f32[24,128]{1,0:T(8,128)S(1)} %get-tuple-element.54), channel_id=1, source_target_pairs={{0,4},{4,8},{8,12},{12,16},{16,20},{20,24},{24,28},{28,0},{1,5},{5... | collective-permute-start | bytes 36872 | tf_op jit(solution)/shard_map/ppermute | solution.py:28
  8.1 3.1 %collective-permute-start.1 = (f32[24,128]{1,0:T(8,128)S(1)}, f32[24,128]{1,0:T(8,128)S(1)}, u32[]{:S(2)}, u32[]{:S(2)}) collective-permute-start(f32[24,128]{1,0:T(8,128)S(1)} %get-tuple-element.55), channel_id=1, source_target_pairs={{0,28},{4,0},{8,4},{12,8},{16,12},{20,16},{24,20},{28,24},{1,29},{... | collective-permute-start | bytes 36872 | tf_op jit(solution)/shard_map/ppermute | solution.py:28
  11.2 2.2 %collective-permute-start.2 = (f32[24,128]{1,0:T(8,128)S(1)}, f32[24,128]{1,0:T(8,128)S(1)}, u32[]{:S(2)}, u32[]{:S(2)}) collective-permute-start(f32[24,128]{1,0:T(8,128)S(1)} %get-tuple-element.56), channel_id=1, source_target_pairs={{0,1},{1,2},{2,3},{3,0},{4,5},{5,6},{6,7},{7,4},{8,9},{9,10},{10,1... | collective-permute-start | bytes 36872 | tf_op jit(solution)/shard_map/ppermute | solution.py:28
  13.4 0.0 collective-permute-start.3
  13.4 0.1 copy.22.lift_ref
  13.5 0.0 copy-start.9
  13.5 0.9 %copy-done.9 = f32[4,9,9,64]{3,0,2,1:T(4,128)S(1)} copy-done((f32[4,9,9,64]{3,0,2,1:T(4,128)S(1)}, f32[4,9,9,64]{3,0,2,1:T(4,128)}, u32[]{:S(2)}) %copy-start.9) | copy-done | bytes 82968
  14.5 0.8 %copy-done = f32[4,56,56]{2,1,0:T(8,128)S(1)} copy-done((f32[4,56,56]{2,1,0:T(8,128)S(1)}, f32[4,56,56]{2,1,0:T(8,128)}, u32[]{:S(2)}) %copy-start) | copy-done | bytes 50200
  15.3 0.0 copy-done.1
  15.4 0.9 %prepare.1 = (f32[35,9,128]{2,1,0:T(8,128)S(1)}, f32[18,9,128]{2,1,0:T(8,128)S(1)}, f32[392,192]{1,0:T(8,128)S(1)}, f32[4,168,80]{2,1,0:T(8,128)S(1)}, bf16[256,...) custom-call(f32[3,9,9,64]{3,2,1,0:T(8,128)S(1)} %copy.17.star_ref, f32[4,9,9,64]{3,2,1,0:T(8,128)S(1)} %copy.20.aminus_ref, ...), custom_call_target="tpu_custom_call" | custom-call | flops 100000000 | bytes 341036 | tf_op jit(solution)/shard_map/prepare/pallas_call | solution.py:410
  16.3 1.1 %local0.1 = (f32[56,640]{1,0:T(8,128)S(1)}, f32[56,640]{1,0:T(8,128)S(1)}, f32[240,256]{1,0:T(8,128)S(1)}) custom-call(f32[56,640]{1,0:T(8,128)S(1)} %get-tuple-element.58.i_ref.own_ref, f32[56,640]{1,0:T(8,128)S(1)} %get-tuple-element.59.packed_ref, f32[240,256]{1,0:T(8,128)S(1)} %get-tuple-element.60.table_ref.seen_ref.rest_0_, s32[1,64]{1,0:T(1,128)S(1)} %bitcast.3, ...), custom_call_target="tpu_custom_call" | custom-call | flops 300000000 | bytes 1364736 | tf_op jit(solution)/shard_map/local0/pallas_call | solution.py:410
  17.5 0.0 collective-permute-done.r0
  17.5 0.0 collective-permute-done.2.r2
  17.5 0.0 collective-permute-done.3.r3
  17.5 0.0 copy-start.5
  17.5 0.7 %copy-done.5 = s32[4,64]{1,0:T(4,128)S(1)} copy-done((s32[4,64]{1,0:T(4,128)S(1)}, s32[4,64]{1,0:T(4,128)}, u32[]{:S(2)}) %copy-start.5) | copy-done | bytes 1048
  18.2 4.3 %tick1.1 = (f32[48,128]{1,0:T(8,128)S(1)}, f32[48,128]{1,0:T(8,128)S(1)}, f32[48,128]{1,0:T(8,128)S(1)}, f32[48,128]{1,0:T(8,128)S(1)}, f32[56,640]{1,0:T(8,128)...) custom-call(f32[24,128]{1,0:T(8,128)S(1)} %collective-permute-done.r0, ...), custom_call_target="tpu_custom_call" | custom-call | flops 500000000 | bytes 1310464 | tf_op jit(solution)/shard_map/tick1/pallas_call | solution.py:410
  22.5 0.1 collective-permute-start.4
  22.5 4.1 %collective-permute-start.5 = (f32[48,128]{1,0:T(8,128)S(1)}, f32[48,128]{1,0:T(8,128)S(1)}, u32[]{:S(2)}, u32[]{:S(2)}) collective-permute-start(f32[48,128]{1,0:T(8,128)S(1)} %get-tuple-element.73), channel_id=1, source_target_pairs={{0,28},{4,0},{8,4},{12,8},{16,12},{20,16},{24,20},{28,24},{1,29},{... | collective-permute-start | bytes 73736 | tf_op jit(solution)/shard_map/ppermute | solution.py:28
  26.7 2.3 %collective-permute-start.6 = (f32[48,128]{1,0:T(8,128)S(1)}, f32[48,128]{1,0:T(8,128)S(1)}, u32[]{:S(2)}, u32[]{:S(2)}) collective-permute-start(f32[48,128]{1,0:T(8,128)S(1)} %get-tuple-element.74), channel_id=1, source_target_pairs={{0,1},{1,2},{2,3},{3,0},{4,5},{5,6},{6,7},{7,4},{8,9},{9,10},{10,1... | collective-permute-start | bytes 73736 | tf_op jit(solution)/shard_map/ppermute | solution.py:28
  29.0 0.0 collective-permute-start.7
  29.0 1.1 %local1.1 = (f32[56,640]{1,0:T(8,128)S(1)}, f32[56,640]{1,0:T(8,128)S(1)}, f32[240,256]{1,0:T(8,128)S(1)}) custom-call(f32[56,640]{1,0:T(8,128)S(1)} %get-tuple-element.76.i_ref, f32[56,640]{1,0:T(8,128)S(1)} %get-tuple-element.77.packed_ref, f32[240,256]{1,0:T(8,128)S(1)} %get-tuple-element.78.table_ref, s32[1,64]{1,0:T(1,128)S(1)} %bitcast.5, ...), custom_call_target="tpu_custom_call" | custom-call | flops 300000000 | bytes 1364736 | tf_op jit(solution)/shard_map/local1/pallas_call | solution.py:410
  30.1 0.0 collective-permute-done.5.r1
  30.1 0.0 collective-permute-done.6.r2
  30.1 2.1 %collective-permute-done.7.r3 = f32[48,128]{1,0:T(8,128)S(1)} collective-permute-done((f32[48,128]{1,0:T(8,128)S(1)}, f32[48,128]{1,0:T(8,128)S(1)}, u32[]{:S(2)}, u32[]{:S(2)}) %collective-permute-start.7) | collective-permute-done | bytes 24608 | tf_op jit(solution)/shard_map/ppermute | solution.py:28
  32.2 4.2 %tick2.1 = (f32[24,128]{1,0:T(8,128)S(1)}, f32[24,128]{1,0:T(8,128)S(1)}, f32[24,128]{1,0:T(8,128)S(1)}, f32[24,128]{1,0:T(8,128)S(1)}, f32[56,640]{1,0:T(8,128)...) custom-call(f32[48,128]{1,0:T(8,128)S(1)} %collective-permute-done.4.r0, f32[48,128]{1,0:T(8,128)S(1)} %collective-permute-done.5.r1, ...), custom_call_target="tpu_custom_call" | custom-call | flops 500000000 | bytes 1113856 | tf_op jit(solution)/shard_map/tick2/pallas_call | solution.py:410
  36.5 0.1 collective-permute-start.8
  36.5 4.1 %collective-permute-start.9 = (f32[24,128]{1,0:T(8,128)S(1)}, f32[24,128]{1,0:T(8,128)S(1)}, u32[]{:S(2)}, u32[]{:S(2)}) collective-permute-start(f32[24,128]{1,0:T(8,128)S(1)} %get-tuple-element.83), channel_id=1, source_target_pairs={{0,28},{4,0},{8,4},{12,8},{16,12},{20,16},{24,20},{28,24},{1,29},{... | collective-permute-start | bytes 36872 | tf_op jit(solution)/shard_map/ppermute | solution.py:28
  40.7 0.6 collective-permute-start.10
  41.3 1.1 %local2.1 = (f32[56,640]{1,0:T(8,128)S(1)}, f32[56,640]{1,0:T(8,128)S(1)}, f32[240,256]{1,0:T(8,128)S(1)}) custom-call(f32[56,640]{1,0:T(8,128)S(1)} %get-tuple-element.86.i_ref, f32[56,640]{1,0:T(8,128)S(1)} %get-tuple-element.87.packed_ref, f32[240,256]{1,0:T(8,128)S(1)} %get-tuple-element.88.table_ref.rest_0_, s32[1,64]{1,0:T(1,128)S(1)} %bitcast.7, ...), custom_call_target="tpu_custom_call" | custom-call | flops 300000000 | bytes 1364736 | tf_op jit(solution)/shard_map/local2/pallas_call | solution.py:410
  42.4 2.0 %collective-permute-done.11.r3 = f32[24,128]{1,0:T(8,128)S(1)} collective-permute-done((f32[24,128]{1,0:T(8,128)S(1)}, f32[24,128]{1,0:T(8,128)S(1)}, u32[]{:S(2)}, u32[]{:S(2)}) %collective-permute-start.11) | collective-permute-done | bytes 12320 | tf_op jit(solution)/shard_map/ppermute | solution.py:28
  44.4 4.4 %tick3.1 = (f32[96,128]{1,0:T(8,128)S(1)}, f32[96,128]{1,0:T(8,128)S(1)}, f32[96,128]{1,0:T(8,128)S(1)}, f32[96,128]{1,0:T(8,128)S(1)}, f32[56,640]{1,0:T(8,128)...) custom-call(f32[24,128]{1,0:T(8,128)S(1)} %collective-permute-done.8.r0, f32[24,128]{1,0:T(8,128)S(1)} %collective-permute-done.9.r1, ...), custom_call_target="tpu_custom_call" | custom-call | flops 500000000 | bytes 1556224 | tf_op jit(solution)/shard_map/tick3/pallas_call | solution.py:410
  48.8 0.1 collective-permute-start.12
  48.8 4.1 %collective-permute-start.13 = (f32[96,128]{1,0:T(8,128)S(1)}, f32[96,128]{1,0:T(8,128)S(1)}, u32[]{:S(2)}, u32[]{:S(2)}) collective-permute-start(f32[96,128]{1,0:T(8,128)S(1)} %get-tuple-element.94), channel_id=1, source_target_pairs={{0,28},{4,0},{8,4},{12,8},{16,12},{20,16},{24,20},{28,24},{1,29},{... | collective-permute-start | bytes 147464 | tf_op jit(solution)/shard_map/ppermute | solution.py:28
  53.0 0.6 %collective-permute-start.14 = (f32[96,128]{1,0:T(8,128)S(1)}, f32[96,128]{1,0:T(8,128)S(1)}, u32[]{:S(2)}, u32[]{:S(2)}) collective-permute-start(f32[96,128]{1,0:T(8,128)S(1)} %get-tuple-element.95), channel_id=1, source_target_pairs={{0,1},{1,2},{2,3},{3,0},{4,5},{5,6},{6,7},{7,4},{8,9},{9,10},{10,1... | collective-permute-start | bytes 147464 | tf_op jit(solution)/shard_map/ppermute | solution.py:28
  53.6 1.1 %local3.1 = (f32[56,640]{1,0:T(8,128)S(1)}, f32[56,640]{1,0:T(8,128)}, f32[240,256]{1,0:T(8,128)S(1)}) custom-call(f32[56,640]{1,0:T(8,128)S(1)} %get-tuple-element.97.i_ref, f32[56,640]{1,0:T(8,128)S(1)} %get-tuple-element.98.packed_ref, f32[240,256]{1,0:T(8,128)S(1)} %get-tuple-element.99.table_ref, s32[1,64]{1,0:T(1,128)S(1)} %bitcast.9, ...), custom_call_target="tpu_custom_call" | custom-call | flops 300000000 | bytes 1364736 | tf_op jit(solution)/shard_map/local3/pallas_call | solution.py:410
  54.7 0.1 collective-permute-done.14.r2
  54.8 2.3 %collective-permute-done.15.r3 = f32[96,128]{1,0:T(8,128)S(1)} collective-permute-done((f32[96,128]{1,0:T(8,128)S(1)}, f32[96,128]{1,0:T(8,128)S(1)}, u32[]{:S(2)}, u32[]{:S(2)}) %collective-permute-start.15) | collective-permute-done | bytes 49184 | tf_op jit(solution)/shard_map/ppermute | solution.py:28
  57.1 1.9 %last.1 = f32[9,56,64]{2,1,0:T(8,128)} custom-call(f32[96,128]{1,0:T(8,128)S(1)} %collective-permute-done.12.r0, f32[96,128]{1,0:T(8,128)S(1)} %collective-permute-done.13.r1, f32[96,128]{1,0:T(8,128)S(1)} %collective-permute-done.14.r2, f32[96,128]{1,0:T(8,128)S(1)} %collective-permute-done.15.r3, f32[240,256]{1,0:T(8,128)S(1)} %get-tuple-element.101.near_ref, ...), custom_call_target="tpu_custom_call" | custom-call | flops 100000000 | bytes 1039616 | tf_op jit(solution)/shard_map/last/pallas_call | solution.py:410
  (31 shorter events, 0.2 us)
Async XLA Ops:
  0.0 1.0 %copy-start.10 = (f32[4,21,56]{2,0,1:T(4,128)S(1)}, f32[4,21,56]{2,0,1:T(4,128)}, u32[]{:S(2)}) copy-start(f32[4,21,56]{2,0,1:T(4,128)} %param.24) | copy-start | bytes 56452
  0.8 1.2 %copy-start.6 = (f32[9,56,64]{2,1,0:T(8,128)S(1)}, f32[9,56,64]{2,1,0:T(8,128)}, u32[]{:S(2)}) copy-start(f32[9,56,64]{2,1,0:T(8,128)} %state_ref.1) | copy-start | bytes 387076
  1.0 1.0 %copy-start.7 = (f32[3,56,56]{2,1,0:T(8,128)S(1)}, f32[3,56,56]{2,1,0:T(8,128)}, u32[]{:S(2)}) copy-start(f32[3,56,56]{2,1,0:T(8,128)} %ck_ref.1) | copy-start | bytes 112900
  2.0 0.7 %copy-start.3 = (s32[64]{0:T(128)S(1)}, s32[64]{0:T(128)}, u32[]{:S(2)}) copy-start(s32[64]{0:T(128)} %param.25) | copy-start | bytes 772
  2.6 10.7 %copy-start.11 = (f32[4,56,21]{1,0,2:T(4,128)S(1)}, f32[4,56,21]{1,0,2:T(4,128)}, u32[]{:S(2)}) copy-start(f32[4,56,21]{1,0,2:T(4,128)} %param.22) | copy-start | bytes 56452
  2.6 10.8 %copy-start.8 = (f32[4,9,9,64]{3,0,2,1:T(4,128)S(1)}, f32[4,9,9,64]{3,0,2,1:T(4,128)}, u32[]{:S(2)}) copy-start(f32[4,9,9,64]{3,0,2,1:T(4,128)} %param.17) | copy-start | bytes 248836
  6.0 11.5 %collective-permute-start = (f32[24,128]{1,0:T(8,128)S(1)}, f32[24,128]{1,0:T(8,128)S(1)}, u32[]{:S(2)}, u32[]{:S(2)}) collective-permute-start(f32[24,128]{1,0:T(8,128)S(1)} %get-tuple-element.54), channel_id=1, source_target_pairs={{0,4},{4,8},{8,12},{12,16},{16,20},{20,24},{24,28},{28,0},{1,5},{5... | collective-permute-start | bytes 36872 | tf_op jit(solution)/shard_map/ppermute | solution.py:28
  8.1 9.4 %collective-permute-start.1 = (f32[24,128]{1,0:T(8,128)S(1)}, f32[24,128]{1,0:T(8,128)S(1)}, u32[]{:S(2)}, u32[]{:S(2)}) collective-permute-start(f32[24,128]{1,0:T(8,128)S(1)} %get-tuple-element.55), channel_id=1, source_target_pairs={{0,28},{4,0},{8,4},{12,8},{16,12},{20,16},{24,20},{28,24},{1,29},{... | collective-permute-start | bytes 36872 | tf_op jit(solution)/shard_map/ppermute | solution.py:28
  11.2 6.3 %collective-permute-start.2 = (f32[24,128]{1,0:T(8,128)S(1)}, f32[24,128]{1,0:T(8,128)S(1)}, u32[]{:S(2)}, u32[]{:S(2)}) collective-permute-start(f32[24,128]{1,0:T(8,128)S(1)} %get-tuple-element.56), channel_id=1, source_target_pairs={{0,1},{1,2},{2,3},{3,0},{4,5},{5,6},{6,7},{7,4},{8,9},{9,10},{10,1... | collective-permute-start | bytes 36872 | tf_op jit(solution)/shard_map/ppermute | solution.py:28
  13.4 4.1 %collective-permute-start.3 = (f32[24,128]{1,0:T(8,128)S(1)}, f32[24,128]{1,0:T(8,128)S(1)}, u32[]{:S(2)}, u32[]{:S(2)}) collective-permute-start(f32[24,128]{1,0:T(8,128)S(1)} %get-tuple-element.57), channel_id=1, source_target_pairs={{0,3},{1,0},{2,1},{3,2},{4,7},{5,4},{6,5},{7,6},{8,11},{9,8},{10,9... | collective-permute-start | bytes 36872 | tf_op jit(solution)/shard_map/ppermute | solution.py:28
  13.5 0.9 %copy-start.9 = (f32[4,9,9,64]{3,0,2,1:T(4,128)S(1)}, f32[4,9,9,64]{3,0,2,1:T(4,128)}, u32[]{:S(2)}) copy-start(f32[4,9,9,64]{3,0,2,1:T(4,128)} %param.18) | copy-start | bytes 248836
  14.4 0.9 %copy-start = (f32[4,56,56]{2,1,0:T(8,128)S(1)}, f32[4,56,56]{2,1,0:T(8,128)}, u32[]{:S(2)}) copy-start(f32[4,56,56]{2,1,0:T(8,128)} %flux_ref.1) | copy-start | bytes 150532
  14.4 0.9 %copy-start.1 = (f32[3,56,56]{2,1,0:T(8,128)S(1)}, f32[3,56,56]{2,1,0:T(8,128)}, u32[]{:S(2)}) copy-start(f32[3,56,56]{2,1,0:T(8,128)} %vol_ref.1) | copy-start | bytes 112900
  14.4 0.9 %copy-start.2 = (f32[3,21,21]{2,1,0:T(8,128)S(1)}, f32[3,21,21]{2,1,0:T(8,128)}, u32[]{:S(2)}) copy-start(f32[3,21,21]{2,1,0:T(8,128)} %rotate_ref.1) | copy-start | bytes 15880
  14.4 0.9 %copy-start.4 = (s32[4,64]{1,0:T(4,128)S(1)}, s32[4,64]{1,0:T(4,128)}, u32[]{:S(2)}) copy-start(s32[4,64]{1,0:T(4,128)} %neighbour_ref.1) | copy-start | bytes 3076
  17.5 0.7 %copy-start.5 = (s32[4,64]{1,0:T(4,128)S(1)}, s32[4,64]{1,0:T(4,128)}, u32[]{:S(2)}) copy-start(s32[4,64]{1,0:T(4,128)} %orient_ref.7) | copy-start | bytes 3076
  22.5 7.6 %collective-permute-start.4 = (f32[48,128]{1,0:T(8,128)S(1)}, f32[48,128]{1,0:T(8,128)S(1)}, u32[]{:S(2)}, u32[]{:S(2)}) collective-permute-start(f32[48,128]{1,0:T(8,128)S(1)} %get-tuple-element.72), channel_id=1, source_target_pairs={{0,4},{4,8},{8,12},{12,16},{16,20},{20,24},{24,28},{28,0},{1,5},{5... | collective-permute-start | bytes 73736 | tf_op jit(solution)/shard_map/ppermute | solution.py:28
  22.5 7.5 %collective-permute-start.5 = (f32[48,128]{1,0:T(8,128)S(1)}, f32[48,128]{1,0:T(8,128)S(1)}, u32[]{:S(2)}, u32[]{:S(2)}) collective-permute-start(f32[48,128]{1,0:T(8,128)S(1)} %get-tuple-element.73), channel_id=1, source_target_pairs={{0,28},{4,0},{8,4},{12,8},{16,12},{20,16},{24,20},{28,24},{1,29},{... | collective-permute-start | bytes 73736 | tf_op jit(solution)/shard_map/ppermute | solution.py:28
  26.7 3.4 %collective-permute-start.6 = (f32[48,128]{1,0:T(8,128)S(1)}, f32[48,128]{1,0:T(8,128)S(1)}, u32[]{:S(2)}, u32[]{:S(2)}) collective-permute-start(f32[48,128]{1,0:T(8,128)S(1)} %get-tuple-element.74), channel_id=1, source_target_pairs={{0,1},{1,2},{2,3},{3,0},{4,5},{5,6},{6,7},{7,4},{8,9},{9,10},{10,1... | collective-permute-start | bytes 73736 | tf_op jit(solution)/shard_map/ppermute | solution.py:28
  29.0 3.3 %collective-permute-start.7 = (f32[48,128]{1,0:T(8,128)S(1)}, f32[48,128]{1,0:T(8,128)S(1)}, u32[]{:S(2)}, u32[]{:S(2)}) collective-permute-start(f32[48,128]{1,0:T(8,128)S(1)} %get-tuple-element.75), channel_id=1, source_target_pairs={{0,3},{1,0},{2,1},{3,2},{4,7},{5,4},{6,5},{7,6},{8,11},{9,8},{10,9... | collective-permute-start | bytes 73736 | tf_op jit(solution)/shard_map/ppermute | solution.py:28
  36.5 5.9 %collective-permute-start.8 = (f32[24,128]{1,0:T(8,128)S(1)}, f32[24,128]{1,0:T(8,128)S(1)}, u32[]{:S(2)}, u32[]{:S(2)}) collective-permute-start(f32[24,128]{1,0:T(8,128)S(1)} %get-tuple-element.82), channel_id=1, source_target_pairs={{0,4},{4,8},{8,12},{12,16},{16,20},{20,24},{24,28},{28,0},{1,5},{5... | collective-permute-start | bytes 36872 | tf_op jit(solution)/shard_map/ppermute | solution.py:28
  36.5 5.8 %collective-permute-start.9 = (f32[24,128]{1,0:T(8,128)S(1)}, f32[24,128]{1,0:T(8,128)S(1)}, u32[]{:S(2)}, u32[]{:S(2)}) collective-permute-start(f32[24,128]{1,0:T(8,128)S(1)} %get-tuple-element.83), channel_id=1, source_target_pairs={{0,28},{4,0},{8,4},{12,8},{16,12},{20,16},{24,20},{28,24},{1,29},{... | collective-permute-start | bytes 36872 | tf_op jit(solution)/shard_map/ppermute | solution.py:28
  40.7 1.7 %collective-permute-start.10 = (f32[24,128]{1,0:T(8,128)S(1)}, f32[24,128]{1,0:T(8,128)S(1)}, u32[]{:S(2)}, u32[]{:S(2)}) collective-permute-start(f32[24,128]{1,0:T(8,128)S(1)} %get-tuple-element.84), channel_id=1, source_target_pairs={{0,1},{1,2},{2,3},{3,0},{4,5},{5,6},{6,7},{7,4},{8,9},{9,10},{10,1... | collective-permute-start | bytes 36872 | tf_op jit(solution)/shard_map/ppermute | solution.py:28
  41.3 3.1 %collective-permute-start.11 = (f32[24,128]{1,0:T(8,128)S(1)}, f32[24,128]{1,0:T(8,128)S(1)}, u32[]{:S(2)}, u32[]{:S(2)}) collective-permute-start(f32[24,128]{1,0:T(8,128)S(1)} %get-tuple-element.85), channel_id=1, source_target_pairs={{0,3},{1,0},{2,1},{3,2},{4,7},{5,4},{6,5},{7,6},{8,11},{9,8},{10,9... | collective-permute-start | bytes 36872 | tf_op jit(solution)/shard_map/ppermute | solution.py:28
  48.8 5.9 %collective-permute-start.12 = (f32[96,128]{1,0:T(8,128)S(1)}, f32[96,128]{1,0:T(8,128)S(1)}, u32[]{:S(2)}, u32[]{:S(2)}) collective-permute-start(f32[96,128]{1,0:T(8,128)S(1)} %get-tuple-element.93), channel_id=1, source_target_pairs={{0,4},{4,8},{8,12},{12,16},{16,20},{20,24},{24,28},{28,0},{1,5},{5... | collective-permute-start | bytes 147464 | tf_op jit(solution)/shard_map/ppermute | solution.py:28
  48.8 5.8 %collective-permute-start.13 = (f32[96,128]{1,0:T(8,128)S(1)}, f32[96,128]{1,0:T(8,128)S(1)}, u32[]{:S(2)}, u32[]{:S(2)}) collective-permute-start(f32[96,128]{1,0:T(8,128)S(1)} %get-tuple-element.94), channel_id=1, source_target_pairs={{0,28},{4,0},{8,4},{12,8},{16,12},{20,16},{24,20},{28,24},{1,29},{... | collective-permute-start | bytes 147464 | tf_op jit(solution)/shard_map/ppermute | solution.py:28
  53.0 1.8 %collective-permute-start.14 = (f32[96,128]{1,0:T(8,128)S(1)}, f32[96,128]{1,0:T(8,128)S(1)}, u32[]{:S(2)}, u32[]{:S(2)}) collective-permute-start(f32[96,128]{1,0:T(8,128)S(1)} %get-tuple-element.95), channel_id=1, source_target_pairs={{0,1},{1,2},{2,3},{3,0},{4,5},{5,6},{6,7},{7,4},{8,9},{9,10},{10,1... | collective-permute-start | bytes 147464 | tf_op jit(solution)/shard_map/ppermute | solution.py:28
  53.6 3.5 %collective-permute-start.15 = (f32[96,128]{1,0:T(8,128)S(1)}, f32[96,128]{1,0:T(8,128)S(1)}, u32[]{:S(2)}, u32[]{:S(2)}) collective-permute-start(f32[96,128]{1,0:T(8,128)S(1)} %get-tuple-element.96), channel_id=1, source_target_pairs={{0,3},{1,0},{2,1},{3,2},{4,7},{5,4},{6,5},{7,6},{8,11},{9,8},{10,9... | collective-permute-start | bytes 147464 | tf_op jit(solution)/shard_map/ppermute | solution.py:28
where the time goes:
time: 59.2 us; the launch traced here: 58.9 us
  starting transfers between devices  23.5 us (40%)
  Pallas kernels  23.3 us (39%)
  waiting for transfers between devices  6.57 us (11%)
  local copies, waits for them, and re-layouts  4.52 us (8%)
  other arithmetic  0.75 us (1%)
    ppermute x16, starting transfers between devices, from_behind(): return lax.ppermute(x, axis, [(i, (i + by) % size) for i in range(size)])  23.5 us
    pallas_call x10, Pallas kernels, call(): pl.pallas_call(body, out_shape=outs, in_specs=[pl.BlockSpec(memory_space=...  23.3 us
    ppermute x16, waiting for transfers between devices, from_behind(): return lax.ppermute(x, axis, [(i, (i + by) % size) for i in range(size)])  6.57 us
    unnamed x29, local copies, waits for them, and re-layouts  4.26 us
  transfers between devices with their start and end apart: 16, of which 4 were waited for; matrix products, arithmetic and copies ran while one was open for 0% of the time, Pallas kernels for 9%

commit v1 on v0

v1 whole, which is shorter than its diff:
```python
import functools

import jax
import jax.numpy as jnp
from jax import lax
from jax.experimental import pallas as pl
from jax.experimental.pallas import tpu as pltpu
from jax.sharding import PartitionSpec as P

FIELDS = 9
PAIRS = 5
MODES = 56
MODES_UP = 64
FACE_MODES = 21
FACE_UP = 24
ROWS = 2 * PAIRS * FACE_UP
DERIVS = 6
TICKS = 4
SLOT = 8
TIME_STEP = 1.0
F32 = jnp.float32
BF16 = jnp.bfloat16
BLOCKS = ((0, 32), (32, 24))
GROUPS = ((0, 1), (2, 3), (4,))


def paired(axis):
    return lax.axis_size(axis) % 2 == 0


def exchange(x, axis, phase):
    size = lax.axis_size(axis)
    if paired(axis):
        pairs = []
        for i in range(phase, size + phase, 2):
            one, two = i % size, (i + 1) % size
            pairs += [(one, two), (two, one)]
    else:
        by = 1 if phase == 0 else -1
        pairs = [(i, (i + by) % size) for i in range(size)]
    return lax.ppermute(x, axis, pairs)


def taylor_constants():
    width = TIME_STEP / TICKS
    table = []
    for begin in range(TICKS):
        factorial = 1.0
        row = []
        for order in range(DERIVS):
            factorial = factorial * (order + 1)
            span = float((begin + 1) ** (order + 1) - begin ** (order + 1))
            row.append(span * width ** (order + 1) / factorial)
        table.append(row)
    return table


def low_half(shape, half):
    return lax.broadcasted_iota(jnp.int32, shape, len(shape) - 1) < half


def swap(x, half):
    return pltpu.roll(x, half, x.ndim - 1)


def pair(a, b):
    return jnp.concatenate([a, b], axis=-1)


def halves(x):
    high = x.astype(BF16).astype(F32)
    return high, x - high


def pad_rows(x, rows):
    if x.shape[0] == rows:
        return x
    return jnp.concatenate([x, jnp.zeros((rows - x.shape[0], x.shape[1]), x.dtype)], axis=0)


def timing(cluster, tick):
    period = jnp.where(cluster == 0, 4, jnp.where(cluster == 1, 2, 1))
    offset = jnp.where(cluster == 0, tick % 4, jnp.where(cluster == 1, tick % 2, 0))
    return offset, offset == period - 1


def right_operand(values):
    values = pad_rows(values, MODES_UP)
    high = values.astype(BF16)
    low = (values - high.astype(F32)).astype(BF16)
    return jnp.concatenate([high, high, low], axis=0)


def left_parts(matrix, up):
    rows = matrix.shape[0]
    if up > matrix.shape[1]:
        matrix = jnp.concatenate([matrix, jnp.zeros((rows, up - matrix.shape[1]), F32)], axis=1)
    high, low = halves(matrix)
    return jnp.concatenate([high, low, high], axis=1)


def send_choice(even, forward, backward):
    return jnp.where(even, forward, backward), jnp.where(even, backward, forward)


def parity(axis):
    if not paired(axis):
        return True, False
    even = lax.rem(lax.axis_index(axis), 2) == 0
    return even, even


def products(m_ref, slot, left, values, dirs, group, lanes):
    out = jnp.dot(left, right_operand(values), preferred_element_type=F32)
    if group == GROUPS[-1]:
        low = low_half((MODES, lanes), lanes // 2)
        for i in range(0, dirs, 2):
            one = out[i * MODES : (i + 1) * MODES]
            if i + 1 < dirs:
                one = jnp.where(low, one, out[(i + 1) * MODES : (i + 2) * MODES])
            m_ref[slot, (i // 2) * MODES : (i // 2 + 1) * MODES, group[0] * lanes : (group[0] + 1) * lanes] = one
    else:
        m_ref[slot, 0 : dirs * MODES, group[0] * lanes : (group[-1] + 1) * lanes] = out


def contract(m_ref, slot, coef_ref, dirs, group, lanes):
    half = lanes // 2
    fields = [g for q in group for g in (2 * q, 2 * q + 1) if g < FIELDS]
    terms = [(d, q, q, d) for q in range(PAIRS - 1) for d in range(dirs)]
    terms += [(i, PAIRS - 1, PAIRS - 1, i) for i in range((dirs + 1) // 2)]
    columns = {q: [] for q in group}
    for row, count in BLOCKS:
        sums = {}
        for d, q, block, line in terms:
            values = m_ref[slot, d * MODES + row : d * MODES + row + count, q * lanes : (q + 1) * lanes]
            for g in fields:
                term = coef_ref[block * FIELDS + g, line : line + 1, :] * values
                sums[g] = sums[g] + term if g in sums else term
        low = low_half((count, lanes), half)
        for q in group:
            first = sums[2 * q]
            if 2 * q + 1 < FIELDS:
                second = sums[2 * q + 1]
                result = jnp.where(low, first, second) + swap(jnp.where(low, second, first), half)
            else:
                result = first + swap(first, half)
            columns[q].append(result)
    columns = [jnp.concatenate(columns[q], axis=0) for q in group]
    return columns[0] if len(columns) == 1 else jnp.concatenate(columns, axis=1)


def span(group, lanes):
    return slice(group[0] * lanes, (group[-1] + 1) * lanes)


def predict(state_of, ck_ref, star_ref, weight_ref, proj_ref, face_ref, m_ref, i_ref, lanes):
    def weight(order, group):
        row = weight_ref[order : order + 1, :]
        return row if len(group) == 1 else pair(row, row)

    for group in GROUPS:
        values = state_of(group)
        i_ref[:, span(group, lanes)] = weight(0, group) * values
        products(m_ref, 0, ck_ref[...], values, 3, group, lanes)
    for order in range(1, DERIVS):
        for group in GROUPS:
            values = contract(m_ref, (order - 1) % 2, star_ref, 3, group, lanes)
            total = i_ref[:, span(group, lanes)] + weight(order, group) * values
            i_ref[:, span(group, lanes)] = total
            if order < DERIVS - 1:
                products(m_ref, order % 2, ck_ref[...], values, 3, group, lanes)
            else:
                face_ref[:, span(group, lanes)] = jnp.dot(
                    proj_ref[...], right_operand(total), preferred_element_type=F32
                )


def store_weights(weight_ref, cluster, tick):
    offset, _ = timing(cluster, tick)
    table = taylor_constants()
    for order in range(DERIVS):
        row = jnp.full(cluster.shape, table[0][order], F32)
        for begin in range(1, TICKS):
            row = jnp.where(offset == begin, table[begin][order], row)
        weight_ref[order : order + 1, :] = row


def fill_table(face_ref, table_ref, lanes):
    half = lanes // 2
    low = low_half((FACE_UP, lanes), half)
    for q in range(PAIRS):
        for k in range(2):
            one = face_ref[2 * k * FACE_UP : (2 * k + 1) * FACE_UP, q * lanes : (q + 1) * lanes]
            two = face_ref[(2 * k + 1) * FACE_UP : (2 * k + 2) * FACE_UP, q * lanes : (q + 1) * lanes]
            crossed = swap(jnp.where(low, two, one), half)
            table_ref[2 * q * FACE_UP : (2 * q + 1) * FACE_UP, k * lanes : (k + 1) * lanes] = jnp.where(low, one, crossed)
            table_ref[(2 * q + 1) * FACE_UP : (2 * q + 2) * FACE_UP, k * lanes : (k + 1) * lanes] = jnp.where(
                low, crossed, two
            )


def pick(table, chosen):
    rows = table.shape[0]
    high, low = halves(table)
    both = jnp.concatenate([high, low], axis=0).astype(BF16)
    out = jnp.dot(both, chosen, preferred_element_type=F32)
    return out[:rows] + out[rows:]


def one_hot(index_row, rows):
    sub = lax.broadcasted_iota(jnp.int32, (rows, index_row.shape[1]), 0)
    return jnp.where(sub == index_row, 1.0, 0.0).astype(BF16)


def lane_places(rows, lanes):
    lane = lax.broadcasted_iota(jnp.int32, (rows, lanes), 1)
    return lane // (4 * SLOT), (lane // SLOT) % 4


def send_rows(face_ref, elem_ref, lanes):
    slots = face_ref.shape[1]
    half = lanes // 2
    index = face_ref[...] * half + elem_ref[...]
    index = jnp.concatenate([index] * (lanes // slots), axis=1)
    _, place = lane_places(1, lanes)
    rows = []
    for group in range(slots // SLOT):
        row = None
        for d in range(4):
            shift = ((d - group) * SLOT) % lanes
            moved = index[d : d + 1, :]
            moved = pltpu.roll(moved, shift, 1) if shift else moved
            row = moved if row is None else jnp.where(place == d, moved, row)
        rows.append(row)
    return rows


def fill_messages(tables, chosen, out_refs, lanes):
    column, place = lane_places(FACE_UP, lanes)
    for group, table in enumerate(tables):
        picked = pick(table, chosen(group))
        quads = []
        for quad in range(3):
            merged = picked[4 * quad * FACE_UP : (4 * quad + 1) * FACE_UP]
            for c in range(1, 4):
                f = 4 * quad + c
                if f < FIELDS:
                    merged = jnp.where(column == c, picked[f * FACE_UP : (f + 1) * FACE_UP], merged)
            quads.append(merged)
        messages = []
        for d in range(4):
            message = None
            for quad in range(3):
                shift = ((quad - d) * SLOT) % lanes
                moved = quads[quad] if shift == 0 else pltpu.roll(quads[quad], shift, 1)
                message = moved if message is None else jnp.where(place == quad, moved, message)
            messages.append(message)
        for axis, first in (("slab", 0), ("sub", 2)):
            even, _ = parity(axis)
            one, two = send_choice(even, messages[first], messages[first + 1])
            out_refs[first][group * FACE_UP : (group + 1) * FACE_UP, :] = one
            out_refs[first + 1][group * FACE_UP : (group + 1) * FACE_UP, :] = two


def face_operand(values):
    high, low = halves(values)
    return jnp.concatenate([high, high, low, jnp.zeros((SLOT, values.shape[1]), F32)], axis=0).astype(BF16)


def take_messages(in_refs, groups, far_ref, turn_ref, lanes):
    column, place = lane_places(FACE_UP, lanes)
    quads = []
    for group in range(groups):
        arrived = [ref[group * FACE_UP : (group + 1) * FACE_UP, :] for ref in in_refs]
        for axis, first in (("slab", 0), ("sub", 2)):
            _, even = parity(axis)
            arrived[first], arrived[first + 1] = send_choice(even, arrived[first + 1], arrived[first])
        for quad in range(3):
            merged = None
            for d in range(4):
                shift = ((d - quad) * SLOT) % lanes
                moved = arrived[d] if shift == 0 else pltpu.roll(arrived[d], shift, 1)
                merged = moved if merged is None else jnp.where(place == d, moved, merged)
            quads.append(merged)
    turned = jnp.dot(turn_ref[...], face_operand(jnp.concatenate(quads, axis=1)), preferred_element_type=F32)
    high, low = halves(turned)
    lefts = []
    for part in (high, low):
        columns = []
        for group in range(groups):
            for which in range(3):
                rows = slice(which * FACE_UP, (which + 1) * FACE_UP)
                pieces = []
                for f in range(FIELDS):
                    at = (3 * group + f // 4) * lanes
                    pieces.append(jnp.where(column == f % 4, part[rows, at : at + lanes], 0.0))
                pieces.append(jnp.zeros((FACE_UP, lanes), F32))
                columns.append(jnp.concatenate(pieces, axis=0))
        lefts.append(jnp.concatenate(columns, axis=1))
    left = jnp.concatenate(lefts, axis=0).astype(BF16)
    out = jnp.dot(left, far_ref[0 : 3 * groups * lanes, :], preferred_element_type=F32)
    return out[:ROWS] + out[ROWS:]


def gather_faces(in_refs, groups, near_ref, far_ref, turn_ref, aplus_ref, c_ref, lanes):
    half = lanes // 2
    low = low_half((FACE_UP, lanes), half)
    values = near_ref[...] + take_messages(in_refs, groups, far_ref, turn_ref, lanes)
    for group in GROUPS:
        fields = [g for q in group for g in (2 * q, 2 * q + 1) if g < FIELDS]
        for k in range(2):
            sums = {}
            for f in range(FIELDS):
                part = values[f * FACE_UP : (f + 1) * FACE_UP, k * lanes : (k + 1) * lanes]
                for g in fields:
                    term = aplus_ref[f * FIELDS + g, k : k + 1, :] * part
                    sums[g] = sums[g] + term if g in sums else term
            for q in group:
                first = sums[2 * q]
                second = sums[min(2 * q + 1, FIELDS - 1)]
                crossed = swap(jnp.where(low, second, first), half)
                sides = jnp.concatenate([jnp.where(low, first, crossed), jnp.where(low, crossed, second)], axis=0)
                high = sides.astype(BF16)
                rest = (sides - high.astype(F32)).astype(BF16)
                at, cols = 2 * k * FACE_UP, slice(q * lanes, (q + 1) * lanes)
                c_ref[at : at + 2 * FACE_UP, cols] = high
                c_ref[4 * FACE_UP + at : 4 * FACE_UP + at + 2 * FACE_UP, cols] = high
                c_ref[8 * FACE_UP + at : 8 * FACE_UP + at + 2 * FACE_UP, cols] = rest


def updated(c_ref, lift_ref, base_ref, finished, group, lanes):
    cols = span(group, lanes)
    outer = jnp.dot(lift_ref[...], c_ref[:, cols], preferred_element_type=F32)
    before = base_ref[:, cols]
    done = finished if len(group) == 1 else jnp.concatenate([finished, finished], axis=1)
    return jnp.where(done, before - outer, before)


def pack_coefs(ref, dirs, base, out_ref):
    for q in range(PAIRS - 1):
        for g in range(FIELDS):
            out_ref[q * FIELDS + g, base : base + dirs, :] = pair(ref[2 * q, g], ref[2 * q + 1, g])


def pack_last(lines, g, out_ref):
    for i in range(0, len(lines), 2):
        other = lines[i + 1] if i + 1 < len(lines) else jnp.zeros_like(lines[i])
        out_ref[(PAIRS - 1) * FIELDS + g, i // 2 : i // 2 + 1, :] = pair(lines[i], other)


def first_kernel(
    state_hbm, star_hbm, ck_hbm, project_hbm, cluster_hbm, elem_hbm, face_hbm,
    aminus_hbm, aplus_hbm, vol_hbm, flux_hbm, lift_hbm, rotate_hbm, neighbour_hbm, orient_hbm,
    m0, m1, m2, m3, packed_ref, star_out, ck_out, proj_out, i_ref, table_ref, send_out, star_ref, cluster_ref,
    aminus_out, aplus_out, vol_out, flux_out, lift_out, rotate_out, neighbour_out, orient_out,
    state_ref, ck_ref, project_ref, elem_ref, face_ref, weight_ref, faces_ref, m_ref, early, late, *, lanes,
):
    soon = [
        pltpu.make_async_copy(source, target, early.at[i])
        for i, (source, target) in enumerate((
            (cluster_hbm, cluster_ref), (ck_hbm, ck_ref), (state_hbm, state_ref), (star_hbm, star_ref),
            (project_hbm, project_ref), (elem_hbm, elem_ref), (face_hbm, face_ref),
        ))
    ]
    then = [
        pltpu.make_async_copy(source, target, late.at[i])
        for i, (source, target) in enumerate((
            (aminus_hbm, aminus_out), (aplus_hbm, aplus_out), (vol_hbm, vol_out), (flux_hbm, flux_out),
            (lift_hbm, lift_out), (rotate_hbm, rotate_out), (neighbour_hbm, neighbour_out), (orient_hbm, orient_out),
        ))
    ]
    for copy in soon + then:
        copy.start()
    for copy in soon:
        copy.wait()
    for q in range(PAIRS):
        packed_ref[:, q * lanes : (q + 1) * lanes] = pair(state_ref[2 * q], state_ref[min(2 * q + 1, FIELDS - 1)])
    pack_coefs(star_ref, 3, 0, star_out)
    for g in range(FIELDS):
        both = star_ref[FIELDS - 1, g]
        pack_last([both[d : d + 1] for d in range(3)], g, star_out)
    ck_out[...] = left_parts(-ck_ref[...].reshape(3 * MODES, MODES), MODES_UP).astype(BF16)
    proj_rows = [pad_rows(project_ref[:, j, :], FACE_UP) for j in range(4)]
    proj_out[...] = left_parts(jnp.concatenate(proj_rows, axis=0), MODES_UP).astype(BF16)
    rows = send_rows(face_ref, elem_ref, lanes)
    for i, row in enumerate(rows):
        send_out[i : i + 1, :] = row
    store_weights(weight_ref, pair(cluster_ref[...], cluster_ref[...]), 0)

    def state_of(group):
        return packed_ref[:, span(group, lanes)]

    predict(state_of, ck_out, star_out, weight_ref, proj_out, faces_ref, m_ref, i_ref, lanes)
    fill_table(faces_ref, table_ref, lanes)
    fill_messages([table_ref[...]], lambda group: one_hot(rows[0], 2 * lanes), (m0, m1, m2, m3), lanes)
    for copy in then:
        copy.wait()


def prepare_kernel(
    star_ref, aminus_ref, aplus_ref, vol_ref, flux_ref, lift_ref, rotate_ref, neighbour_ref, orient_ref, send_ref,
    coef_out, aplus_out, left_out, lift_out, turn_out, near_out, far_out, send_out, *, lanes,
):
    half = lanes // 2
    pack_coefs(star_ref, 3, 0, coef_out)
    pack_coefs(aminus_ref, 4, 3, coef_out)
    for g in range(FIELDS):
        ahead, behind = star_ref[FIELDS - 1, g], aminus_ref[FIELDS - 1, g]
        pack_last([ahead[d : d + 1] for d in range(3)] + [behind[j : j + 1] for j in range(4)], g, coef_out)
        for f in range(FIELDS):
            own = aplus_ref[f, g]
            for k in range(2):
                aplus_out[f * FIELDS + g, k : k + 1, :] = pair(own[2 * k : 2 * k + 1], own[2 * k + 1 : 2 * k + 2])
    both = jnp.concatenate([vol_ref[...].reshape(3 * MODES, MODES), -flux_ref[...].reshape(4 * MODES, MODES)], axis=0)
    left_out[...] = left_parts(both, MODES_UP).astype(BF16)
    lift = jnp.concatenate([pad_rows(lift_ref[:, j, :], FACE_UP) for j in range(4)], axis=0)
    lift = jnp.concatenate([lift, jnp.zeros((4 * FACE_UP, lanes - MODES), F32)], axis=1)
    lift = jnp.transpose(pad_rows(lift, lanes))[0:MODES, 0 : 4 * FACE_UP]
    lift_out[...] = left_parts(lift, 4 * FACE_UP).astype(BF16)
    turns = jnp.concatenate([pad_rows(rotate_ref[which], FACE_UP) for which in range(3)], axis=0)
    turn_out[...] = jnp.concatenate([left_parts(turns, FACE_UP), jnp.zeros((3 * FACE_UP, SLOT), F32)], axis=1).astype(BF16)
    row = jnp.concatenate([neighbour_ref[j : j + 1, :] for j in range(4)], axis=1)
    turned = jnp.concatenate([orient_ref[j : j + 1, :] for j in range(4)], axis=1)
    near_out[...] = one_hot(row, 4 * half)
    sub = lax.broadcasted_iota(jnp.int32, (lanes, 4 * half), 0)
    for group in range(4):
        target = 4 * half + ((sub // SLOT) % 4) * (4 * SLOT) + group * SLOT + sub % SLOT
        for which in range(3):
            at = (3 * group + which) * lanes
            hit = (target == row) & (turned == which)
            far_out[at : at + lanes, :] = jnp.where(hit, 1.0, 0.0).astype(BF16)
    for group in range(send_ref.shape[0]):
        send_out[:, group * lanes : (group + 1) * lanes] = one_hot(send_ref[group : group + 1, :], 4 * half)


def local_kernel(
    i_ref, packed_ref, table_ref, cluster_ref, coef_ref, left_ref, near_ref, turn_ref, orient_ref, own_ref, seen_ref,
    base_out, own_out, seen_out, m_ref, *, lanes, tick,
):
    cluster = pair(cluster_ref[...], cluster_ref[...])
    offset, finished = timing(cluster, tick)
    two = jnp.concatenate([offset, offset], axis=1)
    for group in GROUPS:
        cols = span(group, lanes)
        values = i_ref[:, cols]
        if tick:
            fresh = (offset if len(group) == 1 else two) == 0
            values = jnp.where(fresh, values, own_ref[:, cols] + values)
        own_out[:, cols] = values
        products(m_ref, 0, left_ref[...], values, 7, group, lanes)
    seen = pick(table_ref[...], near_ref[...])
    which = jnp.concatenate([orient_ref[j : j + 1, :] for j in range(4)], axis=1)
    for f in range(FIELDS):
        rows = slice(f * FACE_UP, (f + 1) * FACE_UP)
        turned = jnp.dot(turn_ref[...], face_operand(seen[rows]), preferred_element_type=F32)
        part = jnp.where(
            which == 0,
            turned[0:FACE_UP],
            jnp.where(which == 1, turned[FACE_UP : 2 * FACE_UP], turned[2 * FACE_UP : 3 * FACE_UP]),
        )
        seen_out[rows, :] = jnp.where(two == 0, part, seen_ref[rows, :] + part) if tick else part
    seen_out[FIELDS * FACE_UP :, :] = jnp.zeros((ROWS - FIELDS * FACE_UP, 2 * lanes), F32)
    for group in GROUPS:
        cols = span(group, lanes)
        before = packed_ref[:, cols]
        change = contract(m_ref, 0, coef_ref, 7, group, lanes)
        done = finished if len(group) == 1 else jnp.concatenate([finished, finished], axis=1)
        base_out[:, cols] = jnp.where(done, before + change, before)


def tick_kernel(
    r0, r1, r2, r3, near_ref, far_ref, turn_ref, aplus_ref, lift_ref, base_ref, cluster_ref,
    ck_ref, proj_ref, star_ref, send_ref, *rest, lanes, tick, olds, groups,
):
    old_refs = rest[:olds]
    m0, m1, m2, m3, packed_ref, i_ref, table_ref = rest[olds : olds + 7]
    rest = rest[olds + 7 :]
    sum_ref = None
    if tick == 1:
        sum_ref, rest = rest[0], rest[1:]
    weight_ref, faces_ref, m_ref, c_ref = rest
    cluster = pair(cluster_ref[...], cluster_ref[...])
    _, finished = timing(cluster, tick - 1)
    store_weights(weight_ref, cluster, tick)
    gather_faces((r0, r1, r2, r3), groups, near_ref, far_ref, turn_ref, aplus_ref, c_ref, lanes)

    def state_of(group):
        values = updated(c_ref, lift_ref, base_ref, finished, group, lanes)
        packed_ref[:, span(group, lanes)] = values
        return values

    predict(state_of, ck_ref, star_ref, weight_ref, proj_ref, faces_ref, m_ref, i_ref, lanes)
    fill_table(faces_ref, table_ref, lanes)
    table = table_ref[...]
    tables = [table]
    if tick == 1:
        two = old_refs[0][...] + table
        sum_ref[...] = two
        tables.append(two)
    if tick == 3:
        two = old_refs[0][...] + table
        four = old_refs[1][...] + two
        tables += [two, four, four]
    fill_messages(tables, lambda group: send_ref[:, group * lanes : (group + 1) * lanes], (m0, m1, m2, m3), lanes)


def last_kernel(
    r0, r1, r2, r3, near_ref, far_ref, turn_ref, aplus_ref, lift_ref, base_ref, cluster_ref, out_ref, c_ref, *, lanes,
):
    half = lanes // 2
    _, finished = timing(pair(cluster_ref[...], cluster_ref[...]), TICKS - 1)
    gather_faces((r0, r1, r2, r3), 4, near_ref, far_ref, turn_ref, aplus_ref, c_ref, lanes)
    for group in GROUPS:
        values = updated(c_ref, lift_ref, base_ref, finished, group, lanes)
        for i, q in enumerate(group):
            for side in range(2):
                if 2 * q + side < FIELDS:
                    out_ref[2 * q + side] = values[:, i * lanes + side * half : i * lanes + (side + 1) * half]


def call(body, outs, scratch, name, flops, arrays, far=False):
    moved = sum(a.size * a.dtype.itemsize for a in arrays)
    space = pltpu.MemorySpace.HBM if far else pltpu.VMEM
    if far:
        arrays = [pltpu.with_memory_space_constraint(x, pltpu.MemorySpace.HBM) for x in arrays]
    return pl.pallas_call(
        body,
        out_shape=outs,
        in_specs=[pl.BlockSpec(memory_space=space)] * len(arrays),
        out_specs=[pl.BlockSpec(memory_space=pltpu.VMEM)] * len(outs),
        scratch_shapes=scratch,
        compiler_params=pltpu.CompilerParams(vmem_limit_bytes=24 << 20),
        cost_estimate=pl.CostEstimate(flops=flops, bytes_accessed=moved, transcendentals=0),
        name=name,
    )(*arrays)


def shards(
    state, star, aminus, aplus, ck_stiff, vol_stiff, flux_local, lift, rotate, project,
    cluster, orient, neighbour, send_elem, send_face,
):
    elems = state.shape[-1]
    lanes = 2 * elems
    wide = PAIRS * lanes
    groups = send_elem.shape[1] // SLOT
    shape = jax.ShapeDtypeStruct
    cluster_row = cluster.reshape(1, elems)
    star, aminus, aplus = (jnp.transpose(x, (1, 2, 0, 3)) for x in (star, aminus, aplus))
    project = jnp.transpose(project, (1, 0, 2))
    lift = jnp.transpose(lift, (2, 0, 1))

    modal = shape((MODES, wide), F32)
    table = shape((ROWS, 4 * elems), F32)
    weights = pltpu.VMEM((SLOT, lanes), F32)
    faces = pltpu.VMEM((4 * FACE_UP, wide), F32)
    staged = pltpu.VMEM((2, 3 * MODES, wide), F32)
    sides = pltpu.VMEM((12 * FACE_UP, wide), BF16)

    def like(x):
        return shape(x.shape, x.dtype)

    def room(x):
        return pltpu.VMEM(x.shape, x.dtype)

    def message(count):
        return [shape((count * FACE_UP, lanes), F32)] * 4

    late = (aminus, aplus, vol_stiff, flux_local, lift, rotate, neighbour, orient)
    out = call(
        functools.partial(first_kernel, lanes=lanes),
        message(1)
        + [
            modal,
            shape((PAIRS * FIELDS, 3, lanes), F32),
            shape((3 * MODES, 3 * MODES_UP), BF16),
            shape((4 * FACE_UP, 3 * MODES_UP), BF16),
            modal,
            table,
            shape((groups, lanes), jnp.int32),
            like(star),
            like(cluster_row),
        ]
        + [like(x) for x in late],
        [room(state), room(ck_stiff), room(project), room(send_elem), room(send_face), weights, faces, staged]
        + [pltpu.SemaphoreType.DMA((7,)), pltpu.SemaphoreType.DMA((len(late),))],
        "first", 400_000_000,
        (state, star, ck_stiff, project, cluster_row, send_elem, send_face, *late), far=True,
    )
    messages, out = out[:4], out[4:]
    packed, star_pairs, ck_left, proj_left, integral, table_now, send, star, cluster_row = out[:9]
    late = out[9:]
    orient = late[-1]
    coef, aplus_pairs, left, lift_left, turn, near_hot, far_hot, send_hot = call(
        functools.partial(prepare_kernel, lanes=lanes),
        [
            shape((PAIRS * FIELDS, 7, lanes), F32),
            shape((FIELDS * FIELDS, 2, lanes), F32),
            shape((7 * MODES, 3 * MODES_UP), BF16),
            shape((MODES, 12 * FACE_UP), BF16),
            shape((3 * FACE_UP, 80), BF16),
            shape((4 * elems, 4 * elems), BF16),
            shape((12 * lanes, 4 * elems), BF16),
            shape((4 * elems, groups * lanes), BF16),
        ],
        [],
        "prepare", 100_000_000,
        (star, *late, send),
    )
    own = integral
    seen = table_now
    two = None
    for tick in range(TICKS):
        arrived = [None] * 4
        for slot, axis, phase in ((1, "slab", 1), (0, "slab", 0), (3, "sub", 1), (2, "sub", 0)):
            arrived[slot] = exchange(messages[slot], axis, phase)
        base, own, seen = call(
            functools.partial(local_kernel, lanes=lanes, tick=tick),
            [modal, modal, table],
            [pltpu.VMEM((1, 7 * MODES, wide), F32)],
            f"local{tick}", 300_000_000,
            (integral, packed, table_now, cluster_row, coef, left, near_hot, turn, orient, own, seen),
        )
        count = (1, 2, 1, 4)[tick]
        common = (*arrived, seen, far_hot, turn, aplus_pairs, lift_left, base, cluster_row)
        if tick == TICKS - 1:
            return call(
                functools.partial(last_kernel, lanes=lanes),
                [shape(state.shape, F32)],
                [sides],
                "last", 100_000_000, common,
            )[0]
        olds = {0: (table_now,), 1: (), 2: (table_now, two)}[tick]
        sends = (1, 2, 1, 4)[tick + 1]
        out = call(
            functools.partial(tick_kernel, lanes=lanes, tick=tick + 1, olds=len(olds), groups=count),
            message(sends) + [modal, modal, table] + ([table] if tick == 0 else []),
            [weights, faces, staged, sides],
            f"tick{tick + 1}", 500_000_000,
            (*common, ck_left, proj_left, star_pairs, send_hot, *olds),
        )
        messages, (packed, integral, table_now) = out[:4], out[4:7]
        if tick == 0:
            two = out[7]


def solution(mesh):
    placed = (
        P(None, None, ("slab", "sub")),
        P(None, None, None, ("slab", "sub")),
        P(None, None, None, ("slab", "sub")),
        P(None, None, None, ("slab", "sub")),
        P(),
        P(),
        P(),
        P(),
        P(),
        P(),
        P(("slab", "sub")),
        P(None, ("slab", "sub")),
        P(None, ("slab", "sub")),
        P(None, ("slab", "sub")),
        P(None, ("slab", "sub")),
    )
    return jax.shard_map(
        shards,
        mesh=mesh,
        in_specs=placed,
        out_specs=P(None, None, ("slab", "sub")),
        check_vma=False,
    )
```

time: 59.2 us -> 48.8 us (0.82)
  local copies, waits for them, and re-layouts: 4.52 us -> 0 us
  waiting for transfers between devices: 6.57 us -> 2.95 us
  starting transfers between devices: 23.5 us -> 21.4 us
  other arithmetic: 0.75 us -> 0 us
    unnamed x29 -> x0, local copies, waits for them, and re-layouts: 4.26 us -> none
    ppermute x16, waiting for transfers between devices: 6.57 us -> 2.95 us  [exchange(): return lax.ppermute(x, axis, pairs)]
    ppermute x16, starting transfers between devices: 23.5 us -> 21.4 us  [exchange(): return lax.ppermute(x, axis, pairs)]
    add x1 -> x0, other arithmetic: 0.71 us -> none  [shards(): send = (send_face * elems + send_elem).reshape(4, groups, SLOT)]
  transfers between devices with their start and end apart: 16 -> 16, of which waited for: 4 -> 4; matrix products, arithmetic and copies ran while one was open for 0% -> 0% of each run, Pallas kernels for 9% -> 11%
where the time goes in v1:
time: 48.8 us; the launch traced here: 48.4 us
  Pallas kernels  23.8 us (49%)
  starting transfers between devices  21.4 us (44%)
  waiting for transfers between devices  2.95 us (6%)
    pallas_call x10, Pallas kernels, call(): pl.pallas_call(body, out_shape=outs, in_specs=[pl.BlockSpec(memory_space=...  23.8 us
    ppermute x16, starting transfers between devices, exchange(): return lax.ppermute(x, axis, pairs)  21.4 us
    ppermute x16, waiting for transfers between devices, exchange(): return lax.ppermute(x, axis, pairs)  2.95 us
  transfers between devices with their start and end apart: 16, of which 4 were waited for; matrix products, arithmetic and copies ran while one was open for 0% of the time, Pallas kernels for 11%

profile of v1, /device:TPU:1, one launch (start us, length us, event | category | flops | bytes accessed | tf_op | source)
XLA Modules:
  0.0 48.4 jit_solution(1594754533701192136)
XLA Ops:
  0.0 4.3 %first.1 = (f32[24,128]{1,0:T(8,128)S(1)}, f32[24,128]{1,0:T(8,128)S(1)}, f32[24,128]{1,0:T(8,128)S(1)}, f32[24,128]{1,0:T(8,128)S(1)}, f32[56,640]{1,0:T(8,128)...) custom-call(f32[9,56,64]{2,1,0:T(8,128)} %state_hbm.1, ...), custom_call_target="tpu_custom_call" | custom-call | flops 400000000 | bytes 528812 | tf_op jit(solution)/shard_map/first/pallas_call | solution.py:526
  4.3 2.1 %collective-permute-start = (f32[24,128]{1,0:T(8,128)S(1)}, f32[24,128]{1,0:T(8,128)S(1)}, u32[]{:S(2)}, u32[]{:S(2)}) collective-permute-start(f32[24,128]{1,0:T(8,128)S(1)} %get-tuple-element.67), channel_id=1, source_target_pairs={{0,4},{4,0},{8,12},{12,8},{16,20},{20,16},{24,28},{28,24},{1,5},{5... | collective-permute-start | bytes 36872 | tf_op jit(solution)/shard_map/ppermute | solution.py:41
  6.4 3.3 %collective-permute-start.1 = (f32[24,128]{1,0:T(8,128)S(1)}, f32[24,128]{1,0:T(8,128)S(1)}, u32[]{:S(2)}, u32[]{:S(2)}) collective-permute-start(f32[24,128]{1,0:T(8,128)S(1)} %get-tuple-element.68), channel_id=1, source_target_pairs={{4,8},{8,4},{12,16},{16,12},{20,24},{24,20},{28,0},{0,28},{5,9},{9... | collective-permute-start | bytes 36872 | tf_op jit(solution)/shard_map/ppermute | solution.py:41
  9.7 1.2 %collective-permute-start.2 = (f32[24,128]{1,0:T(8,128)S(1)}, f32[24,128]{1,0:T(8,128)S(1)}, u32[]{:S(2)}, u32[]{:S(2)}) collective-permute-start(f32[24,128]{1,0:T(8,128)S(1)} %get-tuple-element.69), channel_id=1, source_target_pairs={{0,1},{1,0},{2,3},{3,2},{4,5},{5,4},{6,7},{7,6},{8,9},{9,8},{10,11... | collective-permute-start | bytes 36872 | tf_op jit(solution)/shard_map/ppermute | solution.py:41
  10.9 1.1 %collective-permute-start.3 = (f32[24,128]{1,0:T(8,128)S(1)}, f32[24,128]{1,0:T(8,128)S(1)}, u32[]{:S(2)}, u32[]{:S(2)}) collective-permute-start(f32[24,128]{1,0:T(8,128)S(1)} %get-tuple-element.70), channel_id=1, source_target_pairs={{1,2},{2,1},{3,0},{0,3},{5,6},{6,5},{7,4},{4,7},{9,10},{10,9},{11,... | collective-permute-start | bytes 36872 | tf_op jit(solution)/shard_map/ppermute | solution.py:41
  12.0 0.6 %prepare.1 = (f32[45,7,128]{2,1,0:T(8,128)S(1)}, f32[81,2,128]{2,1,0:T(2,128)S(1)}, bf16[392,192]{1,0:T(8,128)(2,1)S(1)}, bf16[56,288]{1,0:T(8,128)(2,1)S(1)}, b...) custom-call(f32[9,9,3,64]{3,2,1,0:T(4,128)S(1)} %get-tuple-element.7, ...), custom_call_target="tpu_custom_call" | custom-call | flops 100000000 | bytes 344108 | tf_op jit(solution)/shard_map/prepare/pallas_call | solution.py:526
  12.6 1.1 %local0.1 = (f32[56,640]{1,0:T(8,128)S(1)}, f32[56,640]{1,0:T(8,128)S(1)}, f32[240,256]{1,0:T(8,128)S(1)}) custom-call(f32[56,640]{1,0:T(8,128)S(1)} %get-tuple-element.71.i_ref.own_ref, f32[56,640]{1,0:T(8,128)S(1)} %get-tuple-element.72.packed_ref, f32[240,256]{1,0:T(8,128)S(1)} %get-tuple-element.73.table_ref.seen_ref.rest_0_, ...), custom_call_target="tpu_custom_call" | custom-call | flops 300000000 | bytes 1377280 | tf_op jit(solution)/shard_map/local0/pallas_call | solution.py:526
  13.7 0.0 collective-permute-done.r0
  13.7 0.0 collective-permute-done.1.r1
  13.8 0.0 collective-permute-done.2.r2
  13.8 0.3 collective-permute-done.3.r3
  14.0 4.0 %tick1.1 = (f32[48,128]{1,0:T(8,128)S(1)}, f32[48,128]{1,0:T(8,128)S(1)}, f32[48,128]{1,0:T(8,128)S(1)}, f32[48,128]{1,0:T(8,128)S(1)}, f32[56,640]{1,0:T(8,128)...) custom-call(f32[24,128]{1,0:T(8,128)S(1)} %collective-permute-done.r0, ...), custom_call_target="tpu_custom_call" | custom-call | flops 500000000 | bytes 2030080 | tf_op jit(solution)/shard_map/tick1/pallas_call | solution.py:526
  18.0 0.1 collective-permute-start.4
  18.1 1.6 %collective-permute-start.5 = (f32[48,128]{1,0:T(8,128)S(1)}, f32[48,128]{1,0:T(8,128)S(1)}, u32[]{:S(2)}, u32[]{:S(2)}) collective-permute-start(f32[48,128]{1,0:T(8,128)S(1)} %get-tuple-element.99), channel_id=1, source_target_pairs={{4,8},{8,4},{12,16},{16,12},{20,24},{24,20},{28,0},{0,28},{5,9},{9... | collective-permute-start | bytes 73736 | tf_op jit(solution)/shard_map/ppermute | solution.py:41
  19.7 1.7 %collective-permute-start.6 = (f32[48,128]{1,0:T(8,128)S(1)}, f32[48,128]{1,0:T(8,128)S(1)}, u32[]{:S(2)}, u32[]{:S(2)}) collective-permute-start(f32[48,128]{1,0:T(8,128)S(1)} %get-tuple-element.100), channel_id=1, source_target_pairs={{0,1},{1,0},{2,3},{3,2},{4,5},{5,4},{6,7},{7,6},{8,9},{9,8},{10,11... | collective-permute-start | bytes 73736 | tf_op jit(solution)/shard_map/ppermute | solution.py:41
  21.4 1.1 %collective-permute-start.7 = (f32[48,128]{1,0:T(8,128)S(1)}, f32[48,128]{1,0:T(8,128)S(1)}, u32[]{:S(2)}, u32[]{:S(2)}) collective-permute-start(f32[48,128]{1,0:T(8,128)S(1)} %get-tuple-element.101), channel_id=1, source_target_pairs={{1,2},{2,1},{3,0},{0,3},{5,6},{6,5},{7,4},{4,7},{9,10},{10,9},{11,... | collective-permute-start | bytes 73736 | tf_op jit(solution)/shard_map/ppermute | solution.py:41
  22.6 1.2 %local1.1 = (f32[56,640]{1,0:T(8,128)S(1)}, f32[56,640]{1,0:T(8,128)S(1)}, f32[240,256]{1,0:T(8,128)S(1)}) custom-call(f32[56,640]{1,0:T(8,128)S(1)} %get-tuple-element.102.i_ref, f32[56,640]{1,0:T(8,128)S(1)} %get-tuple-element.103.packed_ref, f32[240,256]{1,0:T(8,128)S(1)} %get-tuple-element.104.table_ref, s32[1,64]{1,0:T(1,128)S(1)} %get-tuple-element.74.cluster_ref, ...), custom_call_target="tpu_custom_call" | custom-call | flops 300000000 | bytes 1377280 | tf_op jit(solution)/shard_map/local1/pallas_call | solution.py:526
  23.7 0.0 collective-permute-done.4.r0
  23.7 0.0 collective-permute-done.5.r1
  23.7 0.0 collective-permute-done.6.r2
  23.7 0.9 %collective-permute-done.7.r3 = f32[48,128]{1,0:T(8,128)S(1)} collective-permute-done((f32[48,128]{1,0:T(8,128)S(1)}, f32[48,128]{1,0:T(8,128)S(1)}, u32[]{:S(2)}, u32[]{:S(2)}) %collective-permute-start.7) | collective-permute-done | bytes 24608 | tf_op jit(solution)/shard_map/ppermute | solution.py:41
  24.7 4.1 %tick2.1 = (f32[24,128]{1,0:T(8,128)S(1)}, f32[24,128]{1,0:T(8,128)S(1)}, f32[24,128]{1,0:T(8,128)S(1)}, f32[24,128]{1,0:T(8,128)S(1)}, f32[56,640]{1,0:T(8,128)...) custom-call(f32[48,128]{1,0:T(8,128)S(1)} %collective-permute-done.4.r0, f32[48,128]{1,0:T(8,128)S(1)} %collective-permute-done.5.r1, ...), custom_call_target="tpu_custom_call" | custom-call | flops 500000000 | bytes 1833472 | tf_op jit(solution)/shard_map/tick2/pallas_call | solution.py:526
  28.7 0.1 collective-permute-start.8
  28.8 1.8 %collective-permute-start.9 = (f32[24,128]{1,0:T(8,128)S(1)}, f32[24,128]{1,0:T(8,128)S(1)}, u32[]{:S(2)}, u32[]{:S(2)}) collective-permute-start(f32[24,128]{1,0:T(8,128)S(1)} %get-tuple-element.109), channel_id=1, source_target_pairs={{4,8},{8,4},{12,16},{16,12},{20,24},{24,20},{28,0},{0,28},{5,9},{9... | collective-permute-start | bytes 36872 | tf_op jit(solution)/shard_map/ppermute | solution.py:41
  30.6 1.6 %collective-permute-start.10 = (f32[24,128]{1,0:T(8,128)S(1)}, f32[24,128]{1,0:T(8,128)S(1)}, u32[]{:S(2)}, u32[]{:S(2)}) collective-permute-start(f32[24,128]{1,0:T(8,128)S(1)} %get-tuple-element.110), channel_id=1, source_target_pairs={{0,1},{1,0},{2,3},{3,2},{4,5},{5,4},{6,7},{7,6},{8,9},{9,8},{10,11... | collective-permute-start | bytes 36872 | tf_op jit(solution)/shard_map/ppermute | solution.py:41
  32.2 1.1 %collective-permute-start.11 = (f32[24,128]{1,0:T(8,128)S(1)}, f32[24,128]{1,0:T(8,128)S(1)}, u32[]{:S(2)}, u32[]{:S(2)}) collective-permute-start(f32[24,128]{1,0:T(8,128)S(1)} %get-tuple-element.111), channel_id=1, source_target_pairs={{1,2},{2,1},{3,0},{0,3},{5,6},{6,5},{7,4},{4,7},{9,10},{10,9},{11,... | collective-permute-start | bytes 36872 | tf_op jit(solution)/shard_map/ppermute | solution.py:41
  33.4 1.3 %local2.1 = (f32[56,640]{1,0:T(8,128)S(1)}, f32[56,640]{1,0:T(8,128)S(1)}, f32[240,256]{1,0:T(8,128)S(1)}) custom-call(f32[56,640]{1,0:T(8,128)S(1)} %get-tuple-element.112.i_ref, f32[56,640]{1,0:T(8,128)S(1)} %get-tuple-element.113.packed_ref, f32[240,256]{1,0:T(8,128)S(1)} %get-tuple-element.114.table_ref.rest_0_, ...), custom_call_target="tpu_custom_call" | custom-call | flops 300000000 | bytes 1377280 | tf_op jit(solution)/shard_map/local2/pallas_call | solution.py:526
  34.7 0.0 collective-permute-done.8.r0
  34.7 0.0 collective-permute-done.9.r1
  34.7 0.0 collective-permute-done.10.r2
  34.7 0.6 %collective-permute-done.11.r3 = f32[24,128]{1,0:T(8,128)S(1)} collective-permute-done((f32[24,128]{1,0:T(8,128)S(1)}, f32[24,128]{1,0:T(8,128)S(1)}, u32[]{:S(2)}, u32[]{:S(2)}) %collective-permute-start.11) | collective-permute-done | bytes 12320 | tf_op jit(solution)/shard_map/ppermute | solution.py:41
  35.4 4.1 %tick3.1 = (f32[96,128]{1,0:T(8,128)S(1)}, f32[96,128]{1,0:T(8,128)S(1)}, f32[96,128]{1,0:T(8,128)S(1)}, f32[96,128]{1,0:T(8,128)S(1)}, f32[56,640]{1,0:T(8,128)...) custom-call(f32[24,128]{1,0:T(8,128)S(1)} %collective-permute-done.8.r0, f32[24,128]{1,0:T(8,128)S(1)} %collective-permute-done.9.r1, ...), custom_call_target="tpu_custom_call" | custom-call | flops 500000000 | bytes 2275840 | tf_op jit(solution)/shard_map/tick3/pallas_call | solution.py:526
  39.5 0.1 collective-permute-start.12
  39.6 1.8 %collective-permute-start.13 = (f32[96,128]{1,0:T(8,128)S(1)}, f32[96,128]{1,0:T(8,128)S(1)}, u32[]{:S(2)}, u32[]{:S(2)}) collective-permute-start(f32[96,128]{1,0:T(8,128)S(1)} %get-tuple-element.120), channel_id=1, source_target_pairs={{4,8},{8,4},{12,16},{16,12},{20,24},{24,20},{28,0},{0,28},{5,9},{9... | collective-permute-start | bytes 147464 | tf_op jit(solution)/shard_map/ppermute | solution.py:41
  41.4 1.6 %collective-permute-start.14 = (f32[96,128]{1,0:T(8,128)S(1)}, f32[96,128]{1,0:T(8,128)S(1)}, u32[]{:S(2)}, u32[]{:S(2)}) collective-permute-start(f32[96,128]{1,0:T(8,128)S(1)} %get-tuple-element.121), channel_id=1, source_target_pairs={{0,1},{1,0},{2,3},{3,2},{4,5},{5,4},{6,7},{7,6},{8,9},{9,8},{10,11... | collective-permute-start | bytes 147464 | tf_op jit(solution)/shard_map/ppermute | solution.py:41
  42.9 1.1 %collective-permute-start.15 = (f32[96,128]{1,0:T(8,128)S(1)}, f32[96,128]{1,0:T(8,128)S(1)}, u32[]{:S(2)}, u32[]{:S(2)}) collective-permute-start(f32[96,128]{1,0:T(8,128)S(1)} %get-tuple-element.122), channel_id=1, source_target_pairs={{1,2},{2,1},{3,0},{0,3},{5,6},{6,5},{7,4},{4,7},{9,10},{10,9},{11,... | collective-permute-start | bytes 147464 | tf_op jit(solution)/shard_map/ppermute | solution.py:41
  44.0 1.3 %local3.1 = (f32[56,640]{1,0:T(8,128)S(1)}, f32[56,640]{1,0:T(8,128)}, f32[240,256]{1,0:T(8,128)S(1)}) custom-call(f32[56,640]{1,0:T(8,128)S(1)} %get-tuple-element.123.i_ref, f32[56,640]{1,0:T(8,128)S(1)} %get-tuple-element.124.packed_ref, f32[240,256]{1,0:T(8,128)S(1)} %get-tuple-element.125.table_ref, s32[1,64]{1,0:T(1,128)S(1)} %get-tuple-element.74.cluster_ref, ...), custom_call_target="tpu_custom_call" | custom-call | flops 300000000 | bytes 1377280 | tf_op jit(solution)/shard_map/local3/pallas_call | solution.py:526
  45.3 0.0 collective-permute-done.12.r0
  45.3 0.0 collective-permute-done.13.r1
  45.3 0.0 collective-permute-done.14.r2
  45.3 1.1 %collective-permute-done.15.r3 = f32[96,128]{1,0:T(8,128)S(1)} collective-permute-done((f32[96,128]{1,0:T(8,128)S(1)}, f32[96,128]{1,0:T(8,128)S(1)}, u32[]{:S(2)}, u32[]{:S(2)}) %collective-permute-start.15) | collective-permute-done | bytes 49184 | tf_op jit(solution)/shard_map/ppermute | solution.py:41
  46.4 1.9 %last.1 = f32[9,56,64]{2,1,0:T(8,128)} custom-call(f32[96,128]{1,0:T(8,128)S(1)} %collective-permute-done.12.r0, f32[96,128]{1,0:T(8,128)S(1)} %collective-permute-done.13.r1, f32[96,128]{1,0:T(8,128)S(1)} %collective-permute-done.14.r2, f32[96,128]{1,0:T(8,128)S(1)} %collective-permute-done.15.r3, f32[240,256]{1,0:T(8,128)S(1)} %get-tuple-element.127.near_ref, ...), custom_call_target="tpu_custom_call" | custom-call | flops 100000000 | bytes 1499136 | tf_op jit(solution)/shard_map/last/pallas_call | solution.py:526
Async XLA Ops:
  4.3 9.5 %collective-permute-start = (f32[24,128]{1,0:T(8,128)S(1)}, f32[24,128]{1,0:T(8,128)S(1)}, u32[]{:S(2)}, u32[]{:S(2)}) collective-permute-start(f32[24,128]{1,0:T(8,128)S(1)} %get-tuple-element.67), channel_id=1, source_target_pairs={{0,4},{4,0},{8,12},{12,8},{16,20},{20,16},{24,28},{28,24},{1,5},{5... | collective-permute-start | bytes 36872 | tf_op jit(solution)/shard_map/ppermute | solution.py:41
  6.4 7.4 %collective-permute-start.1 = (f32[24,128]{1,0:T(8,128)S(1)}, f32[24,128]{1,0:T(8,128)S(1)}, u32[]{:S(2)}, u32[]{:S(2)}) collective-permute-start(f32[24,128]{1,0:T(8,128)S(1)} %get-tuple-element.68), channel_id=1, source_target_pairs={{4,8},{8,4},{12,16},{16,12},{20,24},{24,20},{28,0},{0,28},{5,9},{9... | collective-permute-start | bytes 36872 | tf_op jit(solution)/shard_map/ppermute | solution.py:41
  9.7 4.1 %collective-permute-start.2 = (f32[24,128]{1,0:T(8,128)S(1)}, f32[24,128]{1,0:T(8,128)S(1)}, u32[]{:S(2)}, u32[]{:S(2)}) collective-permute-start(f32[24,128]{1,0:T(8,128)S(1)} %get-tuple-element.69), channel_id=1, source_target_pairs={{0,1},{1,0},{2,3},{3,2},{4,5},{5,4},{6,7},{7,6},{8,9},{9,8},{10,11... | collective-permute-start | bytes 36872 | tf_op jit(solution)/shard_map/ppermute | solution.py:41
  10.9 3.1 %collective-permute-start.3 = (f32[24,128]{1,0:T(8,128)S(1)}, f32[24,128]{1,0:T(8,128)S(1)}, u32[]{:S(2)}, u32[]{:S(2)}) collective-permute-start(f32[24,128]{1,0:T(8,128)S(1)} %get-tuple-element.70), channel_id=1, source_target_pairs={{1,2},{2,1},{3,0},{0,3},{5,6},{6,5},{7,4},{4,7},{9,10},{10,9},{11,... | collective-permute-start | bytes 36872 | tf_op jit(solution)/shard_map/ppermute | solution.py:41
  18.0 5.7 %collective-permute-start.4 = (f32[48,128]{1,0:T(8,128)S(1)}, f32[48,128]{1,0:T(8,128)S(1)}, u32[]{:S(2)}, u32[]{:S(2)}) collective-permute-start(f32[48,128]{1,0:T(8,128)S(1)} %get-tuple-element.98), channel_id=1, source_target_pairs={{0,4},{4,0},{8,12},{12,8},{16,20},{20,16},{24,28},{28,24},{1,5},{5... | collective-permute-start | bytes 73736 | tf_op jit(solution)/shard_map/ppermute | solution.py:41
  18.1 5.6 %collective-permute-start.5 = (f32[48,128]{1,0:T(8,128)S(1)}, f32[48,128]{1,0:T(8,128)S(1)}, u32[]{:S(2)}, u32[]{:S(2)}) collective-permute-start(f32[48,128]{1,0:T(8,128)S(1)} %get-tuple-element.99), channel_id=1, source_target_pairs={{4,8},{8,4},{12,16},{16,12},{20,24},{24,20},{28,0},{0,28},{5,9},{9... | collective-permute-start | bytes 73736 | tf_op jit(solution)/shard_map/ppermute | solution.py:41
  19.7 4.0 %collective-permute-start.6 = (f32[48,128]{1,0:T(8,128)S(1)}, f32[48,128]{1,0:T(8,128)S(1)}, u32[]{:S(2)}, u32[]{:S(2)}) collective-permute-start(f32[48,128]{1,0:T(8,128)S(1)} %get-tuple-element.100), channel_id=1, source_target_pairs={{0,1},{1,0},{2,3},{3,2},{4,5},{5,4},{6,7},{7,6},{8,9},{9,8},{10,11... | collective-permute-start | bytes 73736 | tf_op jit(solution)/shard_map/ppermute | solution.py:41
  21.4 3.3 %collective-permute-start.7 = (f32[48,128]{1,0:T(8,128)S(1)}, f32[48,128]{1,0:T(8,128)S(1)}, u32[]{:S(2)}, u32[]{:S(2)}) collective-permute-start(f32[48,128]{1,0:T(8,128)S(1)} %get-tuple-element.101), channel_id=1, source_target_pairs={{1,2},{2,1},{3,0},{0,3},{5,6},{6,5},{7,4},{4,7},{9,10},{10,9},{11,... | collective-permute-start | bytes 73736 | tf_op jit(solution)/shard_map/ppermute | solution.py:41
  28.7 6.0 %collective-permute-start.8 = (f32[24,128]{1,0:T(8,128)S(1)}, f32[24,128]{1,0:T(8,128)S(1)}, u32[]{:S(2)}, u32[]{:S(2)}) collective-permute-start(f32[24,128]{1,0:T(8,128)S(1)} %get-tuple-element.108), channel_id=1, source_target_pairs={{0,4},{4,0},{8,12},{12,8},{16,20},{20,16},{24,28},{28,24},{1,5},{5... | collective-permute-start | bytes 36872 | tf_op jit(solution)/shard_map/ppermute | solution.py:41
  28.8 5.9 %collective-permute-start.9 = (f32[24,128]{1,0:T(8,128)S(1)}, f32[24,128]{1,0:T(8,128)S(1)}, u32[]{:S(2)}, u32[]{:S(2)}) collective-permute-start(f32[24,128]{1,0:T(8,128)S(1)} %get-tuple-element.109), channel_id=1, source_target_pairs={{4,8},{8,4},{12,16},{16,12},{20,24},{24,20},{28,0},{0,28},{5,9},{9... | collective-permute-start | bytes 36872 | tf_op jit(solution)/shard_map/ppermute | solution.py:41
  30.6 4.1 %collective-permute-start.10 = (f32[24,128]{1,0:T(8,128)S(1)}, f32[24,128]{1,0:T(8,128)S(1)}, u32[]{:S(2)}, u32[]{:S(2)}) collective-permute-start(f32[24,128]{1,0:T(8,128)S(1)} %get-tuple-element.110), channel_id=1, source_target_pairs={{0,1},{1,0},{2,3},{3,2},{4,5},{5,4},{6,7},{7,6},{8,9},{9,8},{10,11... | collective-permute-start | bytes 36872 | tf_op jit(solution)/shard_map/ppermute | solution.py:41
  32.2 3.1 %collective-permute-start.11 = (f32[24,128]{1,0:T(8,128)S(1)}, f32[24,128]{1,0:T(8,128)S(1)}, u32[]{:S(2)}, u32[]{:S(2)}) collective-permute-start(f32[24,128]{1,0:T(8,128)S(1)} %get-tuple-element.111), channel_id=1, source_target_pairs={{1,2},{2,1},{3,0},{0,3},{5,6},{6,5},{7,4},{4,7},{9,10},{10,9},{11,... | collective-permute-start | bytes 36872 | tf_op jit(solution)/shard_map/ppermute | solution.py:41
  39.5 5.8 %collective-permute-start.12 = (f32[96,128]{1,0:T(8,128)S(1)}, f32[96,128]{1,0:T(8,128)S(1)}, u32[]{:S(2)}, u32[]{:S(2)}) collective-permute-start(f32[96,128]{1,0:T(8,128)S(1)} %get-tuple-element.119), channel_id=1, source_target_pairs={{0,4},{4,0},{8,12},{12,8},{16,20},{20,16},{24,28},{28,24},{1,5},{5... | collective-permute-start | bytes 147464 | tf_op jit(solution)/shard_map/ppermute | solution.py:41
  39.6 5.8 %collective-permute-start.13 = (f32[96,128]{1,0:T(8,128)S(1)}, f32[96,128]{1,0:T(8,128)S(1)}, u32[]{:S(2)}, u32[]{:S(2)}) collective-permute-start(f32[96,128]{1,0:T(8,128)S(1)} %get-tuple-element.120), channel_id=1, source_target_pairs={{4,8},{8,4},{12,16},{16,12},{20,24},{24,20},{28,0},{0,28},{5,9},{9... | collective-permute-start | bytes 147464 | tf_op jit(solution)/shard_map/ppermute | solution.py:41
  41.4 4.0 %collective-permute-start.14 = (f32[96,128]{1,0:T(8,128)S(1)}, f32[96,128]{1,0:T(8,128)S(1)}, u32[]{:S(2)}, u32[]{:S(2)}) collective-permute-start(f32[96,128]{1,0:T(8,128)S(1)} %get-tuple-element.121), channel_id=1, source_target_pairs={{0,1},{1,0},{2,3},{3,2},{4,5},{5,4},{6,7},{7,6},{8,9},{9,8},{10,11... | collective-permute-start | bytes 147464 | tf_op jit(solution)/shard_map/ppermute | solution.py:41
  42.9 3.5 %collective-permute-start.15 = (f32[96,128]{1,0:T(8,128)S(1)}, f32[96,128]{1,0:T(8,128)S(1)}, u32[]{:S(2)}, u32[]{:S(2)}) collective-permute-start(f32[96,128]{1,0:T(8,128)S(1)} %get-tuple-element.122), channel_id=1, source_target_pairs={{1,2},{2,1},{3,0},{0,3},{5,6},{6,5},{7,4},{4,7},{9,10},{10,9},{11,... | collective-permute-start | bytes 147464 | tf_op jit(solution)/shard_map/ppermute | solution.py:41

commit v2 on v1

--- a/solution.py
+++ b/solution.py
@@ -118,9 +118,9 @@
             one = out[i * MODES : (i + 1) * MODES]
             if i + 1 < dirs:
                 one = jnp.where(low, one, out[(i + 1) * MODES : (i + 2) * MODES])
-            m_ref[slot, (i // 2) * MODES : (i // 2 + 1) * MODES, group[0] * lanes : (group[0] + 1) * lanes] = one
+            m_ref[slot][-1][(i // 2) * MODES : (i // 2 + 1) * MODES, :] = one
     else:
-        m_ref[slot, 0 : dirs * MODES, group[0] * lanes : (group[-1] + 1) * lanes] = out
+        m_ref[slot][GROUPS.index(group)][...] = out
 
 
 def contract(m_ref, slot, coef_ref, dirs, group, lanes):
@@ -132,7 +132,8 @@
     for row, count in BLOCKS:
         sums = {}
         for d, q, block, line in terms:
-            values = m_ref[slot, d * MODES + row : d * MODES + row + count, q * lanes : (q + 1) * lanes]
+            at = (q % 2) * lanes
+            values = m_ref[slot][q // 2][d * MODES + row : d * MODES + row + count, at : at + lanes]
             for g in fields:
                 term = coef_ref[block * FIELDS + g, line : line + 1, :] * values
                 sums[g] = sums[g] + term if g in sums else term
@@ -351,14 +352,14 @@
 def first_kernel(
     state_hbm, star_hbm, ck_hbm, project_hbm, cluster_hbm, elem_hbm, face_hbm,
     aminus_hbm, aplus_hbm, vol_hbm, flux_hbm, lift_hbm, rotate_hbm, neighbour_hbm, orient_hbm,
-    m0, m1, m2, m3, packed_ref, star_out, ck_out, proj_out, i_ref, table_ref, send_out, star_ref, cluster_ref,
+    packed_ref, star_out, ck_out, proj_out, send_out, star_ref, cluster_ref,
     aminus_out, aplus_out, vol_out, flux_out, lift_out, rotate_out, neighbour_out, orient_out,
-    state_ref, ck_ref, project_ref, elem_ref, face_ref, weight_ref, faces_ref, m_ref, early, late, *, lanes,
+    state_ref, ck_ref, project_ref, elem_ref, face_ref, early, late, *, lanes,
 ):
     soon = [
         pltpu.make_async_copy(source, target, early.at[i])
         for i, (source, target) in enumerate((
-            (cluster_hbm, cluster_ref), (ck_hbm, ck_ref), (state_hbm, state_ref), (star_hbm, star_ref),
+            (state_hbm, state_ref), (star_hbm, star_ref), (ck_hbm, ck_ref), (cluster_hbm, cluster_ref),
             (project_hbm, project_ref), (elem_hbm, elem_ref), (face_hbm, face_ref),
         ))
     ]
@@ -382,19 +383,44 @@
     ck_out[...] = left_parts(-ck_ref[...].reshape(3 * MODES, MODES), MODES_UP).astype(BF16)
     proj_rows = [pad_rows(project_ref[:, j, :], FACE_UP) for j in range(4)]
     proj_out[...] = left_parts(jnp.concatenate(proj_rows, axis=0), MODES_UP).astype(BF16)
-    rows = send_rows(face_ref, elem_ref, lanes)
-    for i, row in enumerate(rows):
+    for i, row in enumerate(send_rows(face_ref, elem_ref, lanes)):
         send_out[i : i + 1, :] = row
-    store_weights(weight_ref, pair(cluster_ref[...], cluster_ref[...]), 0)
+    for copy in then:
+        copy.wait()
+
+
+def predict_kernel(
+    packed_ref, cluster_ref, ck_ref, star_ref, proj_ref, i_ref, faces_ref, weight_ref, m_ref, *, lanes, tick
+):
+    store_weights(weight_ref, pair(cluster_ref[...], cluster_ref[...]), tick)
 
     def state_of(group):
         return packed_ref[:, span(group, lanes)]
 
-    predict(state_of, ck_out, star_out, weight_ref, proj_out, faces_ref, m_ref, i_ref, lanes)
+    predict(state_of, ck_ref, star_ref, weight_ref, proj_ref, faces_ref, m_ref, i_ref, lanes)
+
+
+def send_kernel(faces_ref, send_ref, *rest, lanes, tick, olds):
+    old_refs = rest[:olds]
+    m0, m1, m2, m3, table_ref = rest[olds : olds + 5]
     fill_table(faces_ref, table_ref, lanes)
-    fill_messages([table_ref[...]], lambda group: one_hot(rows[0], 2 * lanes), (m0, m1, m2, m3), lanes)
-    for copy in then:
-        copy.wait()
+    table = table_ref[...]
+    tables = [table]
+    if tick == 1:
+        two = old_refs[0][...] + table
+        rest[olds + 5][...] = two
+        tables.append(two)
+    if tick == 3:
+        two = old_refs[0][...] + table
+        four = old_refs[1][...] + two
+        tables += [two, four, four]
+
+    def chosen(group):
+        if tick:
+            return send_ref[:, group * lanes : (group + 1) * lanes]
+        return one_hot(send_ref[group : group + 1, :], 2 * lanes)
+
+    fill_messages(tables, chosen, (m0, m1, m2, m3), lanes)
 
 
 def prepare_kernel(
@@ -468,40 +494,14 @@
         base_out[:, cols] = jnp.where(done, before + change, before)
 
 
-def tick_kernel(
-    r0, r1, r2, r3, near_ref, far_ref, turn_ref, aplus_ref, lift_ref, base_ref, cluster_ref,
-    ck_ref, proj_ref, star_ref, send_ref, *rest, lanes, tick, olds, groups,
+def update_kernel(
+    r0, r1, r2, r3, near_ref, far_ref, turn_ref, aplus_ref, lift_ref, base_ref, cluster_ref, packed_ref, c_ref,
+    *, lanes, tick, groups,
 ):
-    old_refs = rest[:olds]
-    m0, m1, m2, m3, packed_ref, i_ref, table_ref = rest[olds : olds + 7]
-    rest = rest[olds + 7 :]
-    sum_ref = None
-    if tick == 1:
-        sum_ref, rest = rest[0], rest[1:]
-    weight_ref, faces_ref, m_ref, c_ref = rest
-    cluster = pair(cluster_ref[...], cluster_ref[...])
-    _, finished = timing(cluster, tick - 1)
-    store_weights(weight_ref, cluster, tick)
+    _, finished = timing(pair(cluster_ref[...], cluster_ref[...]), tick)
     gather_faces((r0, r1, r2, r3), groups, near_ref, far_ref, turn_ref, aplus_ref, c_ref, lanes)
-
-    def state_of(group):
-        values = updated(c_ref, lift_ref, base_ref, finished, group, lanes)
-        packed_ref[:, span(group, lanes)] = values
-        return values
-
-    predict(state_of, ck_ref, star_ref, weight_ref, proj_ref, faces_ref, m_ref, i_ref, lanes)
-    fill_table(faces_ref, table_ref, lanes)
-    table = table_ref[...]
-    tables = [table]
-    if tick == 1:
-        two = old_refs[0][...] + table
-        sum_ref[...] = two
-        tables.append(two)
-    if tick == 3:
-        two = old_refs[0][...] + table
-        four = old_refs[1][...] + two
-        tables += [two, four, four]
-    fill_messages(tables, lambda group: send_ref[:, group * lanes : (group + 1) * lanes], (m0, m1, m2, m3), lanes)
+    for group in GROUPS:
+        packed_ref[:, span(group, lanes)] = updated(c_ref, lift_ref, base_ref, finished, group, lanes)
 
 
 def last_kernel(
@@ -516,6 +516,12 @@
             for side in range(2):
                 if 2 * q + side < FIELDS:
                     out_ref[2 * q + side] = values[:, i * lanes + side * half : i * lanes + (side + 1) * half]
+
+
+def stages(slots, dirs, lanes):
+    wide = pltpu.VMEM((dirs * MODES, 2 * lanes), F32)
+    last = pltpu.VMEM(((dirs + 1) // 2 * MODES, lanes), F32)
+    return [[wide, wide, last] for _ in range(slots)]
 
 
 def call(body, outs, scratch, name, flops, arrays, far=False):
@@ -552,8 +558,8 @@
     modal = shape((MODES, wide), F32)
     table = shape((ROWS, 4 * elems), F32)
     weights = pltpu.VMEM((SLOT, lanes), F32)
-    faces = pltpu.VMEM((4 * FACE_UP, wide), F32)
-    staged = pltpu.VMEM((2, 3 * MODES, wide), F32)
+    faces = shape((4 * FACE_UP, wide), F32)
+    staged = stages(2, 3, lanes)
     sides = pltpu.VMEM((12 * FACE_UP, wide), BF16)
 
     def like(x):
@@ -566,30 +572,43 @@
         return [shape((count * FACE_UP, lanes), F32)] * 4
 
     late = (aminus, aplus, vol_stiff, flux_local, lift, rotate, neighbour, orient)
-    out = call(
+    packed, star_pairs, ck_left, proj_left, send, star, cluster_row, *late = call(
         functools.partial(first_kernel, lanes=lanes),
-        message(1)
-        + [
+        [
             modal,
             shape((PAIRS * FIELDS, 3, lanes), F32),
             shape((3 * MODES, 3 * MODES_UP), BF16),
             shape((4 * FACE_UP, 3 * MODES_UP), BF16),
-            modal,
-            table,
             shape((groups, lanes), jnp.int32),
             like(star),
             like(cluster_row),
         ]
         + [like(x) for x in late],
-        [room(state), room(ck_stiff), room(project), room(send_elem), room(send_face), weights, faces, staged]
+        [room(state), room(ck_stiff), room(project), room(send_elem), room(send_face)]
         + [pltpu.SemaphoreType.DMA((7,)), pltpu.SemaphoreType.DMA((len(late),))],
-        "first", 400_000_000,
+        "first", 10_000_000,
         (state, star, ck_stiff, project, cluster_row, send_elem, send_face, *late), far=True,
     )
-    messages, out = out[:4], out[4:]
-    packed, star_pairs, ck_left, proj_left, integral, table_now, send, star, cluster_row = out[:9]
-    late = out[9:]
     orient = late[-1]
+
+    def predicted(tick, packed, chosen, olds):
+        integral, face_values = call(
+            functools.partial(predict_kernel, lanes=lanes, tick=tick),
+            [modal, faces],
+            [weights, staged],
+            f"predict{tick}", 400_000_000,
+            (packed, cluster_row, ck_left, star_pairs, proj_left),
+        )
+        out = call(
+            functools.partial(send_kernel, lanes=lanes, tick=tick, olds=len(olds)),
+            message((1, 2, 1, 4)[tick]) + [table] + ([table] if tick == 1 else []),
+            [],
+            f"send{tick}", 50_000_000,
+            (face_values, chosen, *olds),
+        )
+        return integral, out[:4], out[4:]
+
+    integral, messages, (table_now,) = predicted(0, packed, send, ())
     coef, aplus_pairs, left, lift_left, turn, near_hot, far_hot, send_hot = call(
         functools.partial(prepare_kernel, lanes=lanes),
         [
@@ -616,7 +635,7 @@
         base, own, seen = call(
             functools.partial(local_kernel, lanes=lanes, tick=tick),
             [modal, modal, table],
-            [pltpu.VMEM((1, 7 * MODES, wide), F32)],
+            [stages(1, 7, lanes)],
             f"local{tick}", 300_000_000,
             (integral, packed, table_now, cluster_row, coef, left, near_hot, turn, orient, own, seen),
         )
@@ -629,18 +648,17 @@
                 [sides],
                 "last", 100_000_000, common,
             )[0]
+        packed = call(
+            functools.partial(update_kernel, lanes=lanes, tick=tick, groups=count),
+            [modal],
+            [sides],
+            f"update{tick}", 100_000_000, common,
+        )[0]
         olds = {0: (table_now,), 1: (), 2: (table_now, two)}[tick]
-        sends = (1, 2, 1, 4)[tick + 1]
-        out = call(
-            functools.partial(tick_kernel, lanes=lanes, tick=tick + 1, olds=len(olds), groups=count),
-            message(sends) + [modal, modal, table] + ([table] if tick == 0 else []),
-            [weights, faces, staged, sides],
-            f"tick{tick + 1}", 500_000_000,
-            (*common, ck_left, proj_left, star_pairs, send_hot, *olds),
-        )
-        messages, (packed, integral, table_now) = out[:4], out[4:7]
+        integral, messages, tables = predicted(tick + 1, packed, send_hot, olds)
+        table_now = tables[0]
         if tick == 0:
-            two = out[7]
+            two = tables[1]
 
 
 def solution(mesh):

time: 48.8 us -> 48.1 us (0.986)
  Pallas kernels: 23.8 us -> 23.2 us
    pallas_call x10 -> x18, Pallas kernels: 23.8 us -> 23.2 us  [call(): pl.pallas_call(body, out_shape=outs, in_specs=[pl.BlockSpec(memory_space=...]
  transfers between devices with their start and end apart: 16 -> 16, of which waited for: 4 -> 4; matrix products, arithmetic and copies ran while one was open for 0% -> 0% of each run, Pallas kernels for 11% -> 12%
where the time goes in v2:
time: 48.1 us; the launch traced here: 47.7 us
  Pallas kernels  23.2 us (48%)
  starting transfers between devices  21.5 us (45%)
  waiting for transfers between devices  2.75 us (6%)
    pallas_call x18, Pallas kernels, call(): pl.pallas_call(body, out_shape=outs, in_specs=[pl.BlockSpec(memory_space=...  23.2 us
    ppermute x16, starting transfers between devices, exchange(): return lax.ppermute(x, axis, pairs)  21.5 us
    ppermute x16, waiting for transfers between devices, exchange(): return lax.ppermute(x, axis, pairs)  2.75 us
  transfers between devices with their start and end apart: 16, of which 4 were waited for; matrix products, arithmetic and copies ran while one was open for 0% of the time, Pallas kernels for 12%

profile of v2, /device:TPU:1, one launch (start us, length us, event | category | flops | bytes accessed | tf_op | source)
XLA Modules:
  0.0 47.7 jit_solution(11244954114259205998)
XLA Ops:
  0.0 1.6 %first.1 = (f32[56,640]{1,0:T(8,128)S(1)}, f32[45,3,128]{2,1,0:T(4,128)S(1)}, bf16[168,192]{1,0:T(8,128)(2,1)S(1)}, bf16[96,192]{1,0:T(8,128)(2,1)S(1)}, s32[4,1...) custom-call(f32[9,56,64]{2,1,0:T(8,128)} %state_hbm.1, ...), custom_call_target="tpu_custom_call" | custom-call | flops 10000000 | bytes 528812 | tf_op jit(solution)/shard_map/first/pallas_call | solution.py:532
  1.6 2.4 %predict0.1 = (f32[56,640]{1,0:T(8,128)S(1)}, f32[96,640]{1,0:T(8,128)S(1)}) custom-call(f32[56,640]{1,0:T(8,128)S(1)} %get-tuple-element.68.packed_ref, s32[1,64]{1,0:T(1,128)S(1)} %get-tuple-element.69.cluster_ref, bf16[168,192]{1,0:T(8,128)(2,1)S(1)} %get-tuple-element.70.ck_ref, f32[45,3,128]{2,1,0:T(4,128)S(1)} %get-tuple-element.71.star_ref, ...), custom_call_target="tpu_custom_call" | custom-call | flops 400000000 | bytes 314112 | tf_op jit(solution)/shard_map/predict0/pallas_call | solution.py:532
  4.0 0.3 send0.1
  4.4 2.1 %collective-permute-start = (f32[24,128]{1,0:T(8,128)S(1)}, f32[24,128]{1,0:T(8,128)S(1)}, u32[]{:S(2)}, u32[]{:S(2)}) collective-permute-start(f32[24,128]{1,0:T(8,128)S(1)} %get-tuple-element.75), channel_id=1, source_target_pairs={{0,4},{4,0},{8,12},{12,8},{16,20},{20,16},{24,28},{28,24},{1,5},{5... | collective-permute-start | bytes 36872 | tf_op jit(solution)/shard_map/ppermute | solution.py:41
  6.5 3.3 %collective-permute-start.1 = (f32[24,128]{1,0:T(8,128)S(1)}, f32[24,128]{1,0:T(8,128)S(1)}, u32[]{:S(2)}, u32[]{:S(2)}) collective-permute-start(f32[24,128]{1,0:T(8,128)S(1)} %get-tuple-element.76), channel_id=1, source_target_pairs={{4,8},{8,4},{12,16},{16,12},{20,24},{24,20},{28,0},{0,28},{5,9},{9... | collective-permute-start | bytes 36872 | tf_op jit(solution)/shard_map/ppermute | solution.py:41
  9.7 1.2 %collective-permute-start.2 = (f32[24,128]{1,0:T(8,128)S(1)}, f32[24,128]{1,0:T(8,128)S(1)}, u32[]{:S(2)}, u32[]{:S(2)}) collective-permute-start(f32[24,128]{1,0:T(8,128)S(1)} %get-tuple-element.77), channel_id=1, source_target_pairs={{0,1},{1,0},{2,3},{3,2},{4,5},{5,4},{6,7},{7,6},{8,9},{9,8},{10,11... | collective-permute-start | bytes 36872 | tf_op jit(solution)/shard_map/ppermute | solution.py:41
  11.0 1.1 %collective-permute-start.3 = (f32[24,128]{1,0:T(8,128)S(1)}, f32[24,128]{1,0:T(8,128)S(1)}, u32[]{:S(2)}, u32[]{:S(2)}) collective-permute-start(f32[24,128]{1,0:T(8,128)S(1)} %get-tuple-element.78), channel_id=1, source_target_pairs={{1,2},{2,1},{3,0},{0,3},{5,6},{6,5},{7,4},{4,7},{9,10},{10,9},{11,... | collective-permute-start | bytes 36872 | tf_op jit(solution)/shard_map/ppermute | solution.py:41
  12.1 0.6 %prepare.1 = (f32[45,7,128]{2,1,0:T(8,128)S(1)}, f32[81,2,128]{2,1,0:T(2,128)S(1)}, bf16[392,192]{1,0:T(8,128)(2,1)S(1)}, bf16[56,288]{1,0:T(8,128)(2,1)S(1)}, b...) custom-call(f32[9,9,3,64]{3,2,1,0:T(4,128)S(1)} %get-tuple-element.8, ...), custom_call_target="tpu_custom_call" | custom-call | flops 100000000 | bytes 344108 | tf_op jit(solution)/shard_map/prepare/pallas_call | solution.py:532
  12.7 1.1 %local0.1 = (f32[56,640]{1,0:T(8,128)S(1)}, f32[56,640]{1,0:T(8,128)S(1)}, f32[240,256]{1,0:T(8,128)S(1)}) custom-call(f32[56,640]{1,0:T(8,128)S(1)} %get-tuple-element.79.i_ref.own_ref, f32[56,640]{1,0:T(8,128)S(1)} %get-tuple-element.68.packed_ref, f32[240,256]{1,0:T(8,128)S(1)} %get-tuple-element.80.table_ref.seen_ref.rest_0_, ...), custom_call_target="tpu_custom_call" | custom-call | flops 300000000 | bytes 1377280 | tf_op jit(solution)/shard_map/local0/pallas_call | solution.py:532
  13.9 0.0 collective-permute-done.r0
  13.9 0.0 collective-permute-done.1.r1
  13.9 0.0 collective-permute-done.2.r2
  13.9 0.2 collective-permute-done.3.r3
  14.1 0.9 %update0.1.packed_ref = f32[56,640]{1,0:T(8,128)S(1)} custom-call(f32[24,128]{1,0:T(8,128)S(1)} %collective-permute-done.r0, f32[24,128]{1,0:T(8,128)S(1)} %collective-permute-done.1.r1, f32[24,128]{1,0:T(8,128)S(1)} %collective-permute-done.2.r2, f32[24,128]{1,0:T(8,128)S(1)} %collective-permute-done.3.r3, ...), custom_call_target="tpu_custom_call" | custom-call | flops 100000000 | bytes 1351680 | tf_op jit(solution)/shard_map/update0/pallas_call | solution.py:532
  15.0 2.3 %predict1.1 = (f32[56,640]{1,0:T(8,128)S(1)}, f32[96,640]{1,0:T(8,128)S(1)}) custom-call(f32[56,640]{1,0:T(8,128)S(1)} %update0.1.packed_ref, s32[1,64]{1,0:T(1,128)S(1)} %get-tuple-element.69.cluster_ref, bf16[168,192]{1,0:T(8,128)(2,1)S(1)} %get-tuple-element.70.ck_ref, f32[45,3,128]{2,1,0:T(4,128)S(1)} %get-tuple-element.71.star_ref, ...), custom_call_target="tpu_custom_call" | custom-call | flops 400000000 | bytes 314112 | tf_op jit(solution)/shard_map/predict1/pallas_call | solution.py:532
  17.4 0.5 %send1.1 = (f32[48,128]{1,0:T(8,128)S(1)}, f32[48,128]{1,0:T(8,128)S(1)}, f32[48,128]{1,0:T(8,128)S(1)}, f32[48,128]{1,0:T(8,128)S(1)}, f32[240,256]{1,0:T(8,128)S(1)}, /*index=5*/f32[240,256]{1,0:T(8,128)S(1)}) custom-call(f32[96,640]{1,0:T(8,128)S(1)} %get-tuple-element.99.faces_ref, bf16[256,512]{1,0:T(8,128)(2,1)S(1)} %get-tuple-element.100.send_ref, ...), custom_call_target="tpu_custom_call" | custom-call | flops 50000000 | bytes 753664 | tf_op jit(solution)/shard_map/send1/pallas_call | solution.py:532
  17.9 0.1 collective-permute-start.4
  18.0 1.6 %collective-permute-start.5 = (f32[48,128]{1,0:T(8,128)S(1)}, f32[48,128]{1,0:T(8,128)S(1)}, u32[]{:S(2)}, u32[]{:S(2)}) collective-permute-start(f32[48,128]{1,0:T(8,128)S(1)} %get-tuple-element.102), channel_id=1, source_target_pairs={{4,8},{8,4},{12,16},{16,12},{20,24},{24,20},{28,0},{0,28},{5,9},{9... | collective-permute-start | bytes 73736 | tf_op jit(solution)/shard_map/ppermute | solution.py:41
  19.6 1.7 %collective-permute-start.6 = (f32[48,128]{1,0:T(8,128)S(1)}, f32[48,128]{1,0:T(8,128)S(1)}, u32[]{:S(2)}, u32[]{:S(2)}) collective-permute-start(f32[48,128]{1,0:T(8,128)S(1)} %get-tuple-element.103), channel_id=1, source_target_pairs={{0,1},{1,0},{2,3},{3,2},{4,5},{5,4},{6,7},{7,6},{8,9},{9,8},{10,11... | collective-permute-start | bytes 73736 | tf_op jit(solution)/shard_map/ppermute | solution.py:41
  21.3 1.1 %collective-permute-start.7 = (f32[48,128]{1,0:T(8,128)S(1)}, f32[48,128]{1,0:T(8,128)S(1)}, u32[]{:S(2)}, u32[]{:S(2)}) collective-permute-start(f32[48,128]{1,0:T(8,128)S(1)} %get-tuple-element.104), channel_id=1, source_target_pairs={{1,2},{2,1},{3,0},{0,3},{5,6},{6,5},{7,4},{4,7},{9,10},{10,9},{11,... | collective-permute-start | bytes 73736 | tf_op jit(solution)/shard_map/ppermute | solution.py:41
  22.4 1.2 %local1.1 = (f32[56,640]{1,0:T(8,128)S(1)}, f32[56,640]{1,0:T(8,128)S(1)}, f32[240,256]{1,0:T(8,128)S(1)}) custom-call(f32[56,640]{1,0:T(8,128)S(1)} %get-tuple-element.105.i_ref, f32[56,640]{1,0:T(8,128)S(1)} %update0.1.packed_ref, f32[240,256]{1,0:T(8,128)S(1)} %get-tuple-element.106.table_ref, s32[1,64]{1,0:T(1,128)S(1)} %get-tuple-element.69.cluster_ref, ...), custom_call_target="tpu_custom_call" | custom-call | flops 300000000 | bytes 1377280 | tf_op jit(solution)/shard_map/local1/pallas_call | solution.py:532
  23.7 0.0 collective-permute-done.4.r0
  23.7 0.0 collective-permute-done.5.r1
  23.7 0.0 collective-permute-done.6.r2
  23.7 0.9 %collective-permute-done.7.r3 = f32[48,128]{1,0:T(8,128)S(1)} collective-permute-done((f32[48,128]{1,0:T(8,128)S(1)}, f32[48,128]{1,0:T(8,128)S(1)}, u32[]{:S(2)}, u32[]{:S(2)}) %collective-permute-start.7) | collective-permute-done | bytes 24608 | tf_op jit(solution)/shard_map/ppermute | solution.py:41
  24.6 1.0 %update1.1.packed_ref = f32[56,640]{1,0:T(8,128)S(1)} custom-call(f32[48,128]{1,0:T(8,128)S(1)} %collective-permute-done.4.r0, f32[48,128]{1,0:T(8,128)S(1)} %collective-permute-done.5.r1, f32[48,128]{1,0:T(8,128)S(1)} %collective-permute-done.6.r2, f32[48,128]{1,0:T(8,128)S(1)} %collective-permute-done.7.r3, ...), custom_call_target="tpu_custom_call" | custom-call | flops 100000000 | bytes 1400832 | tf_op jit(solution)/shard_map/update1/pallas_call | solution.py:532
  25.6 2.4 %predict2.1 = (f32[56,640]{1,0:T(8,128)S(1)}, f32[96,640]{1,0:T(8,128)S(1)}) custom-call(f32[56,640]{1,0:T(8,128)S(1)} %update1.1.packed_ref, s32[1,64]{1,0:T(1,128)S(1)} %get-tuple-element.69.cluster_ref, bf16[168,192]{1,0:T(8,128)(2,1)S(1)} %get-tuple-element.70.ck_ref, f32[45,3,128]{2,1,0:T(4,128)S(1)} %get-tuple-element.71.star_ref, ...), custom_call_target="tpu_custom_call" | custom-call | flops 400000000 | bytes 314112 | tf_op jit(solution)/shard_map/predict2/pallas_call | solution.py:532
  27.9 0.3 send2.1
  28.3 0.1 collective-permute-start.8
  28.4 1.8 %collective-permute-start.9 = (f32[24,128]{1,0:T(8,128)S(1)}, f32[24,128]{1,0:T(8,128)S(1)}, u32[]{:S(2)}, u32[]{:S(2)}) collective-permute-start(f32[24,128]{1,0:T(8,128)S(1)} %get-tuple-element.112), channel_id=1, source_target_pairs={{4,8},{8,4},{12,16},{16,12},{20,24},{24,20},{28,0},{0,28},{5,9},{9... | collective-permute-start | bytes 36872 | tf_op jit(solution)/shard_map/ppermute | solution.py:41
  30.2 1.6 %collective-permute-start.10 = (f32[24,128]{1,0:T(8,128)S(1)}, f32[24,128]{1,0:T(8,128)S(1)}, u32[]{:S(2)}, u32[]{:S(2)}) collective-permute-start(f32[24,128]{1,0:T(8,128)S(1)} %get-tuple-element.113), channel_id=1, source_target_pairs={{0,1},{1,0},{2,3},{3,2},{4,5},{5,4},{6,7},{7,6},{8,9},{9,8},{10,11... | collective-permute-start | bytes 36872 | tf_op jit(solution)/shard_map/ppermute | solution.py:41
  31.8 1.1 %collective-permute-start.11 = (f32[24,128]{1,0:T(8,128)S(1)}, f32[24,128]{1,0:T(8,128)S(1)}, u32[]{:S(2)}, u32[]{:S(2)}) collective-permute-start(f32[24,128]{1,0:T(8,128)S(1)} %get-tuple-element.114), channel_id=1, source_target_pairs={{1,2},{2,1},{3,0},{0,3},{5,6},{6,5},{7,4},{4,7},{9,10},{10,9},{11,... | collective-permute-start | bytes 36872 | tf_op jit(solution)/shard_map/ppermute | solution.py:41
  32.9 1.4 %local2.1 = (f32[56,640]{1,0:T(8,128)S(1)}, f32[56,640]{1,0:T(8,128)S(1)}, f32[240,256]{1,0:T(8,128)S(1)}) custom-call(f32[56,640]{1,0:T(8,128)S(1)} %get-tuple-element.115.i_ref, f32[56,640]{1,0:T(8,128)S(1)} %update1.1.packed_ref, f32[240,256]{1,0:T(8,128)S(1)} %get-tuple-element.116.table_ref.rest_0_, s32[1,64]{1,0:T(1,128)S(1)} %get-tuple-element.69.cluster_ref, ...), custom_call_target="tpu_custom_call" | custom-call | flops 300000000 | bytes 1377280 | tf_op jit(solution)/shard_map/local2/pallas_call | solution.py:532
  34.3 0.0 collective-permute-done.9.r1
  34.3 0.0 collective-permute-done.10.r2
  34.3 0.6 %collective-permute-done.11.r3 = f32[24,128]{1,0:T(8,128)S(1)} collective-permute-done((f32[24,128]{1,0:T(8,128)S(1)}, f32[24,128]{1,0:T(8,128)S(1)}, u32[]{:S(2)}, u32[]{:S(2)}) %collective-permute-start.11) | collective-permute-done | bytes 12320 | tf_op jit(solution)/shard_map/ppermute | solution.py:41
  34.9 0.9 %update2.1.packed_ref = f32[56,640]{1,0:T(8,128)S(1)} custom-call(f32[24,128]{1,0:T(8,128)S(1)} %collective-permute-done.8.r0, f32[24,128]{1,0:T(8,128)S(1)} %collective-permute-done.9.r1, f32[24,128]{1,0:T(8,128)S(1)} %collective-permute-done.10.r2, f32[24,128]{1,0:T(8,128)S(1)} %collective-permute-done.11.r3, ...), custom_call_target="tpu_custom_call" | custom-call | flops 100000000 | bytes 1351680 | tf_op jit(solution)/shard_map/update2/pallas_call | solution.py:532
  35.8 2.3 %predict3.1 = (f32[56,640]{1,0:T(8,128)S(1)}, f32[96,640]{1,0:T(8,128)S(1)}) custom-call(f32[56,640]{1,0:T(8,128)S(1)} %update2.1.packed_ref, s32[1,64]{1,0:T(1,128)S(1)} %get-tuple-element.69.cluster_ref, bf16[168,192]{1,0:T(8,128)(2,1)S(1)} %get-tuple-element.70.ck_ref, f32[45,3,128]{2,1,0:T(4,128)S(1)} %get-tuple-element.71.star_ref, ...), custom_call_target="tpu_custom_call" | custom-call | flops 400000000 | bytes 314112 | tf_op jit(solution)/shard_map/predict3/pallas_call | solution.py:532
  38.2 0.6 %send3.1 = (f32[96,128]{1,0:T(8,128)S(1)}, f32[96,128]{1,0:T(8,128)S(1)}, f32[96,128]{1,0:T(8,128)S(1)}, f32[96,128]{1,0:T(8,128)S(1)}, f32[240,256]{1,0:T(8,128)S(1)}) custom-call(f32[96,640]{1,0:T(8,128)S(1)} %get-tuple-element.120.faces_ref, bf16[256,512]{1,0:T(8,128)(2,1)S(1)} %get-tuple-element.100.send_ref, ...), custom_call_target="tpu_custom_call" | custom-call | flops 50000000 | bytes 999424 | tf_op jit(solution)/shard_map/send3/pallas_call | solution.py:532
  38.8 0.1 collective-permute-start.12
  38.8 1.8 %collective-permute-start.13 = (f32[96,128]{1,0:T(8,128)S(1)}, f32[96,128]{1,0:T(8,128)S(1)}, u32[]{:S(2)}, u32[]{:S(2)}) collective-permute-start(f32[96,128]{1,0:T(8,128)S(1)} %get-tuple-element.123), channel_id=1, source_target_pairs={{4,8},{8,4},{12,16},{16,12},{20,24},{24,20},{28,0},{0,28},{5,9},{9... | collective-permute-start | bytes 147464 | tf_op jit(solution)/shard_map/ppermute | solution.py:41
  40.7 1.5 %collective-permute-start.14 = (f32[96,128]{1,0:T(8,128)S(1)}, f32[96,128]{1,0:T(8,128)S(1)}, u32[]{:S(2)}, u32[]{:S(2)}) collective-permute-start(f32[96,128]{1,0:T(8,128)S(1)} %get-tuple-element.124), channel_id=1, source_target_pairs={{0,1},{1,0},{2,3},{3,2},{4,5},{5,4},{6,7},{7,6},{8,9},{9,8},{10,11... | collective-permute-start | bytes 147464 | tf_op jit(solution)/shard_map/ppermute | solution.py:41
  42.2 1.1 %collective-permute-start.15 = (f32[96,128]{1,0:T(8,128)S(1)}, f32[96,128]{1,0:T(8,128)S(1)}, u32[]{:S(2)}, u32[]{:S(2)}) collective-permute-start(f32[96,128]{1,0:T(8,128)S(1)} %get-tuple-element.125), channel_id=1, source_target_pairs={{1,2},{2,1},{3,0},{0,3},{5,6},{6,5},{7,4},{4,7},{9,10},{10,9},{11,... | collective-permute-start | bytes 147464 | tf_op jit(solution)/shard_map/ppermute | solution.py:41
  43.3 1.3 %local3.1 = (f32[56,640]{1,0:T(8,128)S(1)}, f32[56,640]{1,0:T(8,128)}, f32[240,256]{1,0:T(8,128)S(1)}) custom-call(f32[56,640]{1,0:T(8,128)S(1)} %get-tuple-element.126.i_ref, f32[56,640]{1,0:T(8,128)S(1)} %update2.1.packed_ref, f32[240,256]{1,0:T(8,128)S(1)} %get-tuple-element.127.table_ref, s32[1,64]{1,0:T(1,128)S(1)} %get-tuple-element.69.cluster_ref, ...), custom_call_target="tpu_custom_call" | custom-call | flops 300000000 | bytes 1377280 | tf_op jit(solution)/shard_map/local3/pallas_call | solution.py:532
  44.6 0.0 collective-permute-done.12.r0
  44.6 0.0 collective-permute-done.13.r1
  44.6 1.1 %collective-permute-done.15.r3 = f32[96,128]{1,0:T(8,128)S(1)} collective-permute-done((f32[96,128]{1,0:T(8,128)S(1)}, f32[96,128]{1,0:T(8,128)S(1)}, u32[]{:S(2)}, u32[]{:S(2)}) %collective-permute-start.15) | collective-permute-done | bytes 49184 | tf_op jit(solution)/shard_map/ppermute | solution.py:41
  45.7 1.9 %last.1 = f32[9,56,64]{2,1,0:T(8,128)} custom-call(f32[96,128]{1,0:T(8,128)S(1)} %collective-permute-done.12.r0, f32[96,128]{1,0:T(8,128)S(1)} %collective-permute-done.13.r1, f32[96,128]{1,0:T(8,128)S(1)} %collective-permute-done.14.r2, f32[96,128]{1,0:T(8,128)S(1)} %collective-permute-done.15.r3, f32[240,256]{1,0:T(8,128)S(1)} %get-tuple-element.129.near_ref, ...), custom_call_target="tpu_custom_call" | custom-call | flops 100000000 | bytes 1499136 | tf_op jit(solution)/shard_map/last/pallas_call | solution.py:532
  (2 shorter events, 0.0 us)
Async XLA Ops:
  4.4 9.5 %collective-permute-start = (f32[24,128]{1,0:T(8,128)S(1)}, f32[24,128]{1,0:T(8,128)S(1)}, u32[]{:S(2)}, u32[]{:S(2)}) collective-permute-start(f32[24,128]{1,0:T(8,128)S(1)} %get-tuple-element.75), channel_id=1, source_target_pairs={{0,4},{4,0},{8,12},{12,8},{16,20},{20,16},{24,28},{28,24},{1,5},{5... | collective-permute-start | bytes 36872 | tf_op jit(solution)/shard_map/ppermute | solution.py:41
  6.5 7.4 %collective-permute-start.1 = (f32[24,128]{1,0:T(8,128)S(1)}, f32[24,128]{1,0:T(8,128)S(1)}, u32[]{:S(2)}, u32[]{:S(2)}) collective-permute-start(f32[24,128]{1,0:T(8,128)S(1)} %get-tuple-element.76), channel_id=1, source_target_pairs={{4,8},{8,4},{12,16},{16,12},{20,24},{24,20},{28,0},{0,28},{5,9},{9... | collective-permute-start | bytes 36872 | tf_op jit(solution)/shard_map/ppermute | solution.py:41
  9.7 4.1 %collective-permute-start.2 = (f32[24,128]{1,0:T(8,128)S(1)}, f32[24,128]{1,0:T(8,128)S(1)}, u32[]{:S(2)}, u32[]{:S(2)}) collective-permute-start(f32[24,128]{1,0:T(8,128)S(1)} %get-tuple-element.77), channel_id=1, source_target_pairs={{0,1},{1,0},{2,3},{3,2},{4,5},{5,4},{6,7},{7,6},{8,9},{9,8},{10,11... | collective-permute-start | bytes 36872 | tf_op jit(solution)/shard_map/ppermute | solution.py:41
  11.0 3.1 %collective-permute-start.3 = (f32[24,128]{1,0:T(8,128)S(1)}, f32[24,128]{1,0:T(8,128)S(1)}, u32[]{:S(2)}, u32[]{:S(2)}) collective-permute-start(f32[24,128]{1,0:T(8,128)S(1)} %get-tuple-element.78), channel_id=1, source_target_pairs={{1,2},{2,1},{3,0},{0,3},{5,6},{6,5},{7,4},{4,7},{9,10},{10,9},{11,... | collective-permute-start | bytes 36872 | tf_op jit(solution)/shard_map/ppermute | solution.py:41
  17.9 5.8 %collective-permute-start.4 = (f32[48,128]{1,0:T(8,128)S(1)}, f32[48,128]{1,0:T(8,128)S(1)}, u32[]{:S(2)}, u32[]{:S(2)}) collective-permute-start(f32[48,128]{1,0:T(8,128)S(1)} %get-tuple-element.101), channel_id=1, source_target_pairs={{0,4},{4,0},{8,12},{12,8},{16,20},{20,16},{24,28},{28,24},{1,5},{5... | collective-permute-start | bytes 73736 | tf_op jit(solution)/shard_map/ppermute | solution.py:41
  18.0 5.7 %collective-permute-start.5 = (f32[48,128]{1,0:T(8,128)S(1)}, f32[48,128]{1,0:T(8,128)S(1)}, u32[]{:S(2)}, u32[]{:S(2)}) collective-permute-start(f32[48,128]{1,0:T(8,128)S(1)} %get-tuple-element.102), channel_id=1, source_target_pairs={{4,8},{8,4},{12,16},{16,12},{20,24},{24,20},{28,0},{0,28},{5,9},{9... | collective-permute-start | bytes 73736 | tf_op jit(solution)/shard_map/ppermute | solution.py:41
  19.6 4.1 %collective-permute-start.6 = (f32[48,128]{1,0:T(8,128)S(1)}, f32[48,128]{1,0:T(8,128)S(1)}, u32[]{:S(2)}, u32[]{:S(2)}) collective-permute-start(f32[48,128]{1,0:T(8,128)S(1)} %get-tuple-element.103), channel_id=1, source_target_pairs={{0,1},{1,0},{2,3},{3,2},{4,5},{5,4},{6,7},{7,6},{8,9},{9,8},{10,11... | collective-permute-start | bytes 73736 | tf_op jit(solution)/shard_map/ppermute | solution.py:41
  21.3 3.3 %collective-permute-start.7 = (f32[48,128]{1,0:T(8,128)S(1)}, f32[48,128]{1,0:T(8,128)S(1)}, u32[]{:S(2)}, u32[]{:S(2)}) collective-permute-start(f32[48,128]{1,0:T(8,128)S(1)} %get-tuple-element.104), channel_id=1, source_target_pairs={{1,2},{2,1},{3,0},{0,3},{5,6},{6,5},{7,4},{4,7},{9,10},{10,9},{11,... | collective-permute-start | bytes 73736 | tf_op jit(solution)/shard_map/ppermute | solution.py:41
  28.3 6.0 %collective-permute-start.8 = (f32[24,128]{1,0:T(8,128)S(1)}, f32[24,128]{1,0:T(8,128)S(1)}, u32[]{:S(2)}, u32[]{:S(2)}) collective-permute-start(f32[24,128]{1,0:T(8,128)S(1)} %get-tuple-element.111), channel_id=1, source_target_pairs={{0,4},{4,0},{8,12},{12,8},{16,20},{20,16},{24,28},{28,24},{1,5},{5... | collective-permute-start | bytes 36872 | tf_op jit(solution)/shard_map/ppermute | solution.py:41
  28.4 6.0 %collective-permute-start.9 = (f32[24,128]{1,0:T(8,128)S(1)}, f32[24,128]{1,0:T(8,128)S(1)}, u32[]{:S(2)}, u32[]{:S(2)}) collective-permute-start(f32[24,128]{1,0:T(8,128)S(1)} %get-tuple-element.112), channel_id=1, source_target_pairs={{4,8},{8,4},{12,16},{16,12},{20,24},{24,20},{28,0},{0,28},{5,9},{9... | collective-permute-start | bytes 36872 | tf_op jit(solution)/shard_map/ppermute | solution.py:41
  30.2 4.1 %collective-permute-start.10 = (f32[24,128]{1,0:T(8,128)S(1)}, f32[24,128]{1,0:T(8,128)S(1)}, u32[]{:S(2)}, u32[]{:S(2)}) collective-permute-start(f32[24,128]{1,0:T(8,128)S(1)} %get-tuple-element.113), channel_id=1, source_target_pairs={{0,1},{1,0},{2,3},{3,2},{4,5},{5,4},{6,7},{7,6},{8,9},{9,8},{10,11... | collective-permute-start | bytes 36872 | tf_op jit(solution)/shard_map/ppermute | solution.py:41
  31.8 3.1 %collective-permute-start.11 = (f32[24,128]{1,0:T(8,128)S(1)}, f32[24,128]{1,0:T(8,128)S(1)}, u32[]{:S(2)}, u32[]{:S(2)}) collective-permute-start(f32[24,128]{1,0:T(8,128)S(1)} %get-tuple-element.114), channel_id=1, source_target_pairs={{1,2},{2,1},{3,0},{0,3},{5,6},{6,5},{7,4},{4,7},{9,10},{10,9},{11,... | collective-permute-start | bytes 36872 | tf_op jit(solution)/shard_map/ppermute | solution.py:41
  38.8 5.9 %collective-permute-start.12 = (f32[96,128]{1,0:T(8,128)S(1)}, f32[96,128]{1,0:T(8,128)S(1)}, u32[]{:S(2)}, u32[]{:S(2)}) collective-permute-start(f32[96,128]{1,0:T(8,128)S(1)} %get-tuple-element.122), channel_id=1, source_target_pairs={{0,4},{4,0},{8,12},{12,8},{16,20},{20,16},{24,28},{28,24},{1,5},{5... | collective-permute-start | bytes 147464 | tf_op jit(solution)/shard_map/ppermute | solution.py:41
  38.8 5.8 %collective-permute-start.13 = (f32[96,128]{1,0:T(8,128)S(1)}, f32[96,128]{1,0:T(8,128)S(1)}, u32[]{:S(2)}, u32[]{:S(2)}) collective-permute-start(f32[96,128]{1,0:T(8,128)S(1)} %get-tuple-element.123), channel_id=1, source_target_pairs={{4,8},{8,4},{12,16},{16,12},{20,24},{24,20},{28,0},{0,28},{5,9},{9... | collective-permute-start | bytes 147464 | tf_op jit(solution)/shard_map/ppermute | solution.py:41
  40.7 3.9 %collective-permute-start.14 = (f32[96,128]{1,0:T(8,128)S(1)}, f32[96,128]{1,0:T(8,128)S(1)}, u32[]{:S(2)}, u32[]{:S(2)}) collective-permute-start(f32[96,128]{1,0:T(8,128)S(1)} %get-tuple-element.124), channel_id=1, source_target_pairs={{0,1},{1,0},{2,3},{3,2},{4,5},{5,4},{6,7},{7,6},{8,9},{9,8},{10,11... | collective-permute-start | bytes 147464 | tf_op jit(solution)/shard_map/ppermute | solution.py:41
  42.2 3.5 %collective-permute-start.15 = (f32[96,128]{1,0:T(8,128)S(1)}, f32[96,128]{1,0:T(8,128)S(1)}, u32[]{:S(2)}, u32[]{:S(2)}) collective-permute-start(f32[96,128]{1,0:T(8,128)S(1)} %get-tuple-element.125), channel_id=1, source_target_pairs={{1,2},{2,1},{3,0},{0,3},{5,6},{6,5},{7,4},{4,7},{9,10},{10,9},{11,... | collective-permute-start | bytes 147464 | tf_op jit(solution)/shard_map/ppermute | solution.py:41

commit v3 on v2

--- a/solution.py
+++ b/solution.py
@@ -22,6 +22,7 @@
 BF16 = jnp.bfloat16
 BLOCKS = ((0, 32), (32, 24))
 GROUPS = ((0, 1), (2, 3), (4,))
+GROUPS_AT = (1, 2, 1, 4)
 
 
 def paired(axis):
@@ -213,6 +214,26 @@
     return jnp.where(sub == index_row, 1.0, 0.0).astype(BF16)
 
 
+def send_hot(index_row, lanes):
+    half = lanes // 2
+    column, _ = lane_places(1, lanes)
+    sub = lax.broadcasted_iota(jnp.int32, (half, lanes), 0)
+    blocks = []
+    for j in range(4):
+        for side in range(2):
+            target = jnp.where(column % 2 == side, index_row - j * half, -1)
+            blocks.append(jnp.where(sub == target, 1.0, 0.0).astype(BF16))
+    return jnp.concatenate(blocks, axis=0)
+
+
+def pick_faces(face_ref, chosen, lanes):
+    rows = []
+    for q in range(PAIRS):
+        cols = slice(q * lanes, (q + 1) * lanes)
+        rows.append(jnp.concatenate([face_ref[j * FACE_UP : (j + 1) * FACE_UP, cols] for j in range(4)], axis=1))
+    return pick(jnp.concatenate(rows, axis=0), chosen)
+
+
 def lane_places(rows, lanes):
     lane = lax.broadcasted_iota(jnp.int32, (rows, lanes), 1)
     return lane // (4 * SLOT), (lane // SLOT) % 4
@@ -236,18 +257,11 @@
     return rows
 
 
-def fill_messages(tables, chosen, out_refs, lanes):
+def fill_messages(picks, out_refs, lanes):
     column, place = lane_places(FACE_UP, lanes)
-    for group, table in enumerate(tables):
-        picked = pick(table, chosen(group))
-        quads = []
-        for quad in range(3):
-            merged = picked[4 * quad * FACE_UP : (4 * quad + 1) * FACE_UP]
-            for c in range(1, 4):
-                f = 4 * quad + c
-                if f < FIELDS:
-                    merged = jnp.where(column == c, picked[f * FACE_UP : (f + 1) * FACE_UP], merged)
-            quads.append(merged)
+    for group, picked in enumerate(picks):
+        pairs = [picked[q * FACE_UP : (q + 1) * FACE_UP] for q in range(PAIRS)]
+        quads = [jnp.where(column < 2, pairs[0], pairs[1]), jnp.where(column < 2, pairs[2], pairs[3]), pairs[4]]
         messages = []
         for d in range(4):
             message = None
@@ -284,29 +298,27 @@
                 merged = moved if merged is None else jnp.where(place == d, moved, merged)
             quads.append(merged)
     turned = jnp.dot(turn_ref[...], face_operand(jnp.concatenate(quads, axis=1)), preferred_element_type=F32)
-    high, low = halves(turned)
-    lefts = []
-    for part in (high, low):
-        columns = []
-        for group in range(groups):
-            for which in range(3):
-                rows = slice(which * FACE_UP, (which + 1) * FACE_UP)
-                pieces = []
-                for f in range(FIELDS):
-                    at = (3 * group + f // 4) * lanes
-                    pieces.append(jnp.where(column == f % 4, part[rows, at : at + lanes], 0.0))
-                pieces.append(jnp.zeros((FACE_UP, lanes), F32))
-                columns.append(jnp.concatenate(pieces, axis=0))
-        lefts.append(jnp.concatenate(columns, axis=1))
-    left = jnp.concatenate(lefts, axis=0).astype(BF16)
-    out = jnp.dot(left, far_ref[0 : 3 * groups * lanes, :], preferred_element_type=F32)
-    return out[:ROWS] + out[ROWS:]
+    columns = []
+    for group in range(groups):
+        pieces = []
+        for f in range(FIELDS):
+            at = (3 * group + f // 4) * lanes
+            piece = None
+            for which in (2, 1, 0):
+                moved = turned[which * FACE_UP : (which + 1) * FACE_UP, at : at + lanes]
+                shift = ((which - f % 4) * 4 * SLOT) % lanes
+                moved = pltpu.roll(moved, shift, 1) if shift else moved
+                piece = moved if piece is None else jnp.where(column == which, moved, piece)
+            pieces.append(piece)
+        columns.append(jnp.concatenate(pieces, axis=0))
+    left = columns[0] if groups == 1 else jnp.concatenate(columns, axis=1)
+    return pick(left, far_ref[0 : groups * lanes, :])
 
 
 def gather_faces(in_refs, groups, near_ref, far_ref, turn_ref, aplus_ref, c_ref, lanes):
     half = lanes // 2
     low = low_half((FACE_UP, lanes), half)
-    values = near_ref[...] + take_messages(in_refs, groups, far_ref, turn_ref, lanes)
+    values = near_ref[0 : FIELDS * FACE_UP, :] + take_messages(in_refs, groups, far_ref, turn_ref, lanes)
     for group in GROUPS:
         fields = [g for q in group for g in (2 * q, 2 * q + 1) if g < FIELDS]
         for k in range(2):
@@ -350,36 +362,33 @@
 
 
 def first_kernel(
-    state_hbm, star_hbm, ck_hbm, project_hbm, cluster_hbm, elem_hbm, face_hbm,
-    aminus_hbm, aplus_hbm, vol_hbm, flux_hbm, lift_hbm, rotate_hbm, neighbour_hbm, orient_hbm,
-    packed_ref, star_out, ck_out, proj_out, send_out, star_ref, cluster_ref,
-    aminus_out, aplus_out, vol_out, flux_out, lift_out, rotate_out, neighbour_out, orient_out,
-    state_ref, ck_ref, project_ref, elem_ref, face_ref, early, late, *, lanes,
+    state_hbm, star_hbm, ck_hbm, project_hbm, cluster_hbm, elem_hbm, face_hbm, *rest, lanes
 ):
+    count = (len(rest) - 14) // 2
+    late_hbm, rest = rest[:count], rest[count:]
+    packed_ref, star_out, ck_out, proj_out, send_out, star_ref, cluster_ref = rest[:7]
+    late_out, rest = rest[7 : 7 + count], rest[7 + count :]
+    state_ref, ck_ref, project_ref, elem_ref, face_ref, early, late = rest
     soon = [
         pltpu.make_async_copy(source, target, early.at[i])
         for i, (source, target) in enumerate((
-            (state_hbm, state_ref), (star_hbm, star_ref), (ck_hbm, ck_ref), (cluster_hbm, cluster_ref),
-            (project_hbm, project_ref), (elem_hbm, elem_ref), (face_hbm, face_ref),
+            (star_hbm, star_ref), (state_hbm, state_ref), (ck_hbm, ck_ref), (project_hbm, project_ref),
+            (elem_hbm, elem_ref), (face_hbm, face_ref), (cluster_hbm, cluster_ref),
         ))
     ]
-    then = [
-        pltpu.make_async_copy(source, target, late.at[i])
-        for i, (source, target) in enumerate((
-            (aminus_hbm, aminus_out), (aplus_hbm, aplus_out), (vol_hbm, vol_out), (flux_hbm, flux_out),
-            (lift_hbm, lift_out), (rotate_hbm, rotate_out), (neighbour_hbm, neighbour_out), (orient_hbm, orient_out),
-        ))
-    ]
+    then = [pltpu.make_async_copy(a, b, late.at[i]) for i, (a, b) in enumerate(zip(late_hbm, late_out))]
     for copy in soon + then:
         copy.start()
-    for copy in soon:
-        copy.wait()
-    for q in range(PAIRS):
-        packed_ref[:, q * lanes : (q + 1) * lanes] = pair(state_ref[2 * q], state_ref[min(2 * q + 1, FIELDS - 1)])
+    soon[0].wait()
     pack_coefs(star_ref, 3, 0, star_out)
     for g in range(FIELDS):
         both = star_ref[FIELDS - 1, g]
         pack_last([both[d : d + 1] for d in range(3)], g, star_out)
+    soon[1].wait()
+    for q in range(PAIRS):
+        packed_ref[:, q * lanes : (q + 1) * lanes] = pair(state_ref[2 * q], state_ref[min(2 * q + 1, FIELDS - 1)])
+    for copy in soon[2:]:
+        copy.wait()
     ck_out[...] = left_parts(-ck_ref[...].reshape(3 * MODES, MODES), MODES_UP).astype(BF16)
     proj_rows = [pad_rows(project_ref[:, j, :], FACE_UP) for j in range(4)]
     proj_out[...] = left_parts(jnp.concatenate(proj_rows, axis=0), MODES_UP).astype(BF16)
@@ -400,27 +409,16 @@
     predict(state_of, ck_ref, star_ref, weight_ref, proj_ref, faces_ref, m_ref, i_ref, lanes)
 
 
-def send_kernel(faces_ref, send_ref, *rest, lanes, tick, olds):
-    old_refs = rest[:olds]
-    m0, m1, m2, m3, table_ref = rest[olds : olds + 5]
-    fill_table(faces_ref, table_ref, lanes)
-    table = table_ref[...]
-    tables = [table]
-    if tick == 1:
-        two = old_refs[0][...] + table
-        rest[olds + 5][...] = two
-        tables.append(two)
-    if tick == 3:
-        two = old_refs[0][...] + table
-        four = old_refs[1][...] + two
-        tables += [two, four, four]
-
-    def chosen(group):
-        if tick:
-            return send_ref[:, group * lanes : (group + 1) * lanes]
-        return one_hot(send_ref[group : group + 1, :], 2 * lanes)
-
-    fill_messages(tables, chosen, (m0, m1, m2, m3), lanes)
+def send_kernel(faces_ref, send_ref, *rest, lanes, tick):
+    if tick % 2:
+        held_ref, rest = rest[0], rest[1:]
+    count = GROUPS_AT[tick]
+    chosen = send_ref[:, 0 : count * lanes] if tick else send_hot(send_ref[0:1, :], lanes)
+    picked = pick_faces(faces_ref, chosen, lanes)
+    picks = [picked[:, group * lanes : (group + 1) * lanes] for group in range(count)]
+    for group in range(1, count):
+        picks[group] = picks[group] + held_ref[:, (group - 1) * lanes : group * lanes]
+    fill_messages(picks, rest, lanes)
 
 
 def prepare_kernel(
@@ -449,20 +447,24 @@
     turned = jnp.concatenate([orient_ref[j : j + 1, :] for j in range(4)], axis=1)
     near_out[...] = one_hot(row, 4 * half)
     sub = lax.broadcasted_iota(jnp.int32, (lanes, 4 * half), 0)
-    for group in range(4):
+    for group in range(send_ref.shape[0]):
         target = 4 * half + ((sub // SLOT) % 4) * (4 * SLOT) + group * SLOT + sub % SLOT
-        for which in range(3):
-            at = (3 * group + which) * lanes
-            hit = (target == row) & (turned == which)
-            far_out[at : at + lanes, :] = jnp.where(hit, 1.0, 0.0).astype(BF16)
+        hit = (target == row) & (turned == sub // (4 * SLOT))
+        far_out[group * lanes : (group + 1) * lanes, :] = jnp.where(hit, 1.0, 0.0).astype(BF16)
     for group in range(send_ref.shape[0]):
-        send_out[:, group * lanes : (group + 1) * lanes] = one_hot(send_ref[group : group + 1, :], 4 * half)
+        send_out[:, group * lanes : (group + 1) * lanes] = send_hot(send_ref[group : group + 1, :], lanes)
 
 
 def local_kernel(
-    i_ref, packed_ref, table_ref, cluster_ref, coef_ref, left_ref, near_ref, turn_ref, orient_ref, own_ref, seen_ref,
-    base_out, own_out, seen_out, m_ref, *, lanes, tick,
+    i_ref, packed_ref, faces_ref, cluster_ref, coef_ref, left_ref, near_ref, turn_ref, orient_ref, own_ref, seen_ref,
+    send_ref, held_ref, base_out, own_out, seen_out, *rest, lanes, tick,
 ):
+    m_ref, table_ref = rest[-2:]
+    fill_table(faces_ref, table_ref, lanes)
+    if tick < TICKS - 1:
+        picked = pick_faces(faces_ref, send_ref[:, lanes:], lanes)
+        rest[0][:, 0:lanes] = picked[:, 0:lanes]
+        rest[0][:, lanes:] = held_ref[:, lanes:] + picked[:, lanes:] if tick else picked[:, lanes:]
     cluster = pair(cluster_ref[...], cluster_ref[...])
     offset, finished = timing(cluster, tick)
     two = jnp.concatenate([offset, offset], axis=1)
@@ -505,9 +507,11 @@
 
 
 def last_kernel(
-    r0, r1, r2, r3, near_ref, far_ref, turn_ref, aplus_ref, lift_ref, base_ref, cluster_ref, out_ref, c_ref, *, lanes,
+    r0, r1, r2, r3, near_ref, far_ref, turn_ref, aplus_ref, lift_ref, base_ref, cluster_ref, result_hbm,
+    c_ref, out_ref, gone, *, lanes,
 ):
     half = lanes // 2
+    copies = []
     _, finished = timing(pair(cluster_ref[...], cluster_ref[...]), TICKS - 1)
     gather_faces((r0, r1, r2, r3), 4, near_ref, far_ref, turn_ref, aplus_ref, c_ref, lanes)
     for group in GROUPS:
@@ -516,6 +520,12 @@
             for side in range(2):
                 if 2 * q + side < FIELDS:
                     out_ref[2 * q + side] = values[:, i * lanes + side * half : i * lanes + (side + 1) * half]
+        fields = pl.ds(2 * group[0], min(2 * len(group), FIELDS - 2 * group[0]))
+        copy = pltpu.make_async_copy(out_ref.at[fields], result_hbm.at[fields], gone.at[GROUPS.index(group)])
+        copy.start()
+        copies.append(copy)
+    for copy in copies:
+        copy.wait()
 
 
 def stages(slots, dirs, lanes):
@@ -524,16 +534,17 @@
     return [[wide, wide, last] for _ in range(slots)]
 
 
-def call(body, outs, scratch, name, flops, arrays, far=False):
+def call(body, outs, scratch, name, flops, arrays, far=0, far_out=False):
     moved = sum(a.size * a.dtype.itemsize for a in arrays)
-    space = pltpu.MemorySpace.HBM if far else pltpu.VMEM
-    if far:
-        arrays = [pltpu.with_memory_space_constraint(x, pltpu.MemorySpace.HBM) for x in arrays]
+    hbm = pltpu.MemorySpace.HBM
+    near = len(arrays) - far
+    arrays = [*arrays[:near], *(pltpu.with_memory_space_constraint(x, hbm) for x in arrays[near:])]
+    spaces = [pltpu.VMEM] * near + [hbm] * far
     return pl.pallas_call(
         body,
         out_shape=outs,
-        in_specs=[pl.BlockSpec(memory_space=space)] * len(arrays),
-        out_specs=[pl.BlockSpec(memory_space=pltpu.VMEM)] * len(outs),
+        in_specs=[pl.BlockSpec(memory_space=space) for space in spaces],
+        out_specs=[pl.BlockSpec(memory_space=hbm if far_out else pltpu.VMEM)] * len(outs),
         scratch_shapes=scratch,
         compiler_params=pltpu.CompilerParams(vmem_limit_bytes=24 << 20),
         cost_estimate=pl.CostEstimate(flops=flops, bytes_accessed=moved, transcendentals=0),
@@ -587,11 +598,11 @@
         [room(state), room(ck_stiff), room(project), room(send_elem), room(send_face)]
         + [pltpu.SemaphoreType.DMA((7,)), pltpu.SemaphoreType.DMA((len(late),))],
         "first", 10_000_000,
-        (state, star, ck_stiff, project, cluster_row, send_elem, send_face, *late), far=True,
+        (state, star, ck_stiff, project, cluster_row, send_elem, send_face, *late), far=7 + len(late),
     )
     orient = late[-1]
 
-    def predicted(tick, packed, chosen, olds):
+    def predicted(tick, packed, chosen, more):
         integral, face_values = call(
             functools.partial(predict_kernel, lanes=lanes, tick=tick),
             [modal, faces],
@@ -599,17 +610,14 @@
             f"predict{tick}", 400_000_000,
             (packed, cluster_row, ck_left, star_pairs, proj_left),
         )
-        out = call(
-            functools.partial(send_kernel, lanes=lanes, tick=tick, olds=len(olds)),
-            message((1, 2, 1, 4)[tick]) + [table] + ([table] if tick == 1 else []),
-            [],
-            f"send{tick}", 50_000_000,
-            (face_values, chosen, *olds),
+        messages = call(
+            functools.partial(send_kernel, lanes=lanes, tick=tick),
+            message(GROUPS_AT[tick]), [], f"send{tick}", 50_000_000, (face_values, chosen, *more),
         )
-        return integral, out[:4], out[4:]
-
-    integral, messages, (table_now,) = predicted(0, packed, send, ())
-    coef, aplus_pairs, left, lift_left, turn, near_hot, far_hot, send_hot = call(
+        return integral, face_values, messages
+
+    integral, face_values, messages = predicted(0, packed, send, ())
+    coef, aplus_pairs, left, lift_left, turn, near_hot, far_hot, chosen = call(
         functools.partial(prepare_kernel, lanes=lanes),
         [
             shape((PAIRS * FIELDS, 7, lanes), F32),
@@ -618,35 +626,37 @@
             shape((MODES, 12 * FACE_UP), BF16),
             shape((3 * FACE_UP, 80), BF16),
             shape((4 * elems, 4 * elems), BF16),
-            shape((12 * lanes, 4 * elems), BF16),
-            shape((4 * elems, groups * lanes), BF16),
+            shape((groups * lanes, 4 * elems), BF16),
+            shape((4 * lanes, groups * lanes), BF16),
         ],
         [],
         "prepare", 100_000_000,
         (star, *late, send),
     )
     own = integral
-    seen = table_now
-    two = None
+    seen = near_hot
+    held = near_hot
     for tick in range(TICKS):
         arrived = [None] * 4
         for slot, axis, phase in ((1, "slab", 1), (0, "slab", 0), (3, "sub", 1), (2, "sub", 0)):
             arrived[slot] = exchange(messages[slot], axis, phase)
-        base, own, seen = call(
+        last = tick == TICKS - 1
+        base, own, seen, *kept = call(
             functools.partial(local_kernel, lanes=lanes, tick=tick),
-            [modal, modal, table],
-            [stages(1, 7, lanes)],
+            [modal, modal, table] + ([] if last else [shape((PAIRS * FACE_UP, (groups - 1) * lanes), F32)]),
+            [stages(1, 7, lanes), pltpu.VMEM((ROWS, 4 * elems), F32)],
             f"local{tick}", 300_000_000,
-            (integral, packed, table_now, cluster_row, coef, left, near_hot, turn, orient, own, seen),
+            (integral, packed, face_values, cluster_row, coef, left, near_hot, turn, orient, own, seen, chosen, held),
         )
-        count = (1, 2, 1, 4)[tick]
+        held = held if last else kept[0]
+        count = GROUPS_AT[tick]
         common = (*arrived, seen, far_hot, turn, aplus_pairs, lift_left, base, cluster_row)
-        if tick == TICKS - 1:
+        if last:
             return call(
                 functools.partial(last_kernel, lanes=lanes),
                 [shape(state.shape, F32)],
-                [sides],
-                "last", 100_000_000, common,
+                [sides, room(state), pltpu.SemaphoreType.DMA((len(GROUPS),))],
+                "last", 100_000_000, common, far_out=True,
             )[0]
         packed = call(
             functools.partial(update_kernel, lanes=lanes, tick=tick, groups=count),
@@ -654,11 +664,7 @@
             [sides],
             f"update{tick}", 100_000_000, common,
         )[0]
-        olds = {0: (table_now,), 1: (), 2: (table_now, two)}[tick]
-        integral, messages, tables = predicted(tick + 1, packed, send_hot, olds)
-        table_now = tables[0]
-        if tick == 0:
-            two = tables[1]
+        integral, face_values, messages = predicted(tick + 1, packed, chosen, (held,) if tick % 2 == 0 else ())
 
 
 def solution(mesh):

time: 48.1 us -> 47.9 us (level)
  no operation moved by 1% of the time
where the time goes in v3:
time: 47.9 us; the launch traced here: 47.4 us
  Pallas kernels  23 us (48%)
  starting transfers between devices  21.4 us (45%)
  waiting for transfers between devices  2.61 us (5%)
    pallas_call x18, Pallas kernels, call(): pl.pallas_call(body, out_shape=outs, in_specs=[pl.BlockSpec(memory_space=...  23 us
    ppermute x16, starting transfers between devices, exchange(): return lax.ppermute(x, axis, pairs)  21.4 us
    ppermute x16, waiting for transfers between devices, exchange(): return lax.ppermute(x, axis, pairs)  2.61 us
  transfers between devices with their start and end apart: 16, of which 4 were waited for; matrix products, arithmetic and copies ran while one was open for 0% of the time, Pallas kernels for 12%

profile of v3, /device:TPU:1, one launch (start us, length us, event | category | flops | bytes accessed | tf_op | source)
XLA Modules:
  0.0 47.4 jit_solution(4643740926795068368)
XLA Ops:
  0.0 1.6 %first.1 = (f32[56,640]{1,0:T(8,128)S(1)}, f32[45,3,128]{2,1,0:T(4,128)S(1)}, bf16[168,192]{1,0:T(8,128)(2,1)S(1)}, bf16[96,192]{1,0:T(8,128)(2,1)S(1)}, s32[4,1...) custom-call(f32[9,56,64]{2,1,0:T(8,128)} %state_hbm.1, ...), custom_call_target="tpu_custom_call" | custom-call | flops 10000000 | bytes 528812 | tf_op jit(solution)/shard_map/first/pallas_call | solution.py:543
  1.6 2.4 %predict0.1 = (f32[56,640]{1,0:T(8,128)S(1)}, f32[96,640]{1,0:T(8,128)S(1)}) custom-call(f32[56,640]{1,0:T(8,128)S(1)} %get-tuple-element.66.packed_ref, s32[1,64]{1,0:T(1,128)S(1)} %get-tuple-element.67.cluster_ref, bf16[168,192]{1,0:T(8,128)(2,1)S(1)} %get-tuple-element.68.ck_ref, f32[45,3,128]{2,1,0:T(4,128)S(1)} %get-tuple-element.69.star_ref, ...), custom_call_target="tpu_custom_call" | custom-call | flops 400000000 | bytes 314112 | tf_op jit(solution)/shard_map/predict0/pallas_call | solution.py:543
  4.0 0.3 send0.1
  4.3 2.1 %collective-permute-start = (f32[24,128]{1,0:T(8,128)S(1)}, f32[24,128]{1,0:T(8,128)S(1)}, u32[]{:S(2)}, u32[]{:S(2)}) collective-permute-start(f32[24,128]{1,0:T(8,128)S(1)} %get-tuple-element.73), channel_id=1, source_target_pairs={{0,4},{4,0},{8,12},{12,8},{16,20},{20,16},{24,28},{28,24},{1,5},{5... | collective-permute-start | bytes 36872 | tf_op jit(solution)/shard_map/ppermute | solution.py:42
  6.4 3.3 %collective-permute-start.1 = (f32[24,128]{1,0:T(8,128)S(1)}, f32[24,128]{1,0:T(8,128)S(1)}, u32[]{:S(2)}, u32[]{:S(2)}) collective-permute-start(f32[24,128]{1,0:T(8,128)S(1)} %get-tuple-element.74), channel_id=1, source_target_pairs={{4,8},{8,4},{12,16},{16,12},{20,24},{24,20},{28,0},{0,28},{5,9},{9... | collective-permute-start | bytes 36872 | tf_op jit(solution)/shard_map/ppermute | solution.py:42
  9.7 1.2 %collective-permute-start.2 = (f32[24,128]{1,0:T(8,128)S(1)}, f32[24,128]{1,0:T(8,128)S(1)}, u32[]{:S(2)}, u32[]{:S(2)}) collective-permute-start(f32[24,128]{1,0:T(8,128)S(1)} %get-tuple-element.75), channel_id=1, source_target_pairs={{0,1},{1,0},{2,3},{3,2},{4,5},{5,4},{6,7},{7,6},{8,9},{9,8},{10,11... | collective-permute-start | bytes 36872 | tf_op jit(solution)/shard_map/ppermute | solution.py:42
  10.9 1.1 %collective-permute-start.3 = (f32[24,128]{1,0:T(8,128)S(1)}, f32[24,128]{1,0:T(8,128)S(1)}, u32[]{:S(2)}, u32[]{:S(2)}) collective-permute-start(f32[24,128]{1,0:T(8,128)S(1)} %get-tuple-element.76), channel_id=1, source_target_pairs={{1,2},{2,1},{3,0},{0,3},{5,6},{6,5},{7,4},{4,7},{9,10},{10,9},{11,... | collective-permute-start | bytes 36872 | tf_op jit(solution)/shard_map/ppermute | solution.py:42
  12.0 0.6 %prepare.1 = (f32[45,7,128]{2,1,0:T(8,128)S(1)}, f32[81,2,128]{2,1,0:T(2,128)S(1)}, bf16[392,192]{1,0:T(8,128)(2,1)S(1)}, bf16[56,288]{1,0:T(8,128)(2,1)S(1)}, b...) custom-call(f32[9,9,3,64]{3,2,1,0:T(4,128)S(1)} %get-tuple-element.7, ...), custom_call_target="tpu_custom_call" | custom-call | flops 100000000 | bytes 344108 | tf_op jit(solution)/shard_map/prepare/pallas_call | solution.py:543
  12.6 1.3 %local0.1 = (f32[56,640]{1,0:T(8,128)S(1)}, f32[56,640]{1,0:T(8,128)S(1)}, f32[240,256]{1,0:T(8,128)S(1)}, f32[120,384]{1,0:T(8,128)S(1)}) custom-call(f32[56,640]{1,0:T(8,128)S(1)} %get-tuple-element.77.i_ref.own_ref, f32[56,640]{1,0:T(8,128)S(1)} %get-tuple-element.66.packed_ref, f32[96,640]{1,0:T(8,128)S(1)} %get-tuple-element.71.faces_ref, ...), custom_call_target="tpu_custom_call" | custom-call | flops 300000000 | bytes 1917952 | tf_op jit(solution)/shard_map/local0/pallas_call | solution.py:543
  13.9 0.0 collective-permute-done.r0
  13.9 0.0 collective-permute-done.1.r1
  13.9 0.0 collective-permute-done.2.r2
  13.9 0.1 collective-permute-done.3.r3
  14.0 0.9 %update0.1.packed_ref = f32[56,640]{1,0:T(8,128)S(1)} custom-call(f32[24,128]{1,0:T(8,128)S(1)} %collective-permute-done.r0, f32[24,128]{1,0:T(8,128)S(1)} %collective-permute-done.1.r1, f32[24,128]{1,0:T(8,128)S(1)} %collective-permute-done.2.r2, f32[24,128]{1,0:T(8,128)S(1)} %collective-permute-done.3.r3, ...), custom_call_target="tpu_custom_call" | custom-call | flops 100000000 | bytes 827392 | tf_op jit(solution)/shard_map/update0/pallas_call | solution.py:543
  14.9 2.4 %predict1.1 = (f32[56,640]{1,0:T(8,128)S(1)}, f32[96,640]{1,0:T(8,128)S(1)}) custom-call(f32[56,640]{1,0:T(8,128)S(1)} %update0.1.packed_ref, s32[1,64]{1,0:T(1,128)S(1)} %get-tuple-element.67.cluster_ref, bf16[168,192]{1,0:T(8,128)(2,1)S(1)} %get-tuple-element.68.ck_ref, f32[45,3,128]{2,1,0:T(4,128)S(1)} %get-tuple-element.69.star_ref, ...), custom_call_target="tpu_custom_call" | custom-call | flops 400000000 | bytes 314112 | tf_op jit(solution)/shard_map/predict1/pallas_call | solution.py:543
  17.3 0.3 send1.1
  17.7 0.1 collective-permute-start.4
  17.7 1.6 %collective-permute-start.5 = (f32[48,128]{1,0:T(8,128)S(1)}, f32[48,128]{1,0:T(8,128)S(1)}, u32[]{:S(2)}, u32[]{:S(2)}) collective-permute-start(f32[48,128]{1,0:T(8,128)S(1)} %get-tuple-element.100), channel_id=1, source_target_pairs={{4,8},{8,4},{12,16},{16,12},{20,24},{24,20},{28,0},{0,28},{5,9},{9... | collective-permute-start | bytes 73736 | tf_op jit(solution)/shard_map/ppermute | solution.py:42
  19.4 1.7 %collective-permute-start.6 = (f32[48,128]{1,0:T(8,128)S(1)}, f32[48,128]{1,0:T(8,128)S(1)}, u32[]{:S(2)}, u32[]{:S(2)}) collective-permute-start(f32[48,128]{1,0:T(8,128)S(1)} %get-tuple-element.101), channel_id=1, source_target_pairs={{0,1},{1,0},{2,3},{3,2},{4,5},{5,4},{6,7},{7,6},{8,9},{9,8},{10,11... | collective-permute-start | bytes 73736 | tf_op jit(solution)/shard_map/ppermute | solution.py:42
  21.1 1.1 %collective-permute-start.7 = (f32[48,128]{1,0:T(8,128)S(1)}, f32[48,128]{1,0:T(8,128)S(1)}, u32[]{:S(2)}, u32[]{:S(2)}) collective-permute-start(f32[48,128]{1,0:T(8,128)S(1)} %get-tuple-element.102), channel_id=1, source_target_pairs={{1,2},{2,1},{3,0},{0,3},{5,6},{6,5},{7,4},{4,7},{9,10},{10,9},{11,... | collective-permute-start | bytes 73736 | tf_op jit(solution)/shard_map/ppermute | solution.py:42
  22.2 1.3 %local1.1 = (f32[56,640]{1,0:T(8,128)S(1)}, f32[56,640]{1,0:T(8,128)S(1)}, f32[240,256]{1,0:T(8,128)S(1)}, f32[120,384]{1,0:T(8,128)S(1)}) custom-call(f32[56,640]{1,0:T(8,128)S(1)} %get-tuple-element.103.i_ref, f32[56,640]{1,0:T(8,128)S(1)} %update0.1.packed_ref, f32[96,640]{1,0:T(8,128)S(1)} %get-tuple-element.97.faces_ref, ...), custom_call_target="tpu_custom_call" | custom-call | flops 300000000 | bytes 2085888 | tf_op jit(solution)/shard_map/local1/pallas_call | solution.py:543
  23.5 0.0 collective-permute-done.4.r0
  23.5 0.0 collective-permute-done.5.r1
  23.5 0.8 %collective-permute-done.7.r3 = f32[48,128]{1,0:T(8,128)S(1)} collective-permute-done((f32[48,128]{1,0:T(8,128)S(1)}, f32[48,128]{1,0:T(8,128)S(1)}, u32[]{:S(2)}, u32[]{:S(2)}) %collective-permute-start.7) | collective-permute-done | bytes 24608 | tf_op jit(solution)/shard_map/ppermute | solution.py:42
  24.4 1.0 %update1.1.packed_ref = f32[56,640]{1,0:T(8,128)S(1)} custom-call(f32[48,128]{1,0:T(8,128)S(1)} %collective-permute-done.4.r0, f32[48,128]{1,0:T(8,128)S(1)} %collective-permute-done.5.r1, f32[48,128]{1,0:T(8,128)S(1)} %collective-permute-done.6.r2, f32[48,128]{1,0:T(8,128)S(1)} %collective-permute-done.7.r3, ...), custom_call_target="tpu_custom_call" | custom-call | flops 100000000 | bytes 876544 | tf_op jit(solution)/shard_map/update1/pallas_call | solution.py:543
  25.3 2.4 %predict2.1 = (f32[56,640]{1,0:T(8,128)S(1)}, f32[96,640]{1,0:T(8,128)S(1)}) custom-call(f32[56,640]{1,0:T(8,128)S(1)} %update1.1.packed_ref, s32[1,64]{1,0:T(1,128)S(1)} %get-tuple-element.67.cluster_ref, bf16[168,192]{1,0:T(8,128)(2,1)S(1)} %get-tuple-element.68.ck_ref, f32[45,3,128]{2,1,0:T(4,128)S(1)} %get-tuple-element.69.star_ref, ...), custom_call_target="tpu_custom_call" | custom-call | flops 400000000 | bytes 314112 | tf_op jit(solution)/shard_map/predict2/pallas_call | solution.py:543
  27.7 0.3 send2.1
  28.0 0.1 collective-permute-start.8
  28.1 1.9 %collective-permute-start.9 = (f32[24,128]{1,0:T(8,128)S(1)}, f32[24,128]{1,0:T(8,128)S(1)}, u32[]{:S(2)}, u32[]{:S(2)}) collective-permute-start(f32[24,128]{1,0:T(8,128)S(1)} %get-tuple-element.109), channel_id=1, source_target_pairs={{4,8},{8,4},{12,16},{16,12},{20,24},{24,20},{28,0},{0,28},{5,9},{9... | collective-permute-start | bytes 36872 | tf_op jit(solution)/shard_map/ppermute | solution.py:42
  30.0 1.5 %collective-permute-start.10 = (f32[24,128]{1,0:T(8,128)S(1)}, f32[24,128]{1,0:T(8,128)S(1)}, u32[]{:S(2)}, u32[]{:S(2)}) collective-permute-start(f32[24,128]{1,0:T(8,128)S(1)} %get-tuple-element.110), channel_id=1, source_target_pairs={{0,1},{1,0},{2,3},{3,2},{4,5},{5,4},{6,7},{7,6},{8,9},{9,8},{10,11... | collective-permute-start | bytes 36872 | tf_op jit(solution)/shard_map/ppermute | solution.py:42
  31.5 1.1 %collective-permute-start.11 = (f32[24,128]{1,0:T(8,128)S(1)}, f32[24,128]{1,0:T(8,128)S(1)}, u32[]{:S(2)}, u32[]{:S(2)}) collective-permute-start(f32[24,128]{1,0:T(8,128)S(1)} %get-tuple-element.111), channel_id=1, source_target_pairs={{1,2},{2,1},{3,0},{0,3},{5,6},{6,5},{7,4},{4,7},{9,10},{10,9},{11,... | collective-permute-start | bytes 36872 | tf_op jit(solution)/shard_map/ppermute | solution.py:42
  32.6 1.5 %local2.1 = (f32[56,640]{1,0:T(8,128)S(1)}, f32[56,640]{1,0:T(8,128)S(1)}, f32[240,256]{1,0:T(8,128)S(1)}, f32[120,384]{1,0:T(8,128)S(1)}) custom-call(f32[56,640]{1,0:T(8,128)S(1)} %get-tuple-element.112.i_ref, f32[56,640]{1,0:T(8,128)S(1)} %update1.1.packed_ref, f32[96,640]{1,0:T(8,128)S(1)} %get-tuple-element.107.faces_ref, ...), custom_call_target="tpu_custom_call" | custom-call | flops 300000000 | bytes 2085888 | tf_op jit(solution)/shard_map/local2/pallas_call | solution.py:543
  34.1 0.0 collective-permute-done.8.r0
  34.1 0.0 collective-permute-done.9.r1
  34.1 0.5 %collective-permute-done.11.r3 = f32[24,128]{1,0:T(8,128)S(1)} collective-permute-done((f32[24,128]{1,0:T(8,128)S(1)}, f32[24,128]{1,0:T(8,128)S(1)}, u32[]{:S(2)}, u32[]{:S(2)}) %collective-permute-start.11) | collective-permute-done | bytes 12320 | tf_op jit(solution)/shard_map/ppermute | solution.py:42
  34.6 0.9 %update2.1.packed_ref = f32[56,640]{1,0:T(8,128)S(1)} custom-call(f32[24,128]{1,0:T(8,128)S(1)} %collective-permute-done.8.r0, f32[24,128]{1,0:T(8,128)S(1)} %collective-permute-done.9.r1, f32[24,128]{1,0:T(8,128)S(1)} %collective-permute-done.10.r2, f32[24,128]{1,0:T(8,128)S(1)} %collective-permute-done.11.r3, ...), custom_call_target="tpu_custom_call" | custom-call | flops 100000000 | bytes 827392 | tf_op jit(solution)/shard_map/update2/pallas_call | solution.py:543
  35.5 2.4 %predict3.1 = (f32[56,640]{1,0:T(8,128)S(1)}, f32[96,640]{1,0:T(8,128)S(1)}) custom-call(f32[56,640]{1,0:T(8,128)S(1)} %update2.1.packed_ref, s32[1,64]{1,0:T(1,128)S(1)} %get-tuple-element.67.cluster_ref, bf16[168,192]{1,0:T(8,128)(2,1)S(1)} %get-tuple-element.68.ck_ref, f32[45,3,128]{2,1,0:T(4,128)S(1)} %get-tuple-element.69.star_ref, ...), custom_call_target="tpu_custom_call" | custom-call | flops 400000000 | bytes 314112 | tf_op jit(solution)/shard_map/predict3/pallas_call | solution.py:543
  37.9 0.5 send3.1
  38.4 0.1 collective-permute-start.12
  38.5 1.9 %collective-permute-start.13 = (f32[96,128]{1,0:T(8,128)S(1)}, f32[96,128]{1,0:T(8,128)S(1)}, u32[]{:S(2)}, u32[]{:S(2)}) collective-permute-start(f32[96,128]{1,0:T(8,128)S(1)} %get-tuple-element.120), channel_id=1, source_target_pairs={{4,8},{8,4},{12,16},{16,12},{20,24},{24,20},{28,0},{0,28},{5,9},{9... | collective-permute-start | bytes 147464 | tf_op jit(solution)/shard_map/ppermute | solution.py:42
  40.4 1.4 %collective-permute-start.14 = (f32[96,128]{1,0:T(8,128)S(1)}, f32[96,128]{1,0:T(8,128)S(1)}, u32[]{:S(2)}, u32[]{:S(2)}) collective-permute-start(f32[96,128]{1,0:T(8,128)S(1)} %get-tuple-element.121), channel_id=1, source_target_pairs={{0,1},{1,0},{2,3},{3,2},{4,5},{5,4},{6,7},{7,6},{8,9},{9,8},{10,11... | collective-permute-start | bytes 147464 | tf_op jit(solution)/shard_map/ppermute | solution.py:42
  41.8 1.1 %collective-permute-start.15 = (f32[96,128]{1,0:T(8,128)S(1)}, f32[96,128]{1,0:T(8,128)S(1)}, u32[]{:S(2)}, u32[]{:S(2)}) collective-permute-start(f32[96,128]{1,0:T(8,128)S(1)} %get-tuple-element.122), channel_id=1, source_target_pairs={{1,2},{2,1},{3,0},{0,3},{5,6},{6,5},{7,4},{4,7},{9,10},{10,9},{11,... | collective-permute-start | bytes 147464 | tf_op jit(solution)/shard_map/ppermute | solution.py:42
  42.9 1.2 %local3.1 = (f32[56,640]{1,0:T(8,128)S(1)}, f32[56,640]{1,0:T(8,128)}, f32[240,256]{1,0:T(8,128)S(1)}) custom-call(f32[56,640]{1,0:T(8,128)S(1)} %get-tuple-element.123.i_ref, f32[56,640]{1,0:T(8,128)S(1)} %update2.1.packed_ref, f32[96,640]{1,0:T(8,128)S(1)} %get-tuple-element.117.faces_ref, s32[1,64]{1,0:T(1,128)S(1)} %get-tuple-element.67.cluster_ref, ...), custom_call_target="tpu_custom_call" | custom-call | flops 300000000 | bytes 2085888 | tf_op jit(solution)/shard_map/local3/pallas_call | solution.py:543
  44.1 0.0 collective-permute-done.12.r0
  44.2 0.0 collective-permute-done.13.r1
  44.2 0.0 collective-permute-done.14.r2
  44.2 1.2 %collective-permute-done.15.r3 = f32[96,128]{1,0:T(8,128)S(1)} collective-permute-done((f32[96,128]{1,0:T(8,128)S(1)}, f32[96,128]{1,0:T(8,128)S(1)}, u32[]{:S(2)}, u32[]{:S(2)}) %collective-permute-start.15) | collective-permute-done | bytes 49184 | tf_op jit(solution)/shard_map/ppermute | solution.py:42
  45.3 1.9 %last.1 = f32[9,56,64]{2,1,0:T(8,128)} custom-call(f32[96,128]{1,0:T(8,128)S(1)} %collective-permute-done.12.r0, f32[96,128]{1,0:T(8,128)S(1)} %collective-permute-done.13.r1, f32[96,128]{1,0:T(8,128)S(1)} %collective-permute-done.14.r2, f32[96,128]{1,0:T(8,128)S(1)} %collective-permute-done.15.r3, f32[240,256]{1,0:T(8,128)S(1)} %get-tuple-element.125.near_ref, ...), custom_call_target="tpu_custom_call" | custom-call | flops 100000000 | bytes 974848 | tf_op jit(solution)/shard_map/last/pallas_call | solution.py:543
  (2 shorter events, 0.0 us)
Async XLA Ops:
  4.3 9.6 %collective-permute-start = (f32[24,128]{1,0:T(8,128)S(1)}, f32[24,128]{1,0:T(8,128)S(1)}, u32[]{:S(2)}, u32[]{:S(2)}) collective-permute-start(f32[24,128]{1,0:T(8,128)S(1)} %get-tuple-element.73), channel_id=1, source_target_pairs={{0,4},{4,0},{8,12},{12,8},{16,20},{20,16},{24,28},{28,24},{1,5},{5... | collective-permute-start | bytes 36872 | tf_op jit(solution)/shard_map/ppermute | solution.py:42
  6.4 7.6 %collective-permute-start.1 = (f32[24,128]{1,0:T(8,128)S(1)}, f32[24,128]{1,0:T(8,128)S(1)}, u32[]{:S(2)}, u32[]{:S(2)}) collective-permute-start(f32[24,128]{1,0:T(8,128)S(1)} %get-tuple-element.74), channel_id=1, source_target_pairs={{4,8},{8,4},{12,16},{16,12},{20,24},{24,20},{28,0},{0,28},{5,9},{9... | collective-permute-start | bytes 36872 | tf_op jit(solution)/shard_map/ppermute | solution.py:42
  9.7 4.3 %collective-permute-start.2 = (f32[24,128]{1,0:T(8,128)S(1)}, f32[24,128]{1,0:T(8,128)S(1)}, u32[]{:S(2)}, u32[]{:S(2)}) collective-permute-start(f32[24,128]{1,0:T(8,128)S(1)} %get-tuple-element.75), channel_id=1, source_target_pairs={{0,1},{1,0},{2,3},{3,2},{4,5},{5,4},{6,7},{7,6},{8,9},{9,8},{10,11... | collective-permute-start | bytes 36872 | tf_op jit(solution)/shard_map/ppermute | solution.py:42
  10.9 3.1 %collective-permute-start.3 = (f32[24,128]{1,0:T(8,128)S(1)}, f32[24,128]{1,0:T(8,128)S(1)}, u32[]{:S(2)}, u32[]{:S(2)}) collective-permute-start(f32[24,128]{1,0:T(8,128)S(1)} %get-tuple-element.76), channel_id=1, source_target_pairs={{1,2},{2,1},{3,0},{0,3},{5,6},{6,5},{7,4},{4,7},{9,10},{10,9},{11,... | collective-permute-start | bytes 36872 | tf_op jit(solution)/shard_map/ppermute | solution.py:42
  17.7 5.8 %collective-permute-start.4 = (f32[48,128]{1,0:T(8,128)S(1)}, f32[48,128]{1,0:T(8,128)S(1)}, u32[]{:S(2)}, u32[]{:S(2)}) collective-permute-start(f32[48,128]{1,0:T(8,128)S(1)} %get-tuple-element.99), channel_id=1, source_target_pairs={{0,4},{4,0},{8,12},{12,8},{16,20},{20,16},{24,28},{28,24},{1,5},{5... | collective-permute-start | bytes 73736 | tf_op jit(solution)/shard_map/ppermute | solution.py:42
  17.7 5.8 %collective-permute-start.5 = (f32[48,128]{1,0:T(8,128)S(1)}, f32[48,128]{1,0:T(8,128)S(1)}, u32[]{:S(2)}, u32[]{:S(2)}) collective-permute-start(f32[48,128]{1,0:T(8,128)S(1)} %get-tuple-element.100), channel_id=1, source_target_pairs={{4,8},{8,4},{12,16},{16,12},{20,24},{24,20},{28,0},{0,28},{5,9},{9... | collective-permute-start | bytes 73736 | tf_op jit(solution)/shard_map/ppermute | solution.py:42
  19.4 4.2 %collective-permute-start.6 = (f32[48,128]{1,0:T(8,128)S(1)}, f32[48,128]{1,0:T(8,128)S(1)}, u32[]{:S(2)}, u32[]{:S(2)}) collective-permute-start(f32[48,128]{1,0:T(8,128)S(1)} %get-tuple-element.101), channel_id=1, source_target_pairs={{0,1},{1,0},{2,3},{3,2},{4,5},{5,4},{6,7},{7,6},{8,9},{9,8},{10,11... | collective-permute-start | bytes 73736 | tf_op jit(solution)/shard_map/ppermute | solution.py:42
  21.1 3.3 %collective-permute-start.7 = (f32[48,128]{1,0:T(8,128)S(1)}, f32[48,128]{1,0:T(8,128)S(1)}, u32[]{:S(2)}, u32[]{:S(2)}) collective-permute-start(f32[48,128]{1,0:T(8,128)S(1)} %get-tuple-element.102), channel_id=1, source_target_pairs={{1,2},{2,1},{3,0},{0,3},{5,6},{6,5},{7,4},{4,7},{9,10},{10,9},{11,... | collective-permute-start | bytes 73736 | tf_op jit(solution)/shard_map/ppermute | solution.py:42
  28.0 6.1 %collective-permute-start.8 = (f32[24,128]{1,0:T(8,128)S(1)}, f32[24,128]{1,0:T(8,128)S(1)}, u32[]{:S(2)}, u32[]{:S(2)}) collective-permute-start(f32[24,128]{1,0:T(8,128)S(1)} %get-tuple-element.108), channel_id=1, source_target_pairs={{0,4},{4,0},{8,12},{12,8},{16,20},{20,16},{24,28},{28,24},{1,5},{5... | collective-permute-start | bytes 36872 | tf_op jit(solution)/shard_map/ppermute | solution.py:42
  28.1 6.0 %collective-permute-start.9 = (f32[24,128]{1,0:T(8,128)S(1)}, f32[24,128]{1,0:T(8,128)S(1)}, u32[]{:S(2)}, u32[]{:S(2)}) collective-permute-start(f32[24,128]{1,0:T(8,128)S(1)} %get-tuple-element.109), channel_id=1, source_target_pairs={{4,8},{8,4},{12,16},{16,12},{20,24},{24,20},{28,0},{0,28},{5,9},{9... | collective-permute-start | bytes 36872 | tf_op jit(solution)/shard_map/ppermute | solution.py:42
  30.0 4.1 %collective-permute-start.10 = (f32[24,128]{1,0:T(8,128)S(1)}, f32[24,128]{1,0:T(8,128)S(1)}, u32[]{:S(2)}, u32[]{:S(2)}) collective-permute-start(f32[24,128]{1,0:T(8,128)S(1)} %get-tuple-element.110), channel_id=1, source_target_pairs={{0,1},{1,0},{2,3},{3,2},{4,5},{5,4},{6,7},{7,6},{8,9},{9,8},{10,11... | collective-permute-start | bytes 36872 | tf_op jit(solution)/shard_map/ppermute | solution.py:42
  31.5 3.2 %collective-permute-start.11 = (f32[24,128]{1,0:T(8,128)S(1)}, f32[24,128]{1,0:T(8,128)S(1)}, u32[]{:S(2)}, u32[]{:S(2)}) collective-permute-start(f32[24,128]{1,0:T(8,128)S(1)} %get-tuple-element.111), channel_id=1, source_target_pairs={{1,2},{2,1},{3,0},{0,3},{5,6},{6,5},{7,4},{4,7},{9,10},{10,9},{11,... | collective-permute-start | bytes 36872 | tf_op jit(solution)/shard_map/ppermute | solution.py:42
  38.4 5.8 %collective-permute-start.12 = (f32[96,128]{1,0:T(8,128)S(1)}, f32[96,128]{1,0:T(8,128)S(1)}, u32[]{:S(2)}, u32[]{:S(2)}) collective-permute-start(f32[96,128]{1,0:T(8,128)S(1)} %get-tuple-element.119), channel_id=1, source_target_pairs={{0,4},{4,0},{8,12},{12,8},{16,20},{20,16},{24,28},{28,24},{1,5},{5... | collective-permute-start | bytes 147464 | tf_op jit(solution)/shard_map/ppermute | solution.py:42
  38.5 5.7 %collective-permute-start.13 = (f32[96,128]{1,0:T(8,128)S(1)}, f32[96,128]{1,0:T(8,128)S(1)}, u32[]{:S(2)}, u32[]{:S(2)}) collective-permute-start(f32[96,128]{1,0:T(8,128)S(1)} %get-tuple-element.120), channel_id=1, source_target_pairs={{4,8},{8,4},{12,16},{16,12},{20,24},{24,20},{28,0},{0,28},{5,9},{9... | collective-permute-start | bytes 147464 | tf_op jit(solution)/shard_map/ppermute | solution.py:42
  40.4 3.8 %collective-permute-start.14 = (f32[96,128]{1,0:T(8,128)S(1)}, f32[96,128]{1,0:T(8,128)S(1)}, u32[]{:S(2)}, u32[]{:S(2)}) collective-permute-start(f32[96,128]{1,0:T(8,128)S(1)} %get-tuple-element.121), channel_id=1, source_target_pairs={{0,1},{1,0},{2,3},{3,2},{4,5},{5,4},{6,7},{7,6},{8,9},{9,8},{10,11... | collective-permute-start | bytes 147464 | tf_op jit(solution)/shard_map/ppermute | solution.py:42
  41.8 3.5 %collective-permute-start.15 = (f32[96,128]{1,0:T(8,128)S(1)}, f32[96,128]{1,0:T(8,128)S(1)}, u32[]{:S(2)}, u32[]{:S(2)}) collective-permute-start(f32[96,128]{1,0:T(8,128)S(1)} %get-tuple-element.122), channel_id=1, source_target_pairs={{1,2},{2,1},{3,0},{0,3},{5,6},{6,5},{7,4},{4,7},{9,10},{10,9},{11,... | collective-permute-start | bytes 147464 | tf_op jit(solution)/shard_map/ppermute | solution.py:42

commit v4 on v3

--- a/solution.py
+++ b/solution.py
@@ -312,7 +312,12 @@
             pieces.append(piece)
         columns.append(jnp.concatenate(pieces, axis=0))
     left = columns[0] if groups == 1 else jnp.concatenate(columns, axis=1)
-    return pick(left, far_ref[0 : groups * lanes, :])
+    chosen = far_ref[0 : groups * lanes, :]
+    if groups > 1:
+        return pick(left, chosen)
+    high, low = halves(left)
+    both = jnp.concatenate([high, low], axis=1).astype(BF16)
+    return jnp.dot(both, jnp.concatenate([chosen, chosen], axis=0), preferred_element_type=F32)
 
 
 def gather_faces(in_refs, groups, near_ref, far_ref, turn_ref, aplus_ref, c_ref, lanes):
@@ -419,6 +424,16 @@
     for group in range(1, count):
         picks[group] = picks[group] + held_ref[:, (group - 1) * lanes : group * lanes]
     fill_messages(picks, rest, lanes)
+
+
+def predict_send_kernel(packed_ref, cluster_ref, ck_ref, star_ref, proj_ref, send_ref, *rest, lanes, tick):
+    held = rest[:1] if tick % 2 else ()
+    i_ref, faces_ref, *outs = rest[len(held) : len(held) + 6]
+    weight_ref, m_ref = rest[len(held) + 6 :]
+    predict_kernel(
+        packed_ref, cluster_ref, ck_ref, star_ref, proj_ref, i_ref, faces_ref, weight_ref, m_ref, lanes=lanes, tick=tick
+    )
+    send_kernel(faces_ref, send_ref, *held, *outs, lanes=lanes, tick=tick)
 
 
 def prepare_kernel(
@@ -603,16 +618,12 @@
     orient = late[-1]
 
     def predicted(tick, packed, chosen, more):
-        integral, face_values = call(
-            functools.partial(predict_kernel, lanes=lanes, tick=tick),
-            [modal, faces],
+        integral, face_values, *messages = call(
+            functools.partial(predict_send_kernel, lanes=lanes, tick=tick),
+            [modal, faces] + message(GROUPS_AT[tick]),
             [weights, staged],
             f"predict{tick}", 400_000_000,
-            (packed, cluster_row, ck_left, star_pairs, proj_left),
-        )
-        messages = call(
-            functools.partial(send_kernel, lanes=lanes, tick=tick),
-            message(GROUPS_AT[tick]), [], f"send{tick}", 50_000_000, (face_values, chosen, *more),
+            (packed, cluster_row, ck_left, star_pairs, proj_left, chosen, *more),
         )
         return integral, face_values, messages
 

time: 47.9 us -> 47.5 us (level)
    pallas_call x18 -> x14, Pallas kernels: 23 us -> 22.6 us  [call(): pl.pallas_call(body, out_shape=outs, in_specs=[pl.BlockSpec(memory_space=...]
where the time goes in v4:
time: 47.5 us; the launch traced here: 47 us
  Pallas kernels  22.6 us (48%)
  starting transfers between devices  21.4 us (45%)
  waiting for transfers between devices  2.63 us (6%)
    pallas_call x14, Pallas kernels, call(): pl.pallas_call(body, out_shape=outs, in_specs=[pl.BlockSpec(memory_space=...  22.6 us
    ppermute x16, starting transfers between devices, exchange(): return lax.ppermute(x, axis, pairs)  21.4 us
    ppermute x16, waiting for transfers between devices, exchange(): return lax.ppermute(x, axis, pairs)  2.63 us
  transfers between devices with their start and end apart: 16, of which 4 were waited for; matrix products, arithmetic and copies ran while one was open for 0% of the time, Pallas kernels for 12%

profile of v4, /device:TPU:1, one launch (start us, length us, event | category | flops | bytes accessed | tf_op | source)
XLA Modules:
  0.0 47.0 jit_solution(6811950798617297128)
XLA Ops:
  0.0 1.6 %first.1 = (f32[56,640]{1,0:T(8,128)S(1)}, f32[45,3,128]{2,1,0:T(4,128)S(1)}, bf16[168,192]{1,0:T(8,128)(2,1)S(1)}, bf16[96,192]{1,0:T(8,128)(2,1)S(1)}, s32[4,1...) custom-call(f32[9,56,64]{2,1,0:T(8,128)} %state_hbm.1, ...), custom_call_target="tpu_custom_call" | custom-call | flops 10000000 | bytes 528812 | tf_op jit(solution)/shard_map/first/pallas_call | solution.py:558
  1.6 2.6 %predict0.1 = (f32[56,640]{1,0:T(8,128)S(1)}, f32[96,640]{1,0:T(8,128)S(1)}, f32[24,128]{1,0:T(8,128)S(1)}, f32[24,128]{1,0:T(8,128)S(1)}, f32[24,128]{1,0:T(8,128)S(1)}, /*index=5*/f32[24,128]{1,0:T(8,128)S(1)}) custom-call(f32[56,640]{1,0:T(8,128)S(1)} %get-tuple-element.66.packed_ref, s32[1,64]{1,0:T(1,128)S(1)} %get-tuple-element.67.cluster_ref, ...), custom_call_target="tpu_custom_call" | custom-call | flops 400000000 | bytes 316160 | tf_op jit(solution)/shard_map/predict0/pallas_call | solution.py:558
  4.2 2.1 %collective-permute-start = (f32[24,128]{1,0:T(8,128)S(1)}, f32[24,128]{1,0:T(8,128)S(1)}, u32[]{:S(2)}, u32[]{:S(2)}) collective-permute-start(f32[24,128]{1,0:T(8,128)S(1)} %get-tuple-element.72), channel_id=1, source_target_pairs={{0,4},{4,0},{8,12},{12,8},{16,20},{20,16},{24,28},{28,24},{1,5},{5... | collective-permute-start | bytes 36872 | tf_op jit(solution)/shard_map/ppermute | solution.py:42
  6.3 3.3 %collective-permute-start.1 = (f32[24,128]{1,0:T(8,128)S(1)}, f32[24,128]{1,0:T(8,128)S(1)}, u32[]{:S(2)}, u32[]{:S(2)}) collective-permute-start(f32[24,128]{1,0:T(8,128)S(1)} %get-tuple-element.73), channel_id=1, source_target_pairs={{4,8},{8,4},{12,16},{16,12},{20,24},{24,20},{28,0},{0,28},{5,9},{9... | collective-permute-start | bytes 36872 | tf_op jit(solution)/shard_map/ppermute | solution.py:42
  9.6 1.2 %collective-permute-start.2 = (f32[24,128]{1,0:T(8,128)S(1)}, f32[24,128]{1,0:T(8,128)S(1)}, u32[]{:S(2)}, u32[]{:S(2)}) collective-permute-start(f32[24,128]{1,0:T(8,128)S(1)} %get-tuple-element.74), channel_id=1, source_target_pairs={{0,1},{1,0},{2,3},{3,2},{4,5},{5,4},{6,7},{7,6},{8,9},{9,8},{10,11... | collective-permute-start | bytes 36872 | tf_op jit(solution)/shard_map/ppermute | solution.py:42
  10.9 1.1 %collective-permute-start.3 = (f32[24,128]{1,0:T(8,128)S(1)}, f32[24,128]{1,0:T(8,128)S(1)}, u32[]{:S(2)}, u32[]{:S(2)}) collective-permute-start(f32[24,128]{1,0:T(8,128)S(1)} %get-tuple-element.75), channel_id=1, source_target_pairs={{1,2},{2,1},{3,0},{0,3},{5,6},{6,5},{7,4},{4,7},{9,10},{10,9},{11,... | collective-permute-start | bytes 36872 | tf_op jit(solution)/shard_map/ppermute | solution.py:42
  12.0 0.6 %prepare.1 = (f32[45,7,128]{2,1,0:T(8,128)S(1)}, f32[81,2,128]{2,1,0:T(2,128)S(1)}, bf16[392,192]{1,0:T(8,128)(2,1)S(1)}, bf16[56,288]{1,0:T(8,128)(2,1)S(1)}, b...) custom-call(f32[9,9,3,64]{3,2,1,0:T(4,128)S(1)} %get-tuple-element.7, ...), custom_call_target="tpu_custom_call" | custom-call | flops 100000000 | bytes 344108 | tf_op jit(solution)/shard_map/prepare/pallas_call | solution.py:558
  12.6 1.3 %local0.1 = (f32[56,640]{1,0:T(8,128)S(1)}, f32[56,640]{1,0:T(8,128)S(1)}, f32[240,256]{1,0:T(8,128)S(1)}, f32[120,384]{1,0:T(8,128)S(1)}) custom-call(f32[56,640]{1,0:T(8,128)S(1)} %get-tuple-element.76.i_ref.own_ref, f32[56,640]{1,0:T(8,128)S(1)} %get-tuple-element.66.packed_ref, f32[96,640]{1,0:T(8,128)S(1)} %get-tuple-element.77.faces_ref, ...), custom_call_target="tpu_custom_call" | custom-call | flops 300000000 | bytes 1917952 | tf_op jit(solution)/shard_map/local0/pallas_call | solution.py:558
  13.9 0.0 collective-permute-done.r0
  13.9 0.0 collective-permute-done.1.r1
  13.9 0.0 collective-permute-done.2.r2
  13.9 0.1 collective-permute-done.3.r3
  14.0 0.8 %update0.1.packed_ref = f32[56,640]{1,0:T(8,128)S(1)} custom-call(f32[24,128]{1,0:T(8,128)S(1)} %collective-permute-done.r0, f32[24,128]{1,0:T(8,128)S(1)} %collective-permute-done.1.r1, f32[24,128]{1,0:T(8,128)S(1)} %collective-permute-done.2.r2, f32[24,128]{1,0:T(8,128)S(1)} %collective-permute-done.3.r3, ...), custom_call_target="tpu_custom_call" | custom-call | flops 100000000 | bytes 827392 | tf_op jit(solution)/shard_map/update0/pallas_call | solution.py:558
  14.8 2.6 %predict1.1 = (f32[56,640]{1,0:T(8,128)S(1)}, f32[96,640]{1,0:T(8,128)S(1)}, f32[48,128]{1,0:T(8,128)S(1)}, f32[48,128]{1,0:T(8,128)S(1)}, f32[48,128]{1,0:T(8,128)S(1)}, /*index=5*/f32[48,128]{1,0:T(8,128)S(1)}) custom-call(f32[56,640]{1,0:T(8,128)S(1)} %update0.1.packed_ref, s32[1,64]{1,0:T(1,128)S(1)} %get-tuple-element.67.cluster_ref, ...), custom_call_target="tpu_custom_call" | custom-call | flops 400000000 | bytes 1022720 | tf_op jit(solution)/shard_map/predict1/pallas_call | solution.py:558
  17.5 0.1 collective-permute-start.4
  17.5 1.6 %collective-permute-start.5 = (f32[48,128]{1,0:T(8,128)S(1)}, f32[48,128]{1,0:T(8,128)S(1)}, u32[]{:S(2)}, u32[]{:S(2)}) collective-permute-start(f32[48,128]{1,0:T(8,128)S(1)} %get-tuple-element.99), channel_id=1, source_target_pairs={{4,8},{8,4},{12,16},{16,12},{20,24},{24,20},{28,0},{0,28},{5,9},{9... | collective-permute-start | bytes 73736 | tf_op jit(solution)/shard_map/ppermute | solution.py:42
  19.2 1.7 %collective-permute-start.6 = (f32[48,128]{1,0:T(8,128)S(1)}, f32[48,128]{1,0:T(8,128)S(1)}, u32[]{:S(2)}, u32[]{:S(2)}) collective-permute-start(f32[48,128]{1,0:T(8,128)S(1)} %get-tuple-element.100), channel_id=1, source_target_pairs={{0,1},{1,0},{2,3},{3,2},{4,5},{5,4},{6,7},{7,6},{8,9},{9,8},{10,11... | collective-permute-start | bytes 73736 | tf_op jit(solution)/shard_map/ppermute | solution.py:42
  20.9 1.1 %collective-permute-start.7 = (f32[48,128]{1,0:T(8,128)S(1)}, f32[48,128]{1,0:T(8,128)S(1)}, u32[]{:S(2)}, u32[]{:S(2)}) collective-permute-start(f32[48,128]{1,0:T(8,128)S(1)} %get-tuple-element.101), channel_id=1, source_target_pairs={{1,2},{2,1},{3,0},{0,3},{5,6},{6,5},{7,4},{4,7},{9,10},{10,9},{11,... | collective-permute-start | bytes 73736 | tf_op jit(solution)/shard_map/ppermute | solution.py:42
  22.0 1.3 %local1.1 = (f32[56,640]{1,0:T(8,128)S(1)}, f32[56,640]{1,0:T(8,128)S(1)}, f32[240,256]{1,0:T(8,128)S(1)}, f32[120,384]{1,0:T(8,128)S(1)}) custom-call(f32[56,640]{1,0:T(8,128)S(1)} %get-tuple-element.102.i_ref, f32[56,640]{1,0:T(8,128)S(1)} %update0.1.packed_ref, f32[96,640]{1,0:T(8,128)S(1)} %get-tuple-element.103.faces_ref, ...), custom_call_target="tpu_custom_call" | custom-call | flops 300000000 | bytes 2085888 | tf_op jit(solution)/shard_map/local1/pallas_call | solution.py:558
  23.3 0.0 collective-permute-done.4.r0
  23.3 0.0 collective-permute-done.5.r1
  23.3 0.0 collective-permute-done.6.r2
  23.3 0.8 %collective-permute-done.7.r3 = f32[48,128]{1,0:T(8,128)S(1)} collective-permute-done((f32[48,128]{1,0:T(8,128)S(1)}, f32[48,128]{1,0:T(8,128)S(1)}, u32[]{:S(2)}, u32[]{:S(2)}) %collective-permute-start.7) | collective-permute-done | bytes 24608 | tf_op jit(solution)/shard_map/ppermute | solution.py:42
  24.2 1.0 %update1.1.packed_ref = f32[56,640]{1,0:T(8,128)S(1)} custom-call(f32[48,128]{1,0:T(8,128)S(1)} %collective-permute-done.4.r0, f32[48,128]{1,0:T(8,128)S(1)} %collective-permute-done.5.r1, f32[48,128]{1,0:T(8,128)S(1)} %collective-permute-done.6.r2, f32[48,128]{1,0:T(8,128)S(1)} %collective-permute-done.7.r3, ...), custom_call_target="tpu_custom_call" | custom-call | flops 100000000 | bytes 876544 | tf_op jit(solution)/shard_map/update1/pallas_call | solution.py:558
  25.2 2.6 %predict2.1 = (f32[56,640]{1,0:T(8,128)S(1)}, f32[96,640]{1,0:T(8,128)S(1)}, f32[24,128]{1,0:T(8,128)S(1)}, f32[24,128]{1,0:T(8,128)S(1)}, f32[24,128]{1,0:T(8,128)S(1)}, /*index=5*/f32[24,128]{1,0:T(8,128)S(1)}) custom-call(f32[56,640]{1,0:T(8,128)S(1)} %update1.1.packed_ref, s32[1,64]{1,0:T(1,128)S(1)} %get-tuple-element.67.cluster_ref, ...), custom_call_target="tpu_custom_call" | custom-call | flops 400000000 | bytes 838400 | tf_op jit(solution)/shard_map/predict2/pallas_call | solution.py:558
  27.8 0.1 collective-permute-start.8
  27.9 1.9 %collective-permute-start.9 = (f32[24,128]{1,0:T(8,128)S(1)}, f32[24,128]{1,0:T(8,128)S(1)}, u32[]{:S(2)}, u32[]{:S(2)}) collective-permute-start(f32[24,128]{1,0:T(8,128)S(1)} %get-tuple-element.108), channel_id=1, source_target_pairs={{4,8},{8,4},{12,16},{16,12},{20,24},{24,20},{28,0},{0,28},{5,9},{9... | collective-permute-start | bytes 36872 | tf_op jit(solution)/shard_map/ppermute | solution.py:42
  29.8 1.5 %collective-permute-start.10 = (f32[24,128]{1,0:T(8,128)S(1)}, f32[24,128]{1,0:T(8,128)S(1)}, u32[]{:S(2)}, u32[]{:S(2)}) collective-permute-start(f32[24,128]{1,0:T(8,128)S(1)} %get-tuple-element.109), channel_id=1, source_target_pairs={{0,1},{1,0},{2,3},{3,2},{4,5},{5,4},{6,7},{7,6},{8,9},{9,8},{10,11... | collective-permute-start | bytes 36872 | tf_op jit(solution)/shard_map/ppermute | solution.py:42
  31.3 1.1 %collective-permute-start.11 = (f32[24,128]{1,0:T(8,128)S(1)}, f32[24,128]{1,0:T(8,128)S(1)}, u32[]{:S(2)}, u32[]{:S(2)}) collective-permute-start(f32[24,128]{1,0:T(8,128)S(1)} %get-tuple-element.110), channel_id=1, source_target_pairs={{1,2},{2,1},{3,0},{0,3},{5,6},{6,5},{7,4},{4,7},{9,10},{10,9},{11,... | collective-permute-start | bytes 36872 | tf_op jit(solution)/shard_map/ppermute | solution.py:42
  32.4 1.5 %local2.1 = (f32[56,640]{1,0:T(8,128)S(1)}, f32[56,640]{1,0:T(8,128)S(1)}, f32[240,256]{1,0:T(8,128)S(1)}, f32[120,384]{1,0:T(8,128)S(1)}) custom-call(f32[56,640]{1,0:T(8,128)S(1)} %get-tuple-element.111.i_ref, f32[56,640]{1,0:T(8,128)S(1)} %update1.1.packed_ref, f32[96,640]{1,0:T(8,128)S(1)} %get-tuple-element.112.faces_ref, ...), custom_call_target="tpu_custom_call" | custom-call | flops 300000000 | bytes 2085888 | tf_op jit(solution)/shard_map/local2/pallas_call | solution.py:558
  33.9 0.0 collective-permute-done.8.r0
  33.9 0.0 collective-permute-done.9.r1
  33.9 0.0 collective-permute-done.10.r2
  33.9 0.5 %collective-permute-done.11.r3 = f32[24,128]{1,0:T(8,128)S(1)} collective-permute-done((f32[24,128]{1,0:T(8,128)S(1)}, f32[24,128]{1,0:T(8,128)S(1)}, u32[]{:S(2)}, u32[]{:S(2)}) %collective-permute-start.11) | collective-permute-done | bytes 12320 | tf_op jit(solution)/shard_map/ppermute | solution.py:42
  34.4 0.8 %update2.1.packed_ref = f32[56,640]{1,0:T(8,128)S(1)} custom-call(f32[24,128]{1,0:T(8,128)S(1)} %collective-permute-done.8.r0, f32[24,128]{1,0:T(8,128)S(1)} %collective-permute-done.9.r1, f32[24,128]{1,0:T(8,128)S(1)} %collective-permute-done.10.r2, f32[24,128]{1,0:T(8,128)S(1)} %collective-permute-done.11.r3, ...), custom_call_target="tpu_custom_call" | custom-call | flops 100000000 | bytes 827392 | tf_op jit(solution)/shard_map/update2/pallas_call | solution.py:558
  35.3 2.8 %predict3.1 = (f32[56,640]{1,0:T(8,128)S(1)}, f32[96,640]{1,0:T(8,128)S(1)}, f32[96,128]{1,0:T(8,128)S(1)}, f32[96,128]{1,0:T(8,128)S(1)}, f32[96,128]{1,0:T(8,128)S(1)}, /*index=5*/f32[96,128]{1,0:T(8,128)S(1)}) custom-call(f32[56,640]{1,0:T(8,128)S(1)} %update2.1.packed_ref, s32[1,64]{1,0:T(1,128)S(1)} %get-tuple-element.67.cluster_ref, ...), custom_call_target="tpu_custom_call" | custom-call | flops 400000000 | bytes 1022720 | tf_op jit(solution)/shard_map/predict3/pallas_call | solution.py:558
  38.0 0.1 collective-permute-start.12
  38.1 1.9 %collective-permute-start.13 = (f32[96,128]{1,0:T(8,128)S(1)}, f32[96,128]{1,0:T(8,128)S(1)}, u32[]{:S(2)}, u32[]{:S(2)}) collective-permute-start(f32[96,128]{1,0:T(8,128)S(1)} %get-tuple-element.119), channel_id=1, source_target_pairs={{4,8},{8,4},{12,16},{16,12},{20,24},{24,20},{28,0},{0,28},{5,9},{9... | collective-permute-start | bytes 147464 | tf_op jit(solution)/shard_map/ppermute | solution.py:42
  40.0 1.4 %collective-permute-start.14 = (f32[96,128]{1,0:T(8,128)S(1)}, f32[96,128]{1,0:T(8,128)S(1)}, u32[]{:S(2)}, u32[]{:S(2)}) collective-permute-start(f32[96,128]{1,0:T(8,128)S(1)} %get-tuple-element.120), channel_id=1, source_target_pairs={{0,1},{1,0},{2,3},{3,2},{4,5},{5,4},{6,7},{7,6},{8,9},{9,8},{10,11... | collective-permute-start | bytes 147464 | tf_op jit(solution)/shard_map/ppermute | solution.py:42
  41.4 1.1 %collective-permute-start.15 = (f32[96,128]{1,0:T(8,128)S(1)}, f32[96,128]{1,0:T(8,128)S(1)}, u32[]{:S(2)}, u32[]{:S(2)}) collective-permute-start(f32[96,128]{1,0:T(8,128)S(1)} %get-tuple-element.121), channel_id=1, source_target_pairs={{1,2},{2,1},{3,0},{0,3},{5,6},{6,5},{7,4},{4,7},{9,10},{10,9},{11,... | collective-permute-start | bytes 147464 | tf_op jit(solution)/shard_map/ppermute | solution.py:42
  42.6 1.2 %local3.1 = (f32[56,640]{1,0:T(8,128)S(1)}, f32[56,640]{1,0:T(8,128)}, f32[240,256]{1,0:T(8,128)S(1)}) custom-call(f32[56,640]{1,0:T(8,128)S(1)} %get-tuple-element.122.i_ref, f32[56,640]{1,0:T(8,128)S(1)} %update2.1.packed_ref, f32[96,640]{1,0:T(8,128)S(1)} %get-tuple-element.123.faces_ref, s32[1,64]{1,0:T(1,128)S(1)} %get-tuple-element.67.cluster_ref, ...), custom_call_target="tpu_custom_call" | custom-call | flops 300000000 | bytes 2085888 | tf_op jit(solution)/shard_map/local3/pallas_call | solution.py:558
  43.8 0.0 collective-permute-done.12.r0
  43.8 0.0 collective-permute-done.13.r1
  43.8 0.0 collective-permute-done.14.r2
  43.8 1.1 %collective-permute-done.15.r3 = f32[96,128]{1,0:T(8,128)S(1)} collective-permute-done((f32[96,128]{1,0:T(8,128)S(1)}, f32[96,128]{1,0:T(8,128)S(1)}, u32[]{:S(2)}, u32[]{:S(2)}) %collective-permute-start.15) | collective-permute-done | bytes 49184 | tf_op jit(solution)/shard_map/ppermute | solution.py:42
  45.0 1.9 %last.1 = f32[9,56,64]{2,1,0:T(8,128)} custom-call(f32[96,128]{1,0:T(8,128)S(1)} %collective-permute-done.12.r0, f32[96,128]{1,0:T(8,128)S(1)} %collective-permute-done.13.r1, f32[96,128]{1,0:T(8,128)S(1)} %collective-permute-done.14.r2, f32[96,128]{1,0:T(8,128)S(1)} %collective-permute-done.15.r3, f32[240,256]{1,0:T(8,128)S(1)} %get-tuple-element.125.near_ref, ...), custom_call_target="tpu_custom_call" | custom-call | flops 100000000 | bytes 974848 | tf_op jit(solution)/shard_map/last/pallas_call | solution.py:558
Async XLA Ops:
  4.2 9.6 %collective-permute-start = (f32[24,128]{1,0:T(8,128)S(1)}, f32[24,128]{1,0:T(8,128)S(1)}, u32[]{:S(2)}, u32[]{:S(2)}) collective-permute-start(f32[24,128]{1,0:T(8,128)S(1)} %get-tuple-element.72), channel_id=1, source_target_pairs={{0,4},{4,0},{8,12},{12,8},{16,20},{20,16},{24,28},{28,24},{1,5},{5... | collective-permute-start | bytes 36872 | tf_op jit(solution)/shard_map/ppermute | solution.py:42
  6.3 7.6 %collective-permute-start.1 = (f32[24,128]{1,0:T(8,128)S(1)}, f32[24,128]{1,0:T(8,128)S(1)}, u32[]{:S(2)}, u32[]{:S(2)}) collective-permute-start(f32[24,128]{1,0:T(8,128)S(1)} %get-tuple-element.73), channel_id=1, source_target_pairs={{4,8},{8,4},{12,16},{16,12},{20,24},{24,20},{28,0},{0,28},{5,9},{9... | collective-permute-start | bytes 36872 | tf_op jit(solution)/shard_map/ppermute | solution.py:42
  9.6 4.3 %collective-permute-start.2 = (f32[24,128]{1,0:T(8,128)S(1)}, f32[24,128]{1,0:T(8,128)S(1)}, u32[]{:S(2)}, u32[]{:S(2)}) collective-permute-start(f32[24,128]{1,0:T(8,128)S(1)} %get-tuple-element.74), channel_id=1, source_target_pairs={{0,1},{1,0},{2,3},{3,2},{4,5},{5,4},{6,7},{7,6},{8,9},{9,8},{10,11... | collective-permute-start | bytes 36872 | tf_op jit(solution)/shard_map/ppermute | solution.py:42
  10.9 3.1 %collective-permute-start.3 = (f32[24,128]{1,0:T(8,128)S(1)}, f32[24,128]{1,0:T(8,128)S(1)}, u32[]{:S(2)}, u32[]{:S(2)}) collective-permute-start(f32[24,128]{1,0:T(8,128)S(1)} %get-tuple-element.75), channel_id=1, source_target_pairs={{1,2},{2,1},{3,0},{0,3},{5,6},{6,5},{7,4},{4,7},{9,10},{10,9},{11,... | collective-permute-start | bytes 36872 | tf_op jit(solution)/shard_map/ppermute | solution.py:42
  17.5 5.8 %collective-permute-start.4 = (f32[48,128]{1,0:T(8,128)S(1)}, f32[48,128]{1,0:T(8,128)S(1)}, u32[]{:S(2)}, u32[]{:S(2)}) collective-permute-start(f32[48,128]{1,0:T(8,128)S(1)} %get-tuple-element.98), channel_id=1, source_target_pairs={{0,4},{4,0},{8,12},{12,8},{16,20},{20,16},{24,28},{28,24},{1,5},{5... | collective-permute-start | bytes 73736 | tf_op jit(solution)/shard_map/ppermute | solution.py:42
  17.5 5.8 %collective-permute-start.5 = (f32[48,128]{1,0:T(8,128)S(1)}, f32[48,128]{1,0:T(8,128)S(1)}, u32[]{:S(2)}, u32[]{:S(2)}) collective-permute-start(f32[48,128]{1,0:T(8,128)S(1)} %get-tuple-element.99), channel_id=1, source_target_pairs={{4,8},{8,4},{12,16},{16,12},{20,24},{24,20},{28,0},{0,28},{5,9},{9... | collective-permute-start | bytes 73736 | tf_op jit(solution)/shard_map/ppermute | solution.py:42
  19.2 4.2 %collective-permute-start.6 = (f32[48,128]{1,0:T(8,128)S(1)}, f32[48,128]{1,0:T(8,128)S(1)}, u32[]{:S(2)}, u32[]{:S(2)}) collective-permute-start(f32[48,128]{1,0:T(8,128)S(1)} %get-tuple-element.100), channel_id=1, source_target_pairs={{0,1},{1,0},{2,3},{3,2},{4,5},{5,4},{6,7},{7,6},{8,9},{9,8},{10,11... | collective-permute-start | bytes 73736 | tf_op jit(solution)/shard_map/ppermute | solution.py:42
  20.9 3.3 %collective-permute-start.7 = (f32[48,128]{1,0:T(8,128)S(1)}, f32[48,128]{1,0:T(8,128)S(1)}, u32[]{:S(2)}, u32[]{:S(2)}) collective-permute-start(f32[48,128]{1,0:T(8,128)S(1)} %get-tuple-element.101), channel_id=1, source_target_pairs={{1,2},{2,1},{3,0},{0,3},{5,6},{6,5},{7,4},{4,7},{9,10},{10,9},{11,... | collective-permute-start | bytes 73736 | tf_op jit(solution)/shard_map/ppermute | solution.py:42
  27.8 6.1 %collective-permute-start.8 = (f32[24,128]{1,0:T(8,128)S(1)}, f32[24,128]{1,0:T(8,128)S(1)}, u32[]{:S(2)}, u32[]{:S(2)}) collective-permute-start(f32[24,128]{1,0:T(8,128)S(1)} %get-tuple-element.107), channel_id=1, source_target_pairs={{0,4},{4,0},{8,12},{12,8},{16,20},{20,16},{24,28},{28,24},{1,5},{5... | collective-permute-start | bytes 36872 | tf_op jit(solution)/shard_map/ppermute | solution.py:42
  27.9 6.0 %collective-permute-start.9 = (f32[24,128]{1,0:T(8,128)S(1)}, f32[24,128]{1,0:T(8,128)S(1)}, u32[]{:S(2)}, u32[]{:S(2)}) collective-permute-start(f32[24,128]{1,0:T(8,128)S(1)} %get-tuple-element.108), channel_id=1, source_target_pairs={{4,8},{8,4},{12,16},{16,12},{20,24},{24,20},{28,0},{0,28},{5,9},{9... | collective-permute-start | bytes 36872 | tf_op jit(solution)/shard_map/ppermute | solution.py:42
  29.8 4.1 %collective-permute-start.10 = (f32[24,128]{1,0:T(8,128)S(1)}, f32[24,128]{1,0:T(8,128)S(1)}, u32[]{:S(2)}, u32[]{:S(2)}) collective-permute-start(f32[24,128]{1,0:T(8,128)S(1)} %get-tuple-element.109), channel_id=1, source_target_pairs={{0,1},{1,0},{2,3},{3,2},{4,5},{5,4},{6,7},{7,6},{8,9},{9,8},{10,11... | collective-permute-start | bytes 36872 | tf_op jit(solution)/shard_map/ppermute | solution.py:42
  31.3 3.2 %collective-permute-start.11 = (f32[24,128]{1,0:T(8,128)S(1)}, f32[24,128]{1,0:T(8,128)S(1)}, u32[]{:S(2)}, u32[]{:S(2)}) collective-permute-start(f32[24,128]{1,0:T(8,128)S(1)} %get-tuple-element.110), channel_id=1, source_target_pairs={{1,2},{2,1},{3,0},{0,3},{5,6},{6,5},{7,4},{4,7},{9,10},{10,9},{11,... | collective-permute-start | bytes 36872 | tf_op jit(solution)/shard_map/ppermute | solution.py:42
  38.0 5.7 %collective-permute-start.12 = (f32[96,128]{1,0:T(8,128)S(1)}, f32[96,128]{1,0:T(8,128)S(1)}, u32[]{:S(2)}, u32[]{:S(2)}) collective-permute-start(f32[96,128]{1,0:T(8,128)S(1)} %get-tuple-element.118), channel_id=1, source_target_pairs={{0,4},{4,0},{8,12},{12,8},{16,20},{20,16},{24,28},{28,24},{1,5},{5... | collective-permute-start | bytes 147464 | tf_op jit(solution)/shard_map/ppermute | solution.py:42
  38.1 5.7 %collective-permute-start.13 = (f32[96,128]{1,0:T(8,128)S(1)}, f32[96,128]{1,0:T(8,128)S(1)}, u32[]{:S(2)}, u32[]{:S(2)}) collective-permute-start(f32[96,128]{1,0:T(8,128)S(1)} %get-tuple-element.119), channel_id=1, source_target_pairs={{4,8},{8,4},{12,16},{16,12},{20,24},{24,20},{28,0},{0,28},{5,9},{9... | collective-permute-start | bytes 147464 | tf_op jit(solution)/shard_map/ppermute | solution.py:42
  40.0 3.8 %collective-permute-start.14 = (f32[96,128]{1,0:T(8,128)S(1)}, f32[96,128]{1,0:T(8,128)S(1)}, u32[]{:S(2)}, u32[]{:S(2)}) collective-permute-start(f32[96,128]{1,0:T(8,128)S(1)} %get-tuple-element.120), channel_id=1, source_target_pairs={{0,1},{1,0},{2,3},{3,2},{4,5},{5,4},{6,7},{7,6},{8,9},{9,8},{10,11... | collective-permute-start | bytes 147464 | tf_op jit(solution)/shard_map/ppermute | solution.py:42
  41.4 3.5 %collective-permute-start.15 = (f32[96,128]{1,0:T(8,128)S(1)}, f32[96,128]{1,0:T(8,128)S(1)}, u32[]{:S(2)}, u32[]{:S(2)}) collective-permute-start(f32[96,128]{1,0:T(8,128)S(1)} %get-tuple-element.121), channel_id=1, source_target_pairs={{1,2},{2,1},{3,0},{0,3},{5,6},{6,5},{7,4},{4,7},{9,10},{10,9},{11,... | collective-permute-start | bytes 147464 | tf_op jit(solution)/shard_map/ppermute | solution.py:42

commit v5 on v4

--- a/solution.py
+++ b/solution.py
@@ -301,15 +301,24 @@
     columns = []
     for group in range(groups):
         pieces = []
-        for f in range(FIELDS):
-            at = (3 * group + f // 4) * lanes
-            piece = None
-            for which in (2, 1, 0):
-                moved = turned[which * FACE_UP : (which + 1) * FACE_UP, at : at + lanes]
-                shift = ((which - f % 4) * 4 * SLOT) % lanes
-                moved = pltpu.roll(moved, shift, 1) if shift else moved
-                piece = moved if piece is None else jnp.where(column == which, moved, piece)
-            pieces.append(piece)
+        for quad in range(3):
+            at = (3 * group + quad) * lanes
+            sides = [turned[which * FACE_UP : (which + 1) * FACE_UP, at : at + lanes] for which in range(3)]
+            count = min(4, FIELDS - 4 * quad)
+            moved = []
+            for by in range(4 if count > 1 else 3):
+                if count > 1:
+                    source = sides[2]
+                    for which in range(2):
+                        source = jnp.where(column == (which - by) % 4, sides[which], source)
+                else:
+                    source = sides[by]
+                moved.append(pltpu.roll(source, by * 4 * SLOT, 1) if by else source)
+            for c in range(count):
+                piece = moved[(2 - c) % 4]
+                for which in range(2):
+                    piece = jnp.where(column == which, moved[(which - c) % 4], piece)
+                pieces.append(piece)
         columns.append(jnp.concatenate(pieces, axis=0))
     left = columns[0] if groups == 1 else jnp.concatenate(columns, axis=1)
     chosen = far_ref[0 : groups * lanes, :]

time: 47.5 us -> 47.4 us (level)
  no operation moved by 1% of the time
where the time goes in v5:
time: 47.4 us; the launch traced here: 46.8 us
  Pallas kernels  22.4 us (47%)
  starting transfers between devices  21.4 us (45%)
  waiting for transfers between devices  2.65 us (6%)
    pallas_call x14, Pallas kernels, call(): pl.pallas_call(body, out_shape=outs, in_specs=[pl.BlockSpec(memory_space=...  22.4 us
    ppermute x16, starting transfers between devices, exchange(): return lax.ppermute(x, axis, pairs)  21.4 us
    ppermute x16, waiting for transfers between devices, exchange(): return lax.ppermute(x, axis, pairs)  2.65 us
  transfers between devices with their start and end apart: 16, of which 4 were waited for; matrix products, arithmetic and copies ran while one was open for 0% of the time, Pallas kernels for 12%

profile of v5, /device:TPU:1, one launch (start us, length us, event | category | flops | bytes accessed | tf_op | source)
XLA Modules:
  0.0 46.8 jit_solution(6558953046218480326)
XLA Ops:
  0.0 1.6 %first.1 = (f32[56,640]{1,0:T(8,128)S(1)}, f32[45,3,128]{2,1,0:T(4,128)S(1)}, bf16[168,192]{1,0:T(8,128)(2,1)S(1)}, bf16[96,192]{1,0:T(8,128)(2,1)S(1)}, s32[4,1...) custom-call(f32[9,56,64]{2,1,0:T(8,128)} %state_hbm.1, ...), custom_call_target="tpu_custom_call" | custom-call | flops 10000000 | bytes 528812 | tf_op jit(solution)/shard_map/first/pallas_call | solution.py:567
  1.6 2.6 %predict0.1 = (f32[56,640]{1,0:T(8,128)S(1)}, f32[96,640]{1,0:T(8,128)S(1)}, f32[24,128]{1,0:T(8,128)S(1)}, f32[24,128]{1,0:T(8,128)S(1)}, f32[24,128]{1,0:T(8,128)S(1)}, /*index=5*/f32[24,128]{1,0:T(8,128)S(1)}) custom-call(f32[56,640]{1,0:T(8,128)S(1)} %get-tuple-element.66.packed_ref, s32[1,64]{1,0:T(1,128)S(1)} %get-tuple-element.67.cluster_ref, ...), custom_call_target="tpu_custom_call" | custom-call | flops 400000000 | bytes 316160 | tf_op jit(solution)/shard_map/predict0/pallas_call | solution.py:567
  4.2 2.1 %collective-permute-start = (f32[24,128]{1,0:T(8,128)S(1)}, f32[24,128]{1,0:T(8,128)S(1)}, u32[]{:S(2)}, u32[]{:S(2)}) collective-permute-start(f32[24,128]{1,0:T(8,128)S(1)} %get-tuple-element.72), channel_id=1, source_target_pairs={{0,4},{4,0},{8,12},{12,8},{16,20},{20,16},{24,28},{28,24},{1,5},{5... | collective-permute-start | bytes 36872 | tf_op jit(solution)/shard_map/ppermute | solution.py:42
  6.3 3.3 %collective-permute-start.1 = (f32[24,128]{1,0:T(8,128)S(1)}, f32[24,128]{1,0:T(8,128)S(1)}, u32[]{:S(2)}, u32[]{:S(2)}) collective-permute-start(f32[24,128]{1,0:T(8,128)S(1)} %get-tuple-element.73), channel_id=1, source_target_pairs={{4,8},{8,4},{12,16},{16,12},{20,24},{24,20},{28,0},{0,28},{5,9},{9... | collective-permute-start | bytes 36872 | tf_op jit(solution)/shard_map/ppermute | solution.py:42
  9.6 1.2 %collective-permute-start.2 = (f32[24,128]{1,0:T(8,128)S(1)}, f32[24,128]{1,0:T(8,128)S(1)}, u32[]{:S(2)}, u32[]{:S(2)}) collective-permute-start(f32[24,128]{1,0:T(8,128)S(1)} %get-tuple-element.74), channel_id=1, source_target_pairs={{0,1},{1,0},{2,3},{3,2},{4,5},{5,4},{6,7},{7,6},{8,9},{9,8},{10,11... | collective-permute-start | bytes 36872 | tf_op jit(solution)/shard_map/ppermute | solution.py:42
  10.9 1.1 %collective-permute-start.3 = (f32[24,128]{1,0:T(8,128)S(1)}, f32[24,128]{1,0:T(8,128)S(1)}, u32[]{:S(2)}, u32[]{:S(2)}) collective-permute-start(f32[24,128]{1,0:T(8,128)S(1)} %get-tuple-element.75), channel_id=1, source_target_pairs={{1,2},{2,1},{3,0},{0,3},{5,6},{6,5},{7,4},{4,7},{9,10},{10,9},{11,... | collective-permute-start | bytes 36872 | tf_op jit(solution)/shard_map/ppermute | solution.py:42
  12.0 0.6 %prepare.1 = (f32[45,7,128]{2,1,0:T(8,128)S(1)}, f32[81,2,128]{2,1,0:T(2,128)S(1)}, bf16[392,192]{1,0:T(8,128)(2,1)S(1)}, bf16[56,288]{1,0:T(8,128)(2,1)S(1)}, b...) custom-call(f32[9,9,3,64]{3,2,1,0:T(4,128)S(1)} %get-tuple-element.7, ...), custom_call_target="tpu_custom_call" | custom-call | flops 100000000 | bytes 344108 | tf_op jit(solution)/shard_map/prepare/pallas_call | solution.py:567
  12.6 1.3 %local0.1 = (f32[56,640]{1,0:T(8,128)S(1)}, f32[56,640]{1,0:T(8,128)S(1)}, f32[240,256]{1,0:T(8,128)S(1)}, f32[120,384]{1,0:T(8,128)S(1)}) custom-call(f32[56,640]{1,0:T(8,128)S(1)} %get-tuple-element.76.i_ref.own_ref, f32[56,640]{1,0:T(8,128)S(1)} %get-tuple-element.66.packed_ref, f32[96,640]{1,0:T(8,128)S(1)} %get-tuple-element.77.faces_ref, ...), custom_call_target="tpu_custom_call" | custom-call | flops 300000000 | bytes 1917952 | tf_op jit(solution)/shard_map/local0/pallas_call | solution.py:567
  13.9 0.0 collective-permute-done.r0
  13.9 0.0 collective-permute-done.1.r1
  13.9 0.0 collective-permute-done.2.r2
  13.9 0.1 collective-permute-done.3.r3
  14.0 0.8 %update0.1.packed_ref = f32[56,640]{1,0:T(8,128)S(1)} custom-call(f32[24,128]{1,0:T(8,128)S(1)} %collective-permute-done.r0, f32[24,128]{1,0:T(8,128)S(1)} %collective-permute-done.1.r1, f32[24,128]{1,0:T(8,128)S(1)} %collective-permute-done.2.r2, f32[24,128]{1,0:T(8,128)S(1)} %collective-permute-done.3.r3, ...), custom_call_target="tpu_custom_call" | custom-call | flops 100000000 | bytes 827392 | tf_op jit(solution)/shard_map/update0/pallas_call | solution.py:567
  14.8 2.6 %predict1.1 = (f32[56,640]{1,0:T(8,128)S(1)}, f32[96,640]{1,0:T(8,128)S(1)}, f32[48,128]{1,0:T(8,128)S(1)}, f32[48,128]{1,0:T(8,128)S(1)}, f32[48,128]{1,0:T(8,128)S(1)}, /*index=5*/f32[48,128]{1,0:T(8,128)S(1)}) custom-call(f32[56,640]{1,0:T(8,128)S(1)} %update0.1.packed_ref, s32[1,64]{1,0:T(1,128)S(1)} %get-tuple-element.67.cluster_ref, ...), custom_call_target="tpu_custom_call" | custom-call | flops 400000000 | bytes 1022720 | tf_op jit(solution)/shard_map/predict1/pallas_call | solution.py:567
  17.5 0.1 collective-permute-start.4
  17.5 1.6 %collective-permute-start.5 = (f32[48,128]{1,0:T(8,128)S(1)}, f32[48,128]{1,0:T(8,128)S(1)}, u32[]{:S(2)}, u32[]{:S(2)}) collective-permute-start(f32[48,128]{1,0:T(8,128)S(1)} %get-tuple-element.99), channel_id=1, source_target_pairs={{4,8},{8,4},{12,16},{16,12},{20,24},{24,20},{28,0},{0,28},{5,9},{9... | collective-permute-start | bytes 73736 | tf_op jit(solution)/shard_map/ppermute | solution.py:42
  19.2 1.7 %collective-permute-start.6 = (f32[48,128]{1,0:T(8,128)S(1)}, f32[48,128]{1,0:T(8,128)S(1)}, u32[]{:S(2)}, u32[]{:S(2)}) collective-permute-start(f32[48,128]{1,0:T(8,128)S(1)} %get-tuple-element.100), channel_id=1, source_target_pairs={{0,1},{1,0},{2,3},{3,2},{4,5},{5,4},{6,7},{7,6},{8,9},{9,8},{10,11... | collective-permute-start | bytes 73736 | tf_op jit(solution)/shard_map/ppermute | solution.py:42
  20.9 1.1 %collective-permute-start.7 = (f32[48,128]{1,0:T(8,128)S(1)}, f32[48,128]{1,0:T(8,128)S(1)}, u32[]{:S(2)}, u32[]{:S(2)}) collective-permute-start(f32[48,128]{1,0:T(8,128)S(1)} %get-tuple-element.101), channel_id=1, source_target_pairs={{1,2},{2,1},{3,0},{0,3},{5,6},{6,5},{7,4},{4,7},{9,10},{10,9},{11,... | collective-permute-start | bytes 73736 | tf_op jit(solution)/shard_map/ppermute | solution.py:42
  22.0 1.3 %local1.1 = (f32[56,640]{1,0:T(8,128)S(1)}, f32[56,640]{1,0:T(8,128)S(1)}, f32[240,256]{1,0:T(8,128)S(1)}, f32[120,384]{1,0:T(8,128)S(1)}) custom-call(f32[56,640]{1,0:T(8,128)S(1)} %get-tuple-element.102.i_ref, f32[56,640]{1,0:T(8,128)S(1)} %update0.1.packed_ref, f32[96,640]{1,0:T(8,128)S(1)} %get-tuple-element.103.faces_ref, ...), custom_call_target="tpu_custom_call" | custom-call | flops 300000000 | bytes 2085888 | tf_op jit(solution)/shard_map/local1/pallas_call | solution.py:567
  23.3 0.0 collective-permute-done.4.r0
  23.3 0.0 collective-permute-done.5.r1
  23.3 0.0 collective-permute-done.6.r2
  23.3 0.8 %collective-permute-done.7.r3 = f32[48,128]{1,0:T(8,128)S(1)} collective-permute-done((f32[48,128]{1,0:T(8,128)S(1)}, f32[48,128]{1,0:T(8,128)S(1)}, u32[]{:S(2)}, u32[]{:S(2)}) %collective-permute-start.7) | collective-permute-done | bytes 24608 | tf_op jit(solution)/shard_map/ppermute | solution.py:42
  24.2 0.9 %update1.1.packed_ref = f32[56,640]{1,0:T(8,128)S(1)} custom-call(f32[48,128]{1,0:T(8,128)S(1)} %collective-permute-done.4.r0, f32[48,128]{1,0:T(8,128)S(1)} %collective-permute-done.5.r1, f32[48,128]{1,0:T(8,128)S(1)} %collective-permute-done.6.r2, f32[48,128]{1,0:T(8,128)S(1)} %collective-permute-done.7.r3, ...), custom_call_target="tpu_custom_call" | custom-call | flops 100000000 | bytes 876544 | tf_op jit(solution)/shard_map/update1/pallas_call | solution.py:567
  25.1 2.6 %predict2.1 = (f32[56,640]{1,0:T(8,128)S(1)}, f32[96,640]{1,0:T(8,128)S(1)}, f32[24,128]{1,0:T(8,128)S(1)}, f32[24,128]{1,0:T(8,128)S(1)}, f32[24,128]{1,0:T(8,128)S(1)}, /*index=5*/f32[24,128]{1,0:T(8,128)S(1)}) custom-call(f32[56,640]{1,0:T(8,128)S(1)} %update1.1.packed_ref, s32[1,64]{1,0:T(1,128)S(1)} %get-tuple-element.67.cluster_ref, ...), custom_call_target="tpu_custom_call" | custom-call | flops 400000000 | bytes 838400 | tf_op jit(solution)/shard_map/predict2/pallas_call | solution.py:567
  27.7 0.1 collective-permute-start.8
  27.8 1.9 %collective-permute-start.9 = (f32[24,128]{1,0:T(8,128)S(1)}, f32[24,128]{1,0:T(8,128)S(1)}, u32[]{:S(2)}, u32[]{:S(2)}) collective-permute-start(f32[24,128]{1,0:T(8,128)S(1)} %get-tuple-element.108), channel_id=1, source_target_pairs={{4,8},{8,4},{12,16},{16,12},{20,24},{24,20},{28,0},{0,28},{5,9},{9... | collective-permute-start | bytes 36872 | tf_op jit(solution)/shard_map/ppermute | solution.py:42
  29.8 1.5 %collective-permute-start.10 = (f32[24,128]{1,0:T(8,128)S(1)}, f32[24,128]{1,0:T(8,128)S(1)}, u32[]{:S(2)}, u32[]{:S(2)}) collective-permute-start(f32[24,128]{1,0:T(8,128)S(1)} %get-tuple-element.109), channel_id=1, source_target_pairs={{0,1},{1,0},{2,3},{3,2},{4,5},{5,4},{6,7},{7,6},{8,9},{9,8},{10,11... | collective-permute-start | bytes 36872 | tf_op jit(solution)/shard_map/ppermute | solution.py:42
  31.2 1.1 %collective-permute-start.11 = (f32[24,128]{1,0:T(8,128)S(1)}, f32[24,128]{1,0:T(8,128)S(1)}, u32[]{:S(2)}, u32[]{:S(2)}) collective-permute-start(f32[24,128]{1,0:T(8,128)S(1)} %get-tuple-element.110), channel_id=1, source_target_pairs={{1,2},{2,1},{3,0},{0,3},{5,6},{6,5},{7,4},{4,7},{9,10},{10,9},{11,... | collective-permute-start | bytes 36872 | tf_op jit(solution)/shard_map/ppermute | solution.py:42
  32.3 1.5 %local2.1 = (f32[56,640]{1,0:T(8,128)S(1)}, f32[56,640]{1,0:T(8,128)S(1)}, f32[240,256]{1,0:T(8,128)S(1)}, f32[120,384]{1,0:T(8,128)S(1)}) custom-call(f32[56,640]{1,0:T(8,128)S(1)} %get-tuple-element.111.i_ref, f32[56,640]{1,0:T(8,128)S(1)} %update1.1.packed_ref, f32[96,640]{1,0:T(8,128)S(1)} %get-tuple-element.112.faces_ref, ...), custom_call_target="tpu_custom_call" | custom-call | flops 300000000 | bytes 2085888 | tf_op jit(solution)/shard_map/local2/pallas_call | solution.py:567
  33.8 0.0 collective-permute-done.8.r0
  33.8 0.0 collective-permute-done.9.r1
  33.8 0.0 collective-permute-done.10.r2
  33.8 0.5 %collective-permute-done.11.r3 = f32[24,128]{1,0:T(8,128)S(1)} collective-permute-done((f32[24,128]{1,0:T(8,128)S(1)}, f32[24,128]{1,0:T(8,128)S(1)}, u32[]{:S(2)}, u32[]{:S(2)}) %collective-permute-start.11) | collective-permute-done | bytes 12320 | tf_op jit(solution)/shard_map/ppermute | solution.py:42
  34.4 0.8 %update2.1.packed_ref = f32[56,640]{1,0:T(8,128)S(1)} custom-call(f32[24,128]{1,0:T(8,128)S(1)} %collective-permute-done.8.r0, f32[24,128]{1,0:T(8,128)S(1)} %collective-permute-done.9.r1, f32[24,128]{1,0:T(8,128)S(1)} %collective-permute-done.10.r2, f32[24,128]{1,0:T(8,128)S(1)} %collective-permute-done.11.r3, ...), custom_call_target="tpu_custom_call" | custom-call | flops 100000000 | bytes 827392 | tf_op jit(solution)/shard_map/update2/pallas_call | solution.py:567
  35.2 2.8 %predict3.1 = (f32[56,640]{1,0:T(8,128)S(1)}, f32[96,640]{1,0:T(8,128)S(1)}, f32[96,128]{1,0:T(8,128)S(1)}, f32[96,128]{1,0:T(8,128)S(1)}, f32[96,128]{1,0:T(8,128)S(1)}, /*index=5*/f32[96,128]{1,0:T(8,128)S(1)}) custom-call(f32[56,640]{1,0:T(8,128)S(1)} %update2.1.packed_ref, s32[1,64]{1,0:T(1,128)S(1)} %get-tuple-element.67.cluster_ref, ...), custom_call_target="tpu_custom_call" | custom-call | flops 400000000 | bytes 1022720 | tf_op jit(solution)/shard_map/predict3/pallas_call | solution.py:567
  38.0 0.1 collective-permute-start.12
  38.1 1.9 %collective-permute-start.13 = (f32[96,128]{1,0:T(8,128)S(1)}, f32[96,128]{1,0:T(8,128)S(1)}, u32[]{:S(2)}, u32[]{:S(2)}) collective-permute-start(f32[96,128]{1,0:T(8,128)S(1)} %get-tuple-element.119), channel_id=1, source_target_pairs={{4,8},{8,4},{12,16},{16,12},{20,24},{24,20},{28,0},{0,28},{5,9},{9... | collective-permute-start | bytes 147464 | tf_op jit(solution)/shard_map/ppermute | solution.py:42
  40.0 1.4 %collective-permute-start.14 = (f32[96,128]{1,0:T(8,128)S(1)}, f32[96,128]{1,0:T(8,128)S(1)}, u32[]{:S(2)}, u32[]{:S(2)}) collective-permute-start(f32[96,128]{1,0:T(8,128)S(1)} %get-tuple-element.120), channel_id=1, source_target_pairs={{0,1},{1,0},{2,3},{3,2},{4,5},{5,4},{6,7},{7,6},{8,9},{9,8},{10,11... | collective-permute-start | bytes 147464 | tf_op jit(solution)/shard_map/ppermute | solution.py:42
  41.4 1.1 %collective-permute-start.15 = (f32[96,128]{1,0:T(8,128)S(1)}, f32[96,128]{1,0:T(8,128)S(1)}, u32[]{:S(2)}, u32[]{:S(2)}) collective-permute-start(f32[96,128]{1,0:T(8,128)S(1)} %get-tuple-element.121), channel_id=1, source_target_pairs={{1,2},{2,1},{3,0},{0,3},{5,6},{6,5},{7,4},{4,7},{9,10},{10,9},{11,... | collective-permute-start | bytes 147464 | tf_op jit(solution)/shard_map/ppermute | solution.py:42
  42.5 1.2 %local3.1 = (f32[56,640]{1,0:T(8,128)S(1)}, f32[56,640]{1,0:T(8,128)}, f32[240,256]{1,0:T(8,128)S(1)}) custom-call(f32[56,640]{1,0:T(8,128)S(1)} %get-tuple-element.122.i_ref, f32[56,640]{1,0:T(8,128)S(1)} %update2.1.packed_ref, f32[96,640]{1,0:T(8,128)S(1)} %get-tuple-element.123.faces_ref, s32[1,64]{1,0:T(1,128)S(1)} %get-tuple-element.67.cluster_ref, ...), custom_call_target="tpu_custom_call" | custom-call | flops 300000000 | bytes 2085888 | tf_op jit(solution)/shard_map/local3/pallas_call | solution.py:567
  43.7 0.0 collective-permute-done.12.r0
  43.8 0.0 collective-permute-done.13.r1
  43.8 0.0 collective-permute-done.14.r2
  43.8 1.2 %collective-permute-done.15.r3 = f32[96,128]{1,0:T(8,128)S(1)} collective-permute-done((f32[96,128]{1,0:T(8,128)S(1)}, f32[96,128]{1,0:T(8,128)S(1)}, u32[]{:S(2)}, u32[]{:S(2)}) %collective-permute-start.15) | collective-permute-done | bytes 49184 | tf_op jit(solution)/shard_map/ppermute | solution.py:42
  44.9 1.7 %last.1 = f32[9,56,64]{2,1,0:T(8,128)} custom-call(f32[96,128]{1,0:T(8,128)S(1)} %collective-permute-done.12.r0, f32[96,128]{1,0:T(8,128)S(1)} %collective-permute-done.13.r1, f32[96,128]{1,0:T(8,128)S(1)} %collective-permute-done.14.r2, f32[96,128]{1,0:T(8,128)S(1)} %collective-permute-done.15.r3, f32[240,256]{1,0:T(8,128)S(1)} %get-tuple-element.125.near_ref, ...), custom_call_target="tpu_custom_call" | custom-call | flops 100000000 | bytes 974848 | tf_op jit(solution)/shard_map/last/pallas_call | solution.py:567
Async XLA Ops:
  4.2 9.6 %collective-permute-start = (f32[24,128]{1,0:T(8,128)S(1)}, f32[24,128]{1,0:T(8,128)S(1)}, u32[]{:S(2)}, u32[]{:S(2)}) collective-permute-start(f32[24,128]{1,0:T(8,128)S(1)} %get-tuple-element.72), channel_id=1, source_target_pairs={{0,4},{4,0},{8,12},{12,8},{16,20},{20,16},{24,28},{28,24},{1,5},{5... | collective-permute-start | bytes 36872 | tf_op jit(solution)/shard_map/ppermute | solution.py:42
  6.3 7.6 %collective-permute-start.1 = (f32[24,128]{1,0:T(8,128)S(1)}, f32[24,128]{1,0:T(8,128)S(1)}, u32[]{:S(2)}, u32[]{:S(2)}) collective-permute-start(f32[24,128]{1,0:T(8,128)S(1)} %get-tuple-element.73), channel_id=1, source_target_pairs={{4,8},{8,4},{12,16},{16,12},{20,24},{24,20},{28,0},{0,28},{5,9},{9... | collective-permute-start | bytes 36872 | tf_op jit(solution)/shard_map/ppermute | solution.py:42
  9.6 4.3 %collective-permute-start.2 = (f32[24,128]{1,0:T(8,128)S(1)}, f32[24,128]{1,0:T(8,128)S(1)}, u32[]{:S(2)}, u32[]{:S(2)}) collective-permute-start(f32[24,128]{1,0:T(8,128)S(1)} %get-tuple-element.74), channel_id=1, source_target_pairs={{0,1},{1,0},{2,3},{3,2},{4,5},{5,4},{6,7},{7,6},{8,9},{9,8},{10,11... | collective-permute-start | bytes 36872 | tf_op jit(solution)/shard_map/ppermute | solution.py:42
  10.9 3.1 %collective-permute-start.3 = (f32[24,128]{1,0:T(8,128)S(1)}, f32[24,128]{1,0:T(8,128)S(1)}, u32[]{:S(2)}, u32[]{:S(2)}) collective-permute-start(f32[24,128]{1,0:T(8,128)S(1)} %get-tuple-element.75), channel_id=1, source_target_pairs={{1,2},{2,1},{3,0},{0,3},{5,6},{6,5},{7,4},{4,7},{9,10},{10,9},{11,... | collective-permute-start | bytes 36872 | tf_op jit(solution)/shard_map/ppermute | solution.py:42
  17.5 5.8 %collective-permute-start.4 = (f32[48,128]{1,0:T(8,128)S(1)}, f32[48,128]{1,0:T(8,128)S(1)}, u32[]{:S(2)}, u32[]{:S(2)}) collective-permute-start(f32[48,128]{1,0:T(8,128)S(1)} %get-tuple-element.98), channel_id=1, source_target_pairs={{0,4},{4,0},{8,12},{12,8},{16,20},{20,16},{24,28},{28,24},{1,5},{5... | collective-permute-start | bytes 73736 | tf_op jit(solution)/shard_map/ppermute | solution.py:42
  17.5 5.8 %collective-permute-start.5 = (f32[48,128]{1,0:T(8,128)S(1)}, f32[48,128]{1,0:T(8,128)S(1)}, u32[]{:S(2)}, u32[]{:S(2)}) collective-permute-start(f32[48,128]{1,0:T(8,128)S(1)} %get-tuple-element.99), channel_id=1, source_target_pairs={{4,8},{8,4},{12,16},{16,12},{20,24},{24,20},{28,0},{0,28},{5,9},{9... | collective-permute-start | bytes 73736 | tf_op jit(solution)/shard_map/ppermute | solution.py:42
  19.2 4.2 %collective-permute-start.6 = (f32[48,128]{1,0:T(8,128)S(1)}, f32[48,128]{1,0:T(8,128)S(1)}, u32[]{:S(2)}, u32[]{:S(2)}) collective-permute-start(f32[48,128]{1,0:T(8,128)S(1)} %get-tuple-element.100), channel_id=1, source_target_pairs={{0,1},{1,0},{2,3},{3,2},{4,5},{5,4},{6,7},{7,6},{8,9},{9,8},{10,11... | collective-permute-start | bytes 73736 | tf_op jit(solution)/shard_map/ppermute | solution.py:42
  20.9 3.3 %collective-permute-start.7 = (f32[48,128]{1,0:T(8,128)S(1)}, f32[48,128]{1,0:T(8,128)S(1)}, u32[]{:S(2)}, u32[]{:S(2)}) collective-permute-start(f32[48,128]{1,0:T(8,128)S(1)} %get-tuple-element.101), channel_id=1, source_target_pairs={{1,2},{2,1},{3,0},{0,3},{5,6},{6,5},{7,4},{4,7},{9,10},{10,9},{11,... | collective-permute-start | bytes 73736 | tf_op jit(solution)/shard_map/ppermute | solution.py:42
  27.7 6.1 %collective-permute-start.8 = (f32[24,128]{1,0:T(8,128)S(1)}, f32[24,128]{1,0:T(8,128)S(1)}, u32[]{:S(2)}, u32[]{:S(2)}) collective-permute-start(f32[24,128]{1,0:T(8,128)S(1)} %get-tuple-element.107), channel_id=1, source_target_pairs={{0,4},{4,0},{8,12},{12,8},{16,20},{20,16},{24,28},{28,24},{1,5},{5... | collective-permute-start | bytes 36872 | tf_op jit(solution)/shard_map/ppermute | solution.py:42
  27.8 6.0 %collective-permute-start.9 = (f32[24,128]{1,0:T(8,128)S(1)}, f32[24,128]{1,0:T(8,128)S(1)}, u32[]{:S(2)}, u32[]{:S(2)}) collective-permute-start(f32[24,128]{1,0:T(8,128)S(1)} %get-tuple-element.108), channel_id=1, source_target_pairs={{4,8},{8,4},{12,16},{16,12},{20,24},{24,20},{28,0},{0,28},{5,9},{9... | collective-permute-start | bytes 36872 | tf_op jit(solution)/shard_map/ppermute | solution.py:42
  29.8 4.1 %collective-permute-start.10 = (f32[24,128]{1,0:T(8,128)S(1)}, f32[24,128]{1,0:T(8,128)S(1)}, u32[]{:S(2)}, u32[]{:S(2)}) collective-permute-start(f32[24,128]{1,0:T(8,128)S(1)} %get-tuple-element.109), channel_id=1, source_target_pairs={{0,1},{1,0},{2,3},{3,2},{4,5},{5,4},{6,7},{7,6},{8,9},{9,8},{10,11... | collective-permute-start | bytes 36872 | tf_op jit(solution)/shard_map/ppermute | solution.py:42
  31.2 3.2 %collective-permute-start.11 = (f32[24,128]{1,0:T(8,128)S(1)}, f32[24,128]{1,0:T(8,128)S(1)}, u32[]{:S(2)}, u32[]{:S(2)}) collective-permute-start(f32[24,128]{1,0:T(8,128)S(1)} %get-tuple-element.110), channel_id=1, source_target_pairs={{1,2},{2,1},{3,0},{0,3},{5,6},{6,5},{7,4},{4,7},{9,10},{10,9},{11,... | collective-permute-start | bytes 36872 | tf_op jit(solution)/shard_map/ppermute | solution.py:42
  38.0 5.8 %collective-permute-start.12 = (f32[96,128]{1,0:T(8,128)S(1)}, f32[96,128]{1,0:T(8,128)S(1)}, u32[]{:S(2)}, u32[]{:S(2)}) collective-permute-start(f32[96,128]{1,0:T(8,128)S(1)} %get-tuple-element.118), channel_id=1, source_target_pairs={{0,4},{4,0},{8,12},{12,8},{16,20},{20,16},{24,28},{28,24},{1,5},{5... | collective-permute-start | bytes 147464 | tf_op jit(solution)/shard_map/ppermute | solution.py:42
  38.1 5.7 %collective-permute-start.13 = (f32[96,128]{1,0:T(8,128)S(1)}, f32[96,128]{1,0:T(8,128)S(1)}, u32[]{:S(2)}, u32[]{:S(2)}) collective-permute-start(f32[96,128]{1,0:T(8,128)S(1)} %get-tuple-element.119), channel_id=1, source_target_pairs={{4,8},{8,4},{12,16},{16,12},{20,24},{24,20},{28,0},{0,28},{5,9},{9... | collective-permute-start | bytes 147464 | tf_op jit(solution)/shard_map/ppermute | solution.py:42
  40.0 3.8 %collective-permute-start.14 = (f32[96,128]{1,0:T(8,128)S(1)}, f32[96,128]{1,0:T(8,128)S(1)}, u32[]{:S(2)}, u32[]{:S(2)}) collective-permute-start(f32[96,128]{1,0:T(8,128)S(1)} %get-tuple-element.120), channel_id=1, source_target_pairs={{0,1},{1,0},{2,3},{3,2},{4,5},{5,4},{6,7},{7,6},{8,9},{9,8},{10,11... | collective-permute-start | bytes 147464 | tf_op jit(solution)/shard_map/ppermute | solution.py:42
  41.4 3.5 %collective-permute-start.15 = (f32[96,128]{1,0:T(8,128)S(1)}, f32[96,128]{1,0:T(8,128)S(1)}, u32[]{:S(2)}, u32[]{:S(2)}) collective-permute-start(f32[96,128]{1,0:T(8,128)S(1)} %get-tuple-element.121), channel_id=1, source_target_pairs={{1,2},{2,1},{3,0},{0,3},{5,6},{6,5},{7,4},{4,7},{9,10},{10,9},{11,... | collective-permute-start | bytes 147464 | tf_op jit(solution)/shard_map/ppermute | solution.py:42
